TPU v7x, 32 devices: a whole 2x2x4 slice. The times are simulated.
32 devices in a mesh: shard: 4 (over x, core), ctx: 4 (over z), tp: 2 (over y).
Axes of the slice: x: 2, y: 2, z: 4, core: 2. Of those that a mesh axis runs over, the one named last changes fastest.
Arguments:
- block_input: float32 [8, 1024, 2048], P('shard', 'ctx'), may hold values from -6 to 6
- segment_ids: int32 [8, 1024], P('shard', 'ctx'), may hold values from 0 to 3, never falling along the last dimension, each value on 1 to 800 neighbouring positions
- norm_gain: float32 [2048], replicated, may hold values from 0.25 to 1.75
- lower: float32 [2048], P('tp'), may hold values from 0.5 to 0.9999
- w_input: float32 [2048, 2048], P(('shard', 'ctx'), 'tp'), may hold values from -0.125 to 0.125
- w_forget: float32 [2048, 2048], P(('shard', 'ctx'), 'tp'), may hold values from -0.125 to 0.125
- w_gate: float32 [2048, 2048], P(('shard', 'ctx'), 'tp'), may hold values from -0.125 to 0.125
- hidden_gain: float32 [2048], P('tp'), may hold values from 0.25 to 1.75
- w_out: float32 [2048, 2048], P(('shard', 'ctx'), 'tp'), may hold values from -0.125 to 0.125
- mlp_gain: float32 [2048], replicated, may hold values from 0.25 to 1.75
- w_mlp_gate: float32 [2048, 5632], P(('shard', 'ctx'), 'tp'), may hold values from -0.125 to 0.125
- w_mlp_up: float32 [2048, 5632], P(('shard', 'ctx'), 'tp'), may hold values from -0.125 to 0.125
- w_down: float32 [2048, 5632], P(('shard', 'ctx'), 'tp'), may hold values from -0.078125 to 0.078125
- cotangent: float32 [8, 1024, 2048], P('shard', 'ctx'), may hold values from -6 to 6
Outputs:
- block_output: float32 [8, 1024, 2048], P('shard', 'ctx')
- input_grad: float32 [8, 1024, 2048], P('shard', 'ctx')
- norm_gain_grad: float32 [2048], replicated
- lower_grad: float32 [2048], P('tp')
- w_input_grad: float32 [2048, 2048], P(('shard', 'ctx'), 'tp')
- w_forget_grad: float32 [2048, 2048], P(('shard', 'ctx'), 'tp')
- w_gate_grad: float32 [2048, 2048], P(('shard', 'ctx'), 'tp')
- hidden_gain_grad: float32 [2048], P('tp')
- w_out_grad: float32 [2048, 2048], P(('shard', 'ctx'), 'tp')
- mlp_gain_grad: float32 [2048], replicated
- w_mlp_gate_grad: float32 [2048, 5632], P(('shard', 'ctx'), 'tp')
- w_mlp_up_grad: float32 [2048, 5632], P(('shard', 'ctx'), 'tp')
- w_down_grad: float32 [2048, 5632], P(('shard', 'ctx'), 'tp')
Inputs may be any that keep to these rules, and one draw needn't show every extreme that they name: `segment_ids`: document ids of each sequence; they never fall along a sequence, and one document holds at most 800 tokens.
All inputs are finite; a program needn't handle non-finite values.
Results may differ from a plain program's by a relative error of at most 0.018.
Values may be sent and summed in bfloat16 or wider, within the bound.
A program may use at most 256 MiB of HBM per device.

v0:
```python
import jax
import jax.numpy as jnp
from jax import lax
from jax.sharding import PartitionSpec as P

epsilon = 1e-06


def carried_in(x, axis, combine, identity, reverse):
    size, position = (lax.axis_size(axis), lax.axis_index(axis))
    everything = jax.tree.map(lambda part: lax.all_gather(part, axis), x)
    start = jax.tree.map(
        lambda part, zero: jnp.broadcast_to(jnp.asarray(zero, part.dtype), part.shape), x, identity
    )

    def turn(k, before):
        at = size - 1 - k if reverse else k
        reached = at > position if reverse else at < position
        new = combine(before, jax.tree.map(lambda part: part[at], everything))
        return jax.tree.map(lambda a, b: jnp.where(reached, a, b), new, before)

    return lax.fori_loop(0, size, turn, start)


def inverse_rms(inputs):
    return lax.rsqrt(jnp.mean(inputs * inputs, axis=-1, keepdims=True) + epsilon)


def rms_backward(inputs, row_scale, gain_vec, upstream):
    weighted = upstream * gain_vec
    inner_sum = jnp.mean(weighted * inputs, axis=-1, keepdims=True)
    return weighted * row_scale - inputs * (row_scale * row_scale * row_scale) * inner_sum


def silu_slope(inputs):
    sig_part = jax.nn.sigmoid(inputs)
    return sig_part * (1.0 + inputs * (1.0 - sig_part))


def times_back(left_mat, right_mat):
    return lax.dot_general(
        left_mat, right_mat, (((1,), (1,)), ((), ())), preferred_element_type=jnp.float32
    )


def outer_sum(left_mat, right_mat):
    return lax.dot_general(
        left_mat, right_mat, (((0,), (0,)), ((), ())), preferred_element_type=jnp.float32
    )


def linear_step(first_part, second_part):
    return (first_part[0] * second_part[0], second_part[0] * first_part[1] + second_part[1])


def joined(last_ids, first_ids):
    return jnp.where((last_ids == first_ids) | (last_ids < 0.0) | (first_ids < 0.0), 1.0, 0.0)


def forward_join(first_part, second_part):
    linked = joined(first_part[3], second_part[2])[:, None]
    return (
        first_part[0] * second_part[0] * linked,
        second_part[0] * linked * first_part[1] + second_part[1],
        jnp.where(first_part[2] < 0.0, second_part[2], first_part[2]),
        jnp.where(second_part[3] < 0.0, first_part[3], second_part[3]),
    )


def backward_join(first_part, second_part):
    linked = joined(second_part[3], first_part[2])[:, None]
    return (
        second_part[0] * linked * first_part[0],
        second_part[0] * linked * first_part[1] + second_part[1],
        jnp.where(second_part[2] < 0.0, first_part[2], second_part[2]),
        jnp.where(first_part[3] < 0.0, second_part[3], first_part[3]),
    )


def on_device(
    block_input,
    segment_ids,
    norm_gain,
    lower,
    w_input,
    w_forget,
    w_gate,
    hidden_gain,
    w_out,
    mlp_gain,
    w_mlp_gate,
    w_mlp_up,
    w_down,
    cotangent,
):
    bfloat = jnp.bfloat16
    seq_count, span_len, model_width = block_input.shape
    rows_all = seq_count * span_len
    wide_input, wide_forget, wide_gate, wide_out = (
        lax.all_gather(w_input.astype(bfloat), ("shard", "ctx"), axis=0, tiled=True),
        lax.all_gather(w_forget.astype(bfloat), ("shard", "ctx"), axis=0, tiled=True),
        lax.all_gather(w_gate.astype(bfloat), ("shard", "ctx"), axis=0, tiled=True),
        lax.all_gather(w_out.astype(bfloat), ("shard", "ctx"), axis=0, tiled=True),
    )
    wide_mgate, wide_mup, wide_down = (
        lax.all_gather(w_mlp_gate.astype(bfloat), ("shard", "ctx"), axis=0, tiled=True),
        lax.all_gather(w_mlp_up.astype(bfloat), ("shard", "ctx"), axis=0, tiled=True),
        lax.all_gather(w_down.astype(bfloat), ("shard", "ctx"), axis=0, tiled=True),
    )
    residual_in = block_input.reshape(rows_all, model_width)
    scale_one = inverse_rms(residual_in)
    normed_one = (residual_in * scale_one * norm_gain).astype(bfloat)
    proj_input = jnp.dot(normed_one, wide_input, preferred_element_type=jnp.float32)
    proj_forget = jnp.dot(normed_one, wide_forget, preferred_element_type=jnp.float32)
    proj_gate = jnp.dot(normed_one, wide_gate, preferred_element_type=jnp.float32)
    channels = proj_input.shape[1]
    sigmoid_f = jax.nn.sigmoid(proj_forget)
    forget = lower + (1.0 - lower) * sigmoid_f
    silu_in = jax.nn.silu(proj_input)
    candidate = silu_in * (1.0 - forget)
    seg_float = segment_ids.astype(jnp.float32)
    inner_link = jnp.concatenate(
        [
            jnp.ones((seq_count, 1), jnp.float32),
            jnp.where(seg_float[:, 1:] == seg_float[:, :-1], 1.0, 0.0),
        ],
        axis=1,
    )
    forget_seq = forget.reshape(seq_count, span_len, channels)
    decay_rate = forget_seq * inner_link[:, :, None]
    decay_prod, local_state = lax.associative_scan(
        linear_step, (decay_rate, candidate.reshape(seq_count, span_len, channels)), axis=1
    )
    first_ids = seg_float[:, 0]
    last_ids = seg_float[:, -1]
    ones_state = jnp.ones((seq_count, channels), jnp.float32)
    zero_state = jnp.zeros((seq_count, channels), jnp.float32)
    minus_ids = -jnp.ones((seq_count,), jnp.float32)
    prefix = carried_in(
        (decay_prod[:, -1], local_state[:, -1], first_ids, last_ids),
        "ctx",
        forward_join,
        (ones_state, zero_state, minus_ids, minus_ids),
        False,
    )
    start_state = joined(prefix[3], first_ids)[:, None] * prefix[1]
    state_seq = local_state + decay_prod * start_state[:, None, :]
    hidden_state = state_seq.reshape(rows_all, channels)
    squares = lax.psum(jnp.sum(hidden_state * hidden_state, axis=1), "tp")
    scale_mid = lax.rsqrt(squares / model_width + epsilon)[:, None]
    silu_gate = jax.nn.silu(proj_gate)
    mixed_in = (hidden_state * scale_mid * hidden_gain * silu_gate).astype(bfloat)
    mixer_out = lax.psum(times_back(mixed_in, wide_out).astype(jnp.bfloat16), "tp").astype(
        jnp.float32
    )
    middle = residual_in + mixer_out
    scale_two = inverse_rms(middle)
    normed_two = (middle * scale_two * mlp_gain).astype(bfloat)
    gate_pre = jnp.dot(normed_two, wide_mgate, preferred_element_type=jnp.float32)
    up_pre = jnp.dot(normed_two, wide_mup, preferred_element_type=jnp.float32)
    silu_mlp = jax.nn.silu(gate_pre)
    activated = (silu_mlp * up_pre).astype(bfloat)
    mlp_out = lax.psum(times_back(activated, wide_down).astype(jnp.bfloat16), "tp").astype(
        jnp.float32
    )
    output = middle + mlp_out
    wide_input, wide_forget, wide_gate, wide_out, wide_mgate, wide_mup, wide_down = (
        lax.all_gather(w_input.astype(bfloat), ("shard", "ctx"), axis=0, tiled=True),
        lax.all_gather(w_forget.astype(bfloat), ("shard", "ctx"), axis=0, tiled=True),
        lax.all_gather(w_gate.astype(bfloat), ("shard", "ctx"), axis=0, tiled=True),
        lax.all_gather(w_out.astype(bfloat), ("shard", "ctx"), axis=0, tiled=True),
        lax.all_gather(w_mlp_gate.astype(bfloat), ("shard", "ctx"), axis=0, tiled=True),
        lax.all_gather(w_mlp_up.astype(bfloat), ("shard", "ctx"), axis=0, tiled=True),
        lax.all_gather(w_down.astype(bfloat), ("shard", "ctx"), axis=0, tiled=True),
    )
    upstream = cotangent.reshape(rows_all, model_width)
    upstream_low = upstream.astype(bfloat)
    grad_activ = jnp.dot(upstream_low, wide_down, preferred_element_type=jnp.float32)
    grad_down = outer_sum(upstream_low, activated)
    grad_gate_pre = (grad_activ * up_pre * silu_slope(gate_pre)).astype(bfloat)
    grad_up_pre = (grad_activ * silu_mlp).astype(bfloat)
    grad_mgate = outer_sum(normed_two, grad_gate_pre)
    grad_mup = outer_sum(normed_two, grad_up_pre)
    grad_normed_two = lax.psum(
        (times_back(grad_gate_pre, wide_mgate) + times_back(grad_up_pre, wide_mup)).astype(
            jnp.bfloat16
        ),
        "tp",
    ).astype(jnp.float32)
    grad_mlp_gain = jnp.sum(grad_normed_two * middle * scale_two, axis=0)
    grad_middle = upstream + rms_backward(middle, scale_two, mlp_gain, grad_normed_two)
    middle_low = grad_middle.astype(bfloat)
    grad_mixed_in = jnp.dot(middle_low, wide_out, preferred_element_type=jnp.float32)
    grad_out = outer_sum(middle_low, mixed_in)
    weighted = grad_mixed_in * hidden_gain * silu_gate
    inner_sum = lax.psum(jnp.sum(weighted * hidden_state, axis=1), "tp")
    grad_state = (
        weighted * scale_mid
        - hidden_state * (scale_mid * scale_mid * scale_mid) * (inner_sum / model_width)[:, None]
    )
    grad_hidden_gain = jnp.sum(grad_mixed_in * hidden_state * scale_mid * silu_gate, axis=0)
    grad_gate_proj = (
        grad_mixed_in * hidden_state * scale_mid * hidden_gain * silu_slope(proj_gate)
    ).astype(bfloat)
    next_decay = jnp.concatenate(
        [decay_rate[:, 1:], jnp.ones((seq_count, 1, channels), jnp.float32)], axis=1
    )
    tail_prod, local_grad = lax.associative_scan(
        linear_step,
        (next_decay, grad_state.reshape(seq_count, span_len, channels)),
        reverse=True,
        axis=1,
    )
    suffix = carried_in(
        (decay_prod[:, -1], forget_seq[:, 0] * local_grad[:, 0], first_ids, last_ids),
        "ctx",
        backward_join,
        (ones_state, zero_state, minus_ids, minus_ids),
        True,
    )
    end_grad = joined(last_ids, suffix[2])[:, None] * suffix[1]
    total_grad = (local_grad + tail_prod * end_grad[:, None, :]).reshape(rows_all, channels)
    previous = jnp.concatenate(
        [start_state[:, None, :], inner_link[:, 1:, None] * state_seq[:, :-1]], axis=1
    ).reshape(rows_all, channels)
    grad_forget = total_grad * (previous - silu_in)
    grad_input_proj = (total_grad * (1.0 - forget) * silu_slope(proj_input)).astype(bfloat)
    grad_forget_proj = (grad_forget * (1.0 - lower) * sigmoid_f * (1.0 - sigmoid_f)).astype(bfloat)
    grad_lower = jnp.sum(grad_forget * (1.0 - sigmoid_f), axis=0)
    grad_w_input = outer_sum(normed_one, grad_input_proj)
    grad_w_forget = outer_sum(normed_one, grad_forget_proj)
    grad_w_gate = outer_sum(normed_one, grad_gate_proj)
    grad_normed_one = lax.psum(
        (
            times_back(grad_input_proj, wide_input)
            + times_back(grad_forget_proj, wide_forget)
            + times_back(grad_gate_proj, wide_gate)
        ).astype(jnp.bfloat16),
        "tp",
    ).astype(jnp.float32)
    grad_norm_gain = jnp.sum(grad_normed_one * residual_in * scale_one, axis=0)
    grad_resid = grad_middle + rms_backward(residual_in, scale_one, norm_gain, grad_normed_one)
    mlp_grads = (
        lax.psum_scatter(grad_mgate, ("shard", "ctx"), scatter_dimension=0, tiled=True),
        lax.psum_scatter(grad_mup, ("shard", "ctx"), scatter_dimension=0, tiled=True),
        lax.psum_scatter(grad_down, ("shard", "ctx"), scatter_dimension=0, tiled=True),
    )
    mixer_grads = (
        lax.psum_scatter(grad_w_input, ("shard", "ctx"), scatter_dimension=0, tiled=True),
        lax.psum_scatter(grad_w_forget, ("shard", "ctx"), scatter_dimension=0, tiled=True),
        lax.psum_scatter(grad_w_gate, ("shard", "ctx"), scatter_dimension=0, tiled=True),
        lax.psum_scatter(grad_out, ("shard", "ctx"), scatter_dimension=0, tiled=True),
    )
    gain_grads = lax.psum(
        (grad_norm_gain, grad_lower, grad_hidden_gain, grad_mlp_gain), ("shard", "ctx")
    )
    return (
        output.reshape(block_input.shape),
        grad_resid.reshape(block_input.shape),
        gain_grads[0],
        gain_grads[1],
        mixer_grads[0],
        mixer_grads[1],
        mixer_grads[2],
        gain_grads[2],
        mixer_grads[3],
        gain_grads[3],
        mlp_grads[0],
        mlp_grads[1],
        mlp_grads[2],
    )


def solution(mesh):
    return jax.shard_map(
        on_device,
        mesh=mesh,
        in_specs=(
            P("shard", "ctx", None),
            P("shard", "ctx"),
            P(),
            P("tp"),
            P(("shard", "ctx"), "tp"),
            P(("shard", "ctx"), "tp"),
            P(("shard", "ctx"), "tp"),
            P("tp"),
            P(("shard", "ctx"), "tp"),
            P(),
            P(("shard", "ctx"), "tp"),
            P(("shard", "ctx"), "tp"),
            P(("shard", "ctx"), "tp"),
            P("shard", "ctx", None),
        ),
        out_specs=(
            P("shard", "ctx", None),
            P("shard", "ctx", None),
            P(),
            P("tp"),
            P(("shard", "ctx"), "tp"),
            P(("shard", "ctx"), "tp"),
            P(("shard", "ctx"), "tp"),
            P("tp"),
            P(("shard", "ctx"), "tp"),
            P(),
            P(("shard", "ctx"), "tp"),
            P(("shard", "ctx"), "tp"),
            P(("shard", "ctx"), "tp"),
        ),
        check_vma=False,
    )
```

profile of v0, /device:TPU:0, one launch (start us, length us, event | category | flops | bytes accessed | tf_op | source)
XLA Modules:
  0.0 2265.1 jit_solution(16217521087929477413)
XLA Ops:
  17.4 13.7 all-reduce.70
  35.1 28.9 %all-gather.15.cloned.1.call-done = bf16[2048,1024]{1,0:T(8,128)(2,1)} async-done(((bf16[128,1024]{1,0:T(8,128)(2,1)}), bf16[2048,1024]{1,0:T(8,128)(2,1)}) %all-gather.15.cloned.1.call-update) | async-done | bytes 4194320 | tf_op jit(solution)/shard_map/all_gather | solution.py:101
  64.0 6.1 add_divide_fusion.2
  70.1 45.6 %all-gather.13.cloned.1.call-done = bf16[2048,1024]{1,0:T(8,128)(2,1)} async-done(((bf16[128,1024]{1,0:T(8,128)(2,1)}), bf16[2048,1024]{1,0:T(8,128)(2,1)}) %all-gather.13.cloned.1.call-update) | async-done | bytes 4194320 | tf_op jit(solution)/shard_map/all_gather | solution.py:100
  115.7 7.5 subtract_multiply_fusion
  130.4 5.4 slice.515
  224.3 5.6 slice.570
  277.6 13.1 all-gather.2
  302.8 13.1 all-gather
  330.0 7.4 fusion.31
  338.4 5.9 convolution_convert_fusion
  354.1 51.9 %all-reduce.76.cloned.1.call-done = bf16[512,2048]{1,0:T(8,128)(2,1)} async-done(((bf16[512,2048]{1,0:T(8,128)(2,1)}), bf16[512,2048]{1,0:T(8,128)(2,1)}) %all-reduce.76.cloned.1.call-update) | async-done | bytes 2097168 | tf_op jit(solution)/shard_map/psum | solution.py:153
  413.2 89.5 %all-gather.21.cloned.1.call-done = bf16[2048,2816]{1,0:T(8,128)(2,1)} async-done(((bf16[128,2816]{1,0:T(8,128)(2,1)}), bf16[2048,2816]{1,0:T(8,128)(2,1)}) %all-gather.21.cloned.1.call-update) | async-done | bytes 11534352 | tf_op jit(solution)/shard_map/all_gather | solution.py:106
  502.8 12.9 fusion.72
  515.7 82.2 %all-gather.23.cloned.1.call-done = bf16[2048,2816]{1,0:T(8,128)(2,1)} async-done(((bf16[128,2816]{1,0:T(8,128)(2,1)}), bf16[2048,2816]{1,0:T(8,128)(2,1)}) %all-gather.23.cloned.1.call-update) | async-done | bytes 11534352 | tf_op jit(solution)/shard_map/all_gather | solution.py:107
  597.9 12.5 fusion.73
  610.4 82.6 %all-gather.25.cloned.1.call-done = bf16[2048,2816]{1,0:T(8,128)(2,1)} async-done(((bf16[128,2816]{1,0:T(8,128)(2,1)}), bf16[2048,2816]{1,0:T(8,128)(2,1)}) %all-gather.25.cloned.1.call-update) | async-done | bytes 11534352 | tf_op jit(solution)/shard_map/all_gather | solution.py:108
  693.0 16.3 multiply_convert_fusion
  709.3 12.3 fusion.74
  721.6 9.2 add_convert_fusion.1
  737.6 8.9 slice.595
  746.4 9.0 slice.602
  763.5 10.0 convolution_convert_fusion.1
  773.5 18.6 all-reduce.78.cloned.1.call-done
  801.0 5.6 multiply_reduce_fusion.2
  816.2 5.7 slice.596
  822.5 8.9 slice.597
  950.1 13.3 all-gather.4
  963.5 6.4 while.35
  972.7 5.4 pad.261
  981.5 16.8 rev.9
  998.2 10.5 rev.8
  1026.9 12.9 convolution_bitcast_fusion
  1041.5 6.9 fusion.78
  1048.5 5.6 fusion.77
  1055.3 8.0 fusion.40
  1064.5 5.6 fusion.79
  1071.7 12.8 fusion.80
  1084.6 13.2 fusion.81
  1098.5 34.8 %all-reduce.80.cloned.1.call-done = (bf16[512,2048]{1,0:T(8,128)(2,1)}, bf16[512,2048]{1,0:T(8,128)(2,1)}) async-done(((bf16[512,2048]{1,0:T(8,128)(2,1)}, bf16[512,2048]{1,0:T(8,128)(2,1)}), (bf16[512,2048]{1,0:T(8,128)(2,1)}, bf16[512,2048]{1,0:T(8,128)(2,1)})) %all-reduce.80.cloned.1.call-update) | async-done | bytes 4194320 | tf_op jit(solution)/shard_map/psum | solution.py:163
  1137.6 63.3 %all-reduce.69 = (f32[2048]{0:T(1024)}, f32[1024]{0:T(1024)}, f32[1024]{0:T(1024)}, f32[2048]{0:T(1024)}) all-reduce(f32[2048]{0:T(1024)S(1)} %get-tuple-element.453, f32[1024]{0:T(1024)S(1)} %get-tuple-element.510, f32[1024]{0:T(1024)S(1)} %copy-done.113, ...), channel_id=1, replica_groups=mesh['shard'=4,'ctx'=4,'tp'=2] {'shard','ctx'}, use_global_device_ids=true, to_apply=%region_17.18 | all-reduce | flops 6144 | bytes 49152 | tf_op jit(solution)/shard_map/psum | solution.py:254
  1211.0 154.2 %reduce-scatter.20.cloned.1.call-done = f32[128,2816]{0,1:T(8,128)} async-done(((f32[2048,2816]{0,1:T(8,128)}), f32[128,2816]{0,1:T(8,128)}) %reduce-scatter.20.cloned.1.call-update) | async-done | bytes 1441808 | tf_op jit(solution)/shard_map/reduce_scatter | solution.py:246
  1368.1 104.2 %reduce-scatter.10.cloned.1.call-done = f32[128,1024]{1,0:T(8,128)} async-done(((f32[2048,1024]{1,0:T(8,128)}), f32[128,1024]{1,0:T(8,128)}) %reduce-scatter.10.cloned.1.call-update) | async-done | bytes 524304 | tf_op jit(solution)/shard_map/reduce_scatter | solution.py:250
  1472.3 107.8 %reduce-scatter.8.cloned.1.call-done = f32[128,1024]{1,0:T(8,128)} async-done(((f32[2048,1024]{1,0:T(8,128)}), f32[128,1024]{1,0:T(8,128)}) %reduce-scatter.8.cloned.1.call-update) | async-done | bytes 524304 | tf_op jit(solution)/shard_map/reduce_scatter | solution.py:249
  1580.0 107.6 %reduce-scatter.14.cloned.1.call-done = f32[128,1024]{1,0:T(8,128)} async-done(((f32[2048,1024]{1,0:T(8,128)}), f32[128,1024]{1,0:T(8,128)}) %reduce-scatter.14.cloned.1.call-update) | async-done | bytes 524304 | tf_op jit(solution)/shard_map/reduce_scatter | solution.py:252
  1687.6 107.6 %reduce-scatter.12.cloned.1.call-done = f32[128,1024]{1,0:T(8,128)} async-done(((f32[2048,1024]{1,0:T(8,128)}), f32[128,1024]{1,0:T(8,128)}) %reduce-scatter.12.cloned.1.call-update) | async-done | bytes 524304 | tf_op jit(solution)/shard_map/reduce_scatter | solution.py:251
  1795.2 231.7 %reduce-scatter.16.cloned.1.call-done = f32[128,2816]{1,0:T(8,128)} async-done(((f32[2048,2816]{1,0:T(8,128)}), f32[128,2816]{1,0:T(8,128)}) %reduce-scatter.16.cloned.1.call-update) | async-done | bytes 1441808 | tf_op jit(solution)/shard_map/reduce_scatter | solution.py:244
  2027.0 231.2 %reduce-scatter.18.cloned.1.call-done = f32[128,2816]{1,0:T(8,128)} async-done(((f32[2048,2816]{1,0:T(8,128)}), f32[128,2816]{1,0:T(8,128)}) %reduce-scatter.18.cloned.1.call-update) | async-done | bytes 1441808 | tf_op jit(solution)/shard_map/reduce_scatter | solution.py:245
  (631 shorter events, 408.9 us)
Async XLA Ops:
  7.2 56.8 %all-gather.15.cloned.1.call-start = ((), (), s32[]{:S(2)}) async-start(), calls=%async_computation.8 | async-start | bytes 4456448 | tf_op jit(solution)/shard_map/all_gather | solution.py:101
  9.1 106.6 %all-gather.13.cloned.1.call-start = ((), (), s32[]{:S(2)}) async-start(), calls=%async_computation.7 | async-start | bytes 4456448 | tf_op jit(solution)/shard_map/all_gather | solution.py:100
  11.0 319.0 %all-gather.17.cloned.1.call-start = ((), (), s32[]{:S(2)}) async-start(), calls=%async_computation.9 | async-start | bytes 4456448 | tf_op jit(solution)/shard_map/all_gather | solution.py:102
  11.8 325.7 %all-gather.19.cloned.1.call-start = ((), (), s32[]{:S(2)}) async-start(), calls=%async_computation.10 | async-start | bytes 4456448 | tf_op jit(solution)/shard_map/all_gather | solution.py:103
  12.6 393.4 %all-reduce.76.cloned.1.call-start = ((), (), s32[]{:S(2)}) async-start(), calls=%async_computation.11 | async-start | bytes 4194304 | tf_op jit(solution)/shard_map/psum | solution.py:153
  12.8 22.3 copy-start.101
  13.0 19.4 copy-start.58
  15.6 100.1 %copy-start.103 = (f32[1024]{0:T(1024)}, f32[1024]{0:T(1024)S(1)}, u32[]{:S(2)}) copy-start(f32[1024]{0:T(1024)S(1)} %broadcast_subtract_fusion) | copy-start | bytes 12292
  17.4 17.7 copy-start.68
  35.1 80.7 %copy-start.27 = (bf16[512,2048]{1,0:T(8,128)(2,1)}, bf16[512,2048]{1,0:T(8,128)(2,1)S(1)}, u32[]{:S(2)}) copy-start(bf16[512,2048]{1,0:T(8,128)(2,1)S(1)} %fusion.24) | copy-start | bytes 6291460
  221.2 10.7 copy-start.98
  221.2 10.7 copy-start.99
  221.2 10.7 copy-start.100
  221.2 10.8 copy-start.61
  221.2 10.8 copy-start.63
  221.2 10.8 copy-start.65
  221.3 11.0 copy-start.53
  221.3 11.0 copy-start.54
  221.3 11.0 copy-start.90
  273.0 17.8 copy-start.70
  298.5 17.5 copy-start.105
  298.5 20.7 copy-start.118
  319.3 10.7 copy-start.110
  344.3 158.4 %all-gather.21.cloned.1.call-start = ((), (), s32[]{:S(2)}) async-start(), calls=%async_computation.12 | async-start | bytes 12255232 | tf_op jit(solution)/shard_map/all_gather | solution.py:106
  346.6 251.2 %all-gather.23.cloned.1.call-start = ((), (), s32[]{:S(2)}) async-start(), calls=%async_computation.13 | async-start | bytes 12255232 | tf_op jit(solution)/shard_map/all_gather | solution.py:107
  349.1 343.9 %all-gather.25.cloned.1.call-start = ((), (), s32[]{:S(2)}) async-start(), calls=%async_computation.14 | async-start | bytes 12255232 | tf_op jit(solution)/shard_map/all_gather | solution.py:108
  350.1 442.1 %all-reduce.78.cloned.1.call-start = ((), (), s32[]{:S(2)}) async-start(), calls=%async_computation.15 | async-start | bytes 4194304 | tf_op jit(solution)/shard_map/psum | solution.py:184
  354.1 57.4 %copy-start.57 = (f32[2048]{0:T(1024)S(1)}, f32[2048]{0:T(1024)}, u32[]{:S(2)}) copy-start(f32[2048]{0:T(1024)} %param.27) | copy-start | bytes 24580
  693.0 28.6 %slice-start = ((s8[11534336]{0:T(1024)(128)(4,1)}), s8[3145728]{0:T(1024)(128)(4,1)S(1)}, s32[]{:S(2)}) async-start(s8[11534336]{0:T(1024)(128)(4,1)} %bitcast.211), calls=%async_computation.24 | async-start | bytes 6291456
  693.0 28.6 %slice-start.1 = ((s8[11534336]{0:T(1024)(128)(4,1)}), s8[4194304]{0:T(1024)(128)(4,1)S(1)}, s32[]{:S(2)}) async-start(s8[11534336]{0:T(1024)(128)(4,1)} %bitcast.211), calls=%async_computation.25 | async-start | bytes 8388608
  709.3 12.3 copy-start.127
  709.3 12.3 slice-start.2
  730.8 402.5 %all-reduce.80.cloned.1.call-start = ((), (), s32[]{:S(2)}) async-start(), calls=%async_computation.23 | async-start | bytes 8388608 | tf_op jit(solution)/shard_map/psum | solution.py:163
  746.4 14.3 copy-start.5
  746.4 14.3 copy-start.102
  946.8 16.7 copy-start.106
  946.8 23.1 %copy-start.116 = (f32[2]{0:T(128)S(1)}, f32[2]{0:T(128)}, u32[]{:S(2)}) copy-start(f32[2]{0:T(128)} %copy-done.115) | copy-start | bytes 28
  950.1 22.1 copy-start.20
  981.5 16.8 copy-start.14
  1025.3 339.9 %reduce-scatter.20.cloned.1.call-start = ((), (), s32[]{:S(2)}) async-start(), calls=%async_computation.22 | async-start | bytes 24510464 | tf_op jit(solution)/shard_map/reduce_scatter | solution.py:246
  1039.8 432.4 %reduce-scatter.10.cloned.1.call-start = ((), (), s32[]{:S(2)}) async-start(), calls=%async_computation.17 | async-start | bytes 8912896 | tf_op jit(solution)/shard_map/reduce_scatter | solution.py:250
  1048.4 531.6 %reduce-scatter.8.cloned.1.call-start = ((), (), s32[]{:S(2)}) async-start(), calls=%async_computation.16 | async-start | bytes 8912896 | tf_op jit(solution)/shard_map/reduce_scatter | solution.py:249
  1054.1 633.5 %reduce-scatter.14.cloned.1.call-start = ((), (), s32[]{:S(2)}) async-start(), calls=%async_computation.19 | async-start | bytes 8912896 | tf_op jit(solution)/shard_map/reduce_scatter | solution.py:252
  1063.3 731.9 %reduce-scatter.12.cloned.1.call-start = ((), (), s32[]{:S(2)}) async-start(), calls=%async_computation.18 | async-start | bytes 8912896 | tf_op jit(solution)/shard_map/reduce_scatter | solution.py:251
  1070.2 956.8 %reduce-scatter.16.cloned.1.call-start = ((), (), s32[]{:S(2)}) async-start(), calls=%async_computation.20 | async-start | bytes 24510464 | tf_op jit(solution)/shard_map/reduce_scatter | solution.py:244
  1084.6 1173.6 %reduce-scatter.18.cloned.1.call-start = ((), (), s32[]{:S(2)}) async-start(), calls=%async_computation.21 | async-start | bytes 24510464 | tf_op jit(solution)/shard_map/reduce_scatter | solution.py:245
  1097.9 35.5 %copy-start.59 = (f32[2048]{0:T(1024)S(1)}, f32[2048]{0:T(1024)}, u32[]{:S(2)}) copy-start(f32[2048]{0:T(1024)} %param.20) | copy-start | bytes 24580
  1133.4 67.6 %copy-start.31 = (bf16[512,2048]{1,0:T(8,128)(2,1)S(1)}, bf16[512,2048]{1,0:T(8,128)(2,1)}, u32[]{:S(2)}) copy-start(bf16[512,2048]{1,0:T(8,128)(2,1)} %get-tuple-element.495) | copy-start | bytes 6291460
  (100 other events, 368.2 us)
Sparse Core Ops, SparseCore 0:
  10.8 53.1 all-gather.14
  66.8 48.8 all-gather.12
  117.9 48.8 all-gather.16
  168.9 48.8 all-gather.18
  344.5 61.4 all-reduce.75
  408.7 93.9 all-gather.20
  505.6 92.2 all-gather.22
  600.8 92.2 all-gather.24
  730.9 61.1 all-reduce.77
  1025.4 107.8 all-reduce.79
  1137.5 227.6 reduce-scatter.19
  1369.7 102.5 reduce-scatter.9
  1476.9 103.0 reduce-scatter.7
  1584.5 103.0 reduce-scatter.13
  1692.1 103.0 reduce-scatter.11
  1799.8 227.1 reduce-scatter.15
  2031.5 226.6 reduce-scatter.17
where the time goes:
time: 2280 us; the launch traced here: 2270 us
  waiting for transfers between devices  1480 us (65%)
  local copies, waits for them, and re-layouts  319 us (14%)
  matrix products  179 us (8%)
  other arithmetic  143 us (6%)
  blocking collectives  126 us (6%)
    reduce_scatter x1, waiting for transfers between devices, on_device(): lax.psum_scatter(grad_mgate, ('shard', 'ctx'), scatter_dimension=0, tiled...  232 us
    reduce_scatter x1, waiting for transfers between devices, on_device(): lax.psum_scatter(grad_mup, ('shard', 'ctx'), scatter_dimension=0, tiled=T...  231 us
    reduce_scatter x1, waiting for transfers between devices, on_device(): lax.psum_scatter(grad_down, ('shard', 'ctx'), scatter_dimension=0, tiled=...  154 us
    slice x57, local copies, waits for them, and re-layouts, on_device(): lax.associative_scan(linear_step, (next_decay, grad_state.reshape(seq_cou...  119 us
    reduce_scatter x1, waiting for transfers between devices, on_device(): lax.psum_scatter(grad_w_input, ('shard', 'ctx'), scatter_dimension=0, til...  108 us
    reduce_scatter x1, waiting for transfers between devices, on_device(): lax.psum_scatter(grad_out, ('shard', 'ctx'), scatter_dimension=0, tiled=T...  108 us
    reduce_scatter x1, waiting for transfers between devices, on_device(): lax.psum_scatter(grad_w_gate, ('shard', 'ctx'), scatter_dimension=0, tile...  108 us
    reduce_scatter x1, waiting for transfers between devices, on_device(): lax.psum_scatter(grad_w_forget, ('shard', 'ctx'), scatter_dimension=0, ti...  104 us
  transfers between devices with their start and end apart: 17, of which 15 were waited for; matrix products, arithmetic and copies ran while one was open for 16% of the time, Pallas kernels for 0%

commit v1 on v0

--- a/solution.py
+++ b/solution.py
@@ -1,9 +1,227 @@
+import functools
 import jax
 import jax.numpy as jnp
 from jax import lax
+from jax.experimental import pallas as pl
+from jax.experimental.pallas import tpu as pltpu
 from jax.sharding import PartitionSpec as P
 
 epsilon = 1e-06
+MESH = pl.DeviceIdType.MESH
+
+
+def remote(src, dst, send_sem, recv_sem, device):
+    return pltpu.make_async_remote_copy(
+        src_ref=src, dst_ref=dst, send_sem=send_sem, recv_sem=recv_sem,
+        device_id=device, device_id_type=MESH)
+
+
+def gather_body(nw, Z, ahead, relay, *refs):
+    own, out = refs[:nw], refs[nw:2 * nw]
+    (s_up, r_up, s_dn, r_dn, s_x, r_x, s_c, r_c, s_h, r_h, l_sem) = refs[2 * nw:]
+    s, z = lax.axis_index("shard"), lax.axis_index("ctx")
+    q, c = s // 2, lax.rem(s, 2)
+    sx, sc = (1 - q) * 2 + c, q * 2 + (1 - c)
+    sxc = (1 - q) * 2 + (1 - c)
+    even = lax.rem(z, 2) == 0
+    zp = jnp.where(even, z + 1, z - 1)
+    rows = [r.shape[0] for r in own]
+
+    def block(w, s_, z_, part=0):
+        R = rows[w]
+        start = pl.multiple_of((s_ * Z + z_) * R, R)
+        if part == 0:
+            return out[w].at[pl.ds(start, R), :]
+        H = R // 2
+        return out[w].at[pl.ds(pl.multiple_of(start + (part - 1) * H, H), H), :]
+
+    UP, DN, XX, CC, ZP = {"ctx": z + 1}, {"ctx": z - 1}, {"shard": sx}, {"shard": sc}, {"ctx": zp}
+
+    def up(w, k, src=None):
+        b = block(w, s, z - k)
+        return remote(b if src is None else src, b, s_up.at[w, k], r_up.at[w, k], UP)
+
+    def dn(w, k, src=None):
+        b = block(w, s, z + k)
+        return remote(b if src is None else src, b, s_dn.at[w, k], r_dn.at[w, k], DN)
+
+    def origin(j):
+        return z if j == 0 else (z - j if j < Z else z + j - Z + 1)
+
+    def valid(j):
+        return (z >= j) if j < Z else (z + j - Z + 1 <= Z - 1)
+
+    def xx(w, j, part, src=None):
+        b = block(w, s, origin(j), part)
+        return remote(b if src is None else src, b, s_x.at[w, j], r_x.at[w, j], XX)
+
+    def xx_in(w, j, part):
+        b = block(w, sx, origin(j), part)
+        return remote(b, b, s_x.at[w, j], r_x.at[w, j], XX)
+
+    def cc(w, j, src=None):
+        b = block(w, s if j < 2 * Z - 1 else sx, origin(j % (2 * Z - 1)))
+        return remote(b if src is None else src, b, s_c.at[w, j], r_c.at[w, j], CC)
+
+    def cc_in(w, j):
+        b = block(w, sc if j < 2 * Z - 1 else sxc, origin(j % (2 * Z - 1)))
+        return remote(b, b, s_c.at[w, j], r_c.at[w, j], CC)
+
+    def half(w):
+        b = block(w, sx, z, 1)
+        return remote(b, b, s_h.at[w], r_h.at[w], ZP)
+
+    def half_in(w):
+        b = block(w, sx, zp, 1)
+        return remote(b, b, s_h.at[w], r_h.at[w], ZP)
+
+    barrier = pltpu.get_barrier_semaphore()
+    for d in (XX, CC):
+        pl.semaphore_signal(barrier, inc=1, device_id=d, device_id_type=MESH)
+
+    @pl.when(z < Z - 1)
+    def _():
+        pl.semaphore_signal(barrier, inc=1, device_id=UP, device_id_type=MESH)
+
+    @pl.when(z > 0)
+    def _():
+        pl.semaphore_signal(barrier, inc=1, device_id=DN, device_id_type=MESH)
+
+    pl.semaphore_wait(barrier, 2 + (z < Z - 1).astype(jnp.int32) + (z > 0).astype(jnp.int32))
+
+    local = []
+    for w in range(nw):
+        cp = pltpu.make_async_copy(own[w], block(w, s, z), l_sem.at[w])
+        cp.start()
+        local.append(cp)
+
+    def begin(w):
+        @pl.when(z < Z - 1)
+        def _():
+            up(w, 0, own[w]).start()
+
+        @pl.when(z > 0)
+        def _():
+            dn(w, 0, own[w]).start()
+
+        xx(w, 0, 0, own[w]).start()
+        cc(w, 0, own[w]).start()
+
+    def is_pair(j):
+        if j == 1:
+            return jnp.logical_not(even)
+        if j == Z:
+            return even
+        return None
+
+    def for_part(w, j, fn):
+        pair = is_pair(j) if relay else None
+        if pair is None:
+            fn(0)
+        else:
+            @pl.when(pair)
+            def _():
+                fn(2)
+
+            @pl.when(jnp.logical_not(pair))
+            def _():
+                fn(0)
+
+    def step(w, k):
+        @pl.when(z >= k)
+        def _():
+            remote(block(w, s, z - k), block(w, s, z - k), s_up.at[w, k - 1], r_up.at[w, k - 1], UP).wait_recv()
+            if k < Z - 1:
+                @pl.when(z < Z - 1)
+                def _():
+                    up(w, k).start()
+            for_part(w, k, lambda p: xx(w, k, p).start())
+            cc(w, k).start()
+
+        @pl.when(z + k <= Z - 1)
+        def _():
+            remote(block(w, s, z + k), block(w, s, z + k), s_dn.at[w, k - 1], r_dn.at[w, k - 1], DN).wait_recv()
+            if k < Z - 1:
+                @pl.when(z > 0)
+                def _():
+                    dn(w, k).start()
+            for_part(w, Z - 1 + k, lambda p: xx(w, Z - 1 + k, p).start())
+            cc(w, Z - 1 + k).start()
+
+    def xstep(w, j):
+        @pl.when(valid(j))
+        def _():
+            for_part(w, j, lambda p: xx_in(w, j, p).wait_recv())
+            if j == 0:
+                if relay:
+                    half(w).start()
+                cc(w, 2 * Z - 1).start()
+            else:
+                if relay and is_pair(j) is not None:
+                    @pl.when(is_pair(j))
+                    def _():
+                        half_in(w).wait_recv()
+                cc(w, 2 * Z - 1 + j).start()
+
+    def finish(w):
+        for j in range(4 * Z - 2):
+            @pl.when(valid(j % (2 * Z - 1)))
+            def _():
+                cc_in(w, j).wait_recv()
+                cc(w, j).wait_send()
+        for j in range(2 * Z - 1):
+            @pl.when(valid(j))
+            def _():
+                for_part(w, j, lambda p: xx(w, j, p).wait_send())
+        for k in range(Z - 1):
+            @pl.when((z >= k) & (z < Z - 1))
+            def _():
+                up(w, k).wait_send()
+
+            @pl.when((z + k <= Z - 1) & (z > 0))
+            def _():
+                dn(w, k).wait_send()
+        if relay:
+            half(w).wait_send()
+        local[w].wait()
+
+    for w in range(min(ahead, nw)):
+        begin(w)
+    for w in range(nw):
+        for k in range(1, Z):
+            step(w, k)
+            if k == 1:
+                xstep(w, 0)
+                if w + ahead < nw:
+                    begin(w + ahead)
+            else:
+                xstep(w, k - 1)
+                xstep(w, Z - 1 + k - 1)
+            if w > 0 and k == 1:
+                xstep(w - 1, Z - 1)
+                xstep(w - 1, 2 * Z - 2)
+    xstep(nw - 1, Z - 1)
+    xstep(nw - 1, 2 * Z - 2)
+    for w in range(nw):
+        finish(w)
+
+
+def gather_all(shards, S, Z, collective_id=0, ahead=2, relay=True):
+    nw = len(shards)
+    dma = pltpu.SemaphoreType.DMA
+    return pl.pallas_call(
+        functools.partial(gather_body, nw, Z, ahead, relay),
+        out_shape=[jax.ShapeDtypeStruct((a.shape[0] * S * Z, a.shape[1]), a.dtype) for a in shards],
+        in_specs=[pl.BlockSpec(memory_space=pltpu.VMEM)] * nw,
+        out_specs=[pl.BlockSpec(memory_space=pl.ANY)] * nw,
+        scratch_shapes=[
+            dma((nw, Z - 1)), dma((nw, Z - 1)), dma((nw, Z - 1)), dma((nw, Z - 1)),
+            dma((nw, 2 * Z - 1)), dma((nw, 2 * Z - 1)),
+            dma((nw, 4 * Z - 2)), dma((nw, 4 * Z - 2)), dma((nw,)), dma((nw,)), dma((nw,)),
+        ],
+        compiler_params=pltpu.CompilerParams(collective_id=collective_id, has_side_effects=True),
+        name="weights_in",
+    )(*shards)
 
 
 def carried_in(x, axis, combine, identity, reverse):
@@ -96,17 +314,14 @@
     bfloat = jnp.bfloat16
     seq_count, span_len, model_width = block_input.shape
     rows_all = seq_count * span_len
-    wide_input, wide_forget, wide_gate, wide_out = (
-        lax.all_gather(w_input.astype(bfloat), ("shard", "ctx"), axis=0, tiled=True),
-        lax.all_gather(w_forget.astype(bfloat), ("shard", "ctx"), axis=0, tiled=True),
-        lax.all_gather(w_gate.astype(bfloat), ("shard", "ctx"), axis=0, tiled=True),
-        lax.all_gather(w_out.astype(bfloat), ("shard", "ctx"), axis=0, tiled=True),
-    )
-    wide_mgate, wide_mup, wide_down = (
-        lax.all_gather(w_mlp_gate.astype(bfloat), ("shard", "ctx"), axis=0, tiled=True),
-        lax.all_gather(w_mlp_up.astype(bfloat), ("shard", "ctx"), axis=0, tiled=True),
-        lax.all_gather(w_down.astype(bfloat), ("shard", "ctx"), axis=0, tiled=True),
-    )
+    shards = [
+        w.astype(bfloat) for w in (w_input, w_forget, w_gate, w_out, w_mlp_gate, w_mlp_up, w_down)
+    ]
+    if lax.axis_size("shard") == 4:
+        wide = gather_all(shards, 4, lax.axis_size("ctx"))
+    else:
+        wide = [lax.all_gather(w, ("shard", "ctx"), axis=0, tiled=True) for w in shards]
+    wide_input, wide_forget, wide_gate, wide_out, wide_mgate, wide_mup, wide_down = wide
     residual_in = block_input.reshape(rows_all, model_width)
     scale_one = inverse_rms(residual_in)
     normed_one = (residual_in * scale_one * norm_gain).astype(bfloat)
@@ -164,15 +379,6 @@
         jnp.float32
     )
     output = middle + mlp_out
-    wide_input, wide_forget, wide_gate, wide_out, wide_mgate, wide_mup, wide_down = (
-        lax.all_gather(w_input.astype(bfloat), ("shard", "ctx"), axis=0, tiled=True),
-        lax.all_gather(w_forget.astype(bfloat), ("shard", "ctx"), axis=0, tiled=True),
-        lax.all_gather(w_gate.astype(bfloat), ("shard", "ctx"), axis=0, tiled=True),
-        lax.all_gather(w_out.astype(bfloat), ("shard", "ctx"), axis=0, tiled=True),
-        lax.all_gather(w_mlp_gate.astype(bfloat), ("shard", "ctx"), axis=0, tiled=True),
-        lax.all_gather(w_mlp_up.astype(bfloat), ("shard", "ctx"), axis=0, tiled=True),
-        lax.all_gather(w_down.astype(bfloat), ("shard", "ctx"), axis=0, tiled=True),
-    )
     upstream = cotangent.reshape(rows_all, model_width)
     upstream_low = upstream.astype(bfloat)
     grad_activ = jnp.dot(upstream_low, wide_down, preferred_element_type=jnp.float32)
@@ -241,15 +447,15 @@
     grad_norm_gain = jnp.sum(grad_normed_one * residual_in * scale_one, axis=0)
     grad_resid = grad_middle + rms_backward(residual_in, scale_one, norm_gain, grad_normed_one)
     mlp_grads = (
-        lax.psum_scatter(grad_mgate, ("shard", "ctx"), scatter_dimension=0, tiled=True),
-        lax.psum_scatter(grad_mup, ("shard", "ctx"), scatter_dimension=0, tiled=True),
-        lax.psum_scatter(grad_down, ("shard", "ctx"), scatter_dimension=0, tiled=True),
+        lax.psum_scatter(grad_mgate.astype(bfloat), ("shard", "ctx"), scatter_dimension=0, tiled=True).astype(jnp.float32),
+        lax.psum_scatter(grad_mup.astype(bfloat), ("shard", "ctx"), scatter_dimension=0, tiled=True).astype(jnp.float32),
+        lax.psum_scatter(grad_down.astype(bfloat), ("shard", "ctx"), scatter_dimension=0, tiled=True).astype(jnp.float32),
     )
     mixer_grads = (
-        lax.psum_scatter(grad_w_input, ("shard", "ctx"), scatter_dimension=0, tiled=True),
-        lax.psum_scatter(grad_w_forget, ("shard", "ctx"), scatter_dimension=0, tiled=True),
-        lax.psum_scatter(grad_w_gate, ("shard", "ctx"), scatter_dimension=0, tiled=True),
-        lax.psum_scatter(grad_out, ("shard", "ctx"), scatter_dimension=0, tiled=True),
+        lax.psum_scatter(grad_w_input.astype(bfloat), ("shard", "ctx"), scatter_dimension=0, tiled=True).astype(jnp.float32),
+        lax.psum_scatter(grad_w_forget.astype(bfloat), ("shard", "ctx"), scatter_dimension=0, tiled=True).astype(jnp.float32),
+        lax.psum_scatter(grad_w_gate.astype(bfloat), ("shard", "ctx"), scatter_dimension=0, tiled=True).astype(jnp.float32),
+        lax.psum_scatter(grad_out.astype(bfloat), ("shard", "ctx"), scatter_dimension=0, tiled=True).astype(jnp.float32),
     )
     gain_grads = lax.psum(
         (grad_norm_gain, grad_lower, grad_hidden_gain, grad_mlp_gain), ("shard", "ctx")

time: 2280 us -> 1790 us (0.79)
  waiting for transfers between devices: 1480 us -> 714 us
  Pallas kernels: 0 us -> 271 us
    reduce_scatter x7 -> x6, waiting for transfers between devices: 1040 us -> 477 us  [the longest x1 128 us: on_device(): lax.psum_scatter(grad_mup.astype(bfloat), ('shard', 'ctx'), scatter_dimen...]
    all_gather x7 -> x0, waiting for transfers between devices: 329 us -> none  [the longest x1 89.5 us: on_device(): lax.all_gather(w_mlp_gate.astype(bfloat), ('shard', 'ctx'), axis=0, tiled...]
    pallas_call x0 -> x1, Pallas kernels: none -> 271 us  [gather_all(): pl.pallas_call(functools.partial(gather_body, nw, Z, ahead, relay), out_s...]
    unnamed x17 -> x11, waiting for transfers between devices: 0.28 us -> 129 us
  transfers between devices with their start and end apart: 17 -> 10, of which waited for: 15 -> 10; matrix products, arithmetic and copies ran while one was open for 16% -> 8% of each run, Pallas kernels for 0% -> 0%
where the time goes in v1:
time: 1790 us; the launch traced here: 1770 us
  waiting for transfers between devices  714 us (40%)
  local copies, waits for them, and re-layouts  333 us (19%)
  Pallas kernels  271 us (15%)
  matrix products  158 us (9%)
  other arithmetic  157 us (9%)
  blocking collectives  123 us (7%)
    pallas_call x1, Pallas kernels, gather_all(): pl.pallas_call(functools.partial(gather_body, nw, Z, ahead, relay), out_s...  271 us
    unnamed x11, waiting for transfers between devices  129 us
    reduce_scatter x1, waiting for transfers between devices, on_device(): lax.psum_scatter(grad_mup.astype(bfloat), ('shard', 'ctx'), scatter_dimen...  128 us
    reduce_scatter x1, waiting for transfers between devices, on_device(): lax.psum_scatter(grad_mgate.astype(bfloat), ('shard', 'ctx'), scatter_dim...  128 us
    slice x57, local copies, waits for them, and re-layouts, on_device(): lax.associative_scan(linear_step, (next_decay, grad_state.reshape(seq_cou...  122 us
    slice x52, local copies, waits for them, and re-layouts, on_device(): lax.associative_scan(linear_step, (decay_rate, candidate.reshape(seq_coun...  85.9 us
    reduce_scatter x1, waiting for transfers between devices, on_device(): lax.psum_scatter(grad_out.astype(bfloat), ('shard', 'ctx'), scatter_dimen...  73.9 us
    reduce_scatter x1, waiting for transfers between devices, on_device(): lax.psum_scatter(grad_w_forget.astype(bfloat), ('shard', 'ctx'), scatter_...  73.8 us
  transfers between devices with their start and end apart: 10, of which 10 were waited for; matrix products, arithmetic and copies ran while one was open for 8% of the time, Pallas kernels for 0%

profile of v1, /device:TPU:0, one launch (start us, length us, event | category | flops | bytes accessed | tf_op | source)
XLA Modules:
  0.0 1772.9 jit_solution(8226616072865317537)
XLA Ops:
  17.2 271.3 %weights_in.1 = (bf16[2048,1024]{1,0:T(8,128)(2,1)}, bf16[2048,1024]{1,0:T(8,128)(2,1)}, bf16[2048,1024]{1,0:T(8,128)(2,1)}, bf16[2048,1024]{1,0:T(8,128)(2,1)},...) custom-call(bf16[128,1024]{1,0:T(8,128)(2,1)} %convert_element_type.127.refs_0_, ...), custom_call_target="tpu_custom_call" | custom-call | tf_op jit(solution)/shard_map/weights_in/pallas_call | solution.py:212
  288.5 4.9 add_divide_fusion.2
  293.4 7.1 subtract_multiply_fusion
  394.5 5.6 slice.570
  434.2 5.3 pad.230
  454.5 5.3 pad.229
  460.7 13.1 all-gather
  475.7 10.8 all-reduce.70
  495.8 13.1 all-gather.2
  509.6 5.2 multiply_reduce_fusion.4
  514.8 4.9 psum.70
  519.8 7.6 fusion.34
  535.0 56.5 %all-reduce.76.cloned.1.call-done = bf16[512,2048]{1,0:T(8,128)(2,1)} async-done(((bf16[512,2048]{1,0:T(8,128)(2,1)}), bf16[512,2048]{1,0:T(8,128)(2,1)}) %all-reduce.76.cloned.1.call-update) | async-done | bytes 2097168 | tf_op jit(solution)/shard_map/psum | solution.py:368
  597.1 12.8 fusion.74
  610.0 8.0 fusion.75
  618.0 15.3 fusion.10
  633.3 12.3 fusion.76
  645.6 9.0 add_convert_fusion.1
  661.6 8.9 slice.593
  670.5 9.0 slice.602
  679.5 5.2 slice.595
  687.5 10.0 convolution_convert_fusion.7
  697.5 20.3 %all-reduce.78.cloned.1.call-done = bf16[512,2048]{1,0:T(8,128)(2,1)} async-done(((bf16[512,2048]{1,0:T(8,128)(2,1)}), bf16[512,2048]{1,0:T(8,128)(2,1)}) %all-reduce.78.cloned.1.call-update) | async-done | bytes 2097168 | tf_op jit(solution)/shard_map/psum | solution.py:390
  726.6 5.5 multiply_reduce_fusion.2
  732.1 4.9 psum.74
  741.7 5.7 slice.598
  747.9 8.9 slice.599
  756.8 5.2 slice.597
  842.3 9.0 slice.655
  881.4 16.8 rev.8
  908.4 16.8 rev.9
  925.3 13.2 all-gather.4
  938.5 6.3 while.35
  962.4 5.6 convolution_convert_fusion.5
  979.4 6.6 convolution_convert_fusion.2
  987.9 10.7 convert_bitcast_fusion
  998.6 15.5 copy.36
  1015.7 10.7 convolution_convert_fusion.1
  1026.5 10.7 convolution_convert_fusion
  1037.9 31.0 %all-reduce.80.cloned.1.call-done = (bf16[512,2048]{1,0:T(8,128)(2,1)}, bf16[512,2048]{1,0:T(8,128)(2,1)}) async-done(((bf16[512,2048]{1,0:T(8,128)(2,1)}, bf16[512,2048]{1,0:T(8,128)(2,1)}), (bf16[512,2048]{1,0:T(8,128)(2,1)}, bf16[512,2048]{1,0:T(8,128)(2,1)})) %all-reduce.80.cloned.1.call-update) | async-done | bytes 4194320 | tf_op jit(solution)/shard_map/psum | solution.py:378
  1073.2 62.4 %all-reduce.69 = (f32[2048]{0:T(1024)}, f32[1024]{0:T(1024)}, f32[1024]{0:T(1024)}, f32[2048]{0:T(1024)}) all-reduce(f32[2048]{0:T(1024)S(1)} %get-tuple-element.467, f32[1024]{0:T(1024)S(1)} %get-tuple-element.524, f32[1024]{0:T(1024)S(1)} %copy-done.96, ...), channel_id=1, replica_groups=mesh['shard'=4,'ctx'=4,'tp'=2] {'shard','ctx'}, use_global_device_ids=true, to_apply=%region_17.18 | all-reduce | flops 6144 | bytes 49152 | tf_op jit(solution)/shard_map/psum | solution.py:460
  1135.6 5.4 convert_add_fusion
  1147.7 73.8 %reduce-scatter.12.cloned.1.call-done = bf16[128,1024]{1,0:T(8,128)(2,1)} async-done(((bf16[2048,1024]{1,0:T(8,128)(2,1)}), bf16[128,1024]{1,0:T(8,128)(2,1)}) %reduce-scatter.12.cloned.1.call-update) | async-done | bytes 262160 | tf_op jit(solution)/shard_map/reduce_scatter | solution.py:456
  1223.3 73.5 %reduce-scatter.14.cloned.1.call-done = bf16[128,1024]{1,0:T(8,128)(2,1)} async-done(((bf16[2048,1024]{1,0:T(8,128)(2,1)}), bf16[128,1024]{1,0:T(8,128)(2,1)}) %reduce-scatter.14.cloned.1.call-update) | async-done | bytes 262160 | tf_op jit(solution)/shard_map/reduce_scatter | solution.py:457
  1298.5 73.9 %reduce-scatter.16.cloned.1.call-done = bf16[128,1024]{1,0:T(8,128)(2,1)} async-done(((bf16[2048,1024]{1,0:T(8,128)(2,1)}), bf16[128,1024]{1,0:T(8,128)(2,1)}) %reduce-scatter.16.cloned.1.call-update) | async-done | bytes 262160 | tf_op jit(solution)/shard_map/reduce_scatter | solution.py:458
  1374.2 128.4 %reduce-scatter.22.cloned.1.call-done = bf16[128,2816]{1,0:T(8,128)(2,1)} async-done(((bf16[2048,2816]{1,0:T(8,128)(2,1)}), bf16[128,2816]{1,0:T(8,128)(2,1)}) %reduce-scatter.22.cloned.1.call-update) | async-done | bytes 720912
  1505.5 127.7 %reduce-scatter.18.cloned.1.call-done = bf16[128,2816]{1,0:T(8,128)(2,1)} async-done(((bf16[2048,2816]{1,0:T(8,128)(2,1)}), bf16[128,2816]{1,0:T(8,128)(2,1)}) %reduce-scatter.18.cloned.1.call-update) | async-done | bytes 720912 | tf_op jit(solution)/shard_map/reduce_scatter | solution.py:450
  1635.5 128.1 %reduce-scatter.20.cloned.1.call-done = bf16[128,2816]{1,0:T(8,128)(2,1)} async-done(((bf16[2048,2816]{1,0:T(8,128)(2,1)}), bf16[128,2816]{1,0:T(8,128)(2,1)}) %reduce-scatter.20.cloned.1.call-update) | async-done | bytes 720912 | tf_op jit(solution)/shard_map/reduce_scatter | solution.py:451
  (598 shorter events, 384.6 us)
Async XLA Ops:
  7.2 584.4 %all-reduce.76.cloned.1.call-start = ((), (), s32[]{:S(2)}) async-start(), calls=%async_computation.7 | async-start | bytes 4194304 | tf_op jit(solution)/shard_map/psum | solution.py:368
  15.8 277.6 %copy-start.90 = (f32[1024]{0:T(1024)}, f32[1024]{0:T(1024)S(1)}, u32[]{:S(2)}) copy-start(f32[1024]{0:T(1024)S(1)} %broadcast_subtract_fusion) | copy-start | bytes 12292
  17.1 276.2 %copy-start.26 = (bf16[512,2048]{1,0:T(8,128)(2,1)}, bf16[512,2048]{1,0:T(8,128)(2,1)S(1)}, u32[]{:S(2)}) copy-start(bf16[512,2048]{1,0:T(8,128)(2,1)S(1)} %fusion.27) | copy-start | bytes 6291460
  394.5 11.4 copy-start.82
  394.5 11.4 copy-start.83
  394.5 11.4 copy-start.84
  394.5 11.4 copy-start.85
  394.5 11.5 copy-start.64
  454.5 19.4 %copy-start.107 = (u32[32]{0:T(128)S(1)}, u32[32]{0:T(128)}, u32[]{:S(2)}) copy-start(u32[32]{0:T(128)} %constant.273) | copy-start | bytes 388
  454.5 20.7 %copy-start.100 = (f32[2]{0:T(128)S(1)}, f32[2]{0:T(128)}, u32[]{:S(2)}) copy-start(f32[2]{0:T(128)} %get-tuple-element.470) | copy-start | bytes 28
  454.5 20.9 %copy-start.98 = (f32[2]{0:T(128)S(1)}, f32[2]{0:T(128)}, u32[]{:S(2)}) copy-start(f32[2]{0:T(128)} %get-tuple-element.469) | copy-start | bytes 28
  454.5 32.1 %copy-start.20 = (f32[2,128,1024]{2,1,0:T(8,128)S(1)}, f32[2,128,1024]{2,1,0:T(8,128)}, u32[]{:S(2)}) copy-start(f32[2,128,1024]{2,1,0:T(8,128)} %add.541) | copy-start | bytes 3145732
  491.4 17.7 copy-start.92
  531.1 186.7 %all-reduce.78.cloned.1.call-start = ((), (), s32[]{:S(2)}) async-start(), calls=%async_computation.8 | async-start | bytes 4194304 | tf_op jit(solution)/shard_map/psum | solution.py:390
  535.0 60.0 %copy-start.59 = (f32[2048]{0:T(1024)S(1)}, f32[2048]{0:T(1024)}, u32[]{:S(2)}) copy-start(f32[2048]{0:T(1024)} %param.27) | copy-start | bytes 24580
  595.0 14.9 slice-start
  597.1 12.8 copy-start.28
  597.1 12.8 slice-start.1
  597.1 12.8 slice-start.2
  618.0 27.6 %slice-start.3 = ((s8[11534336]{0:T(1024)(128)(4,1)}), s8[3145728]{0:T(1024)(128)(4,1)S(1)}, s32[]{:S(2)}) async-start(s8[11534336]{0:T(1024)(128)(4,1)} %bitcast.223), calls=%async_computation.20 | async-start | bytes 6291456
  618.0 27.6 %slice-start.4 = ((s8[11534336]{0:T(1024)(128)(4,1)}), s8[4194304]{0:T(1024)(128)(4,1)S(1)}, s32[]{:S(2)}) async-start(s8[11534336]{0:T(1024)(128)(4,1)} %bitcast.223), calls=%async_computation.21 | async-start | bytes 8388608
  633.3 12.3 copy-start.113
  633.3 12.3 slice-start.5
  654.7 414.2 %all-reduce.80.cloned.1.call-start = ((), (), s32[]{:S(2)}) async-start(), calls=%async_computation.16 | async-start | bytes 8388608 | tf_op jit(solution)/shard_map/psum | solution.py:378
  670.5 14.2 copy-start.4
  670.5 14.2 copy-start.89
  839.4 11.9 copy-start.80
  839.4 11.9 copy-start.81
  839.4 12.0 copy-start.62
  839.4 12.1 copy-start.63
  839.4 12.2 copy-start.78
  839.4 12.2 copy-start.79
  839.4 12.2 copy-start.57
  839.4 12.2 copy-start.58
  839.4 12.3 copy-start.77
  881.4 16.8 copy-start.23
  908.4 30.1 %copy-start.93 = (f32[2]{0:T(128)S(1)}, f32[2]{0:T(128)}, u32[]{:S(2)}) copy-start(f32[2]{0:T(128)} %custom-call.3) | copy-start | bytes 28
  908.4 36.4 %copy-start.99 = (f32[2]{0:T(128)S(1)}, f32[2]{0:T(128)}, u32[]{:S(2)}) copy-start(f32[2]{0:T(128)} %get-tuple-element.469) | copy-start | bytes 28
  908.4 36.5 %copy-start.13 = (f32[2,256,1024]{2,1,0:T(8,128)S(1)}, f32[2,256,1024]{2,1,0:T(8,128)}, u32[]{:S(2)}) copy-start(f32[2,256,1024]{2,1,0:T(8,128)} %rev.8) | copy-start | bytes 6291460
  960.8 185.1 %reduce-scatter.10.cloned.1.call-start = ((), (), s32[]{:S(2)}) async-start(), calls=%async_computation.9 | async-start | bytes 4456448 | tf_op jit(solution)/shard_map/reduce_scatter | solution.py:455
  968.0 253.5 %reduce-scatter.12.cloned.1.call-start = ((), (), s32[]{:S(2)}) async-start(), calls=%async_computation.10 | async-start | bytes 4456448 | tf_op jit(solution)/shard_map/reduce_scatter | solution.py:456
  972.7 324.0 %reduce-scatter.14.cloned.1.call-start = ((), (), s32[]{:S(2)}) async-start(), calls=%async_computation.11 | async-start | bytes 4456448 | tf_op jit(solution)/shard_map/reduce_scatter | solution.py:457
  978.2 394.2 %reduce-scatter.16.cloned.1.call-start = ((), (), s32[]{:S(2)}) async-start(), calls=%async_computation.12 | async-start | bytes 4456448 | tf_op jit(solution)/shard_map/reduce_scatter | solution.py:458
  986.1 516.5 %reduce-scatter.22.cloned.1.call-start = ((), (), s32[]{:S(2)}) async-start(), calls=%async_computation.15 | async-start | bytes 12255232
  1014.1 619.1 %reduce-scatter.18.cloned.1.call-start = ((), (), s32[]{:S(2)}) async-start(), calls=%async_computation.13 | async-start | bytes 12255232 | tf_op jit(solution)/shard_map/reduce_scatter | solution.py:450
  1026.4 737.1 %reduce-scatter.20.cloned.1.call-start = ((), (), s32[]{:S(2)}) async-start(), calls=%async_computation.14 | async-start | bytes 12255232 | tf_op jit(solution)/shard_map/reduce_scatter | solution.py:451
  1037.2 31.7 %copy-start.61 = (f32[2048]{0:T(1024)S(1)}, f32[2048]{0:T(1024)}, u32[]{:S(2)}) copy-start(f32[2048]{0:T(1024)} %param.20) | copy-start | bytes 24580
  1068.9 66.7 %copy-start.32 = (bf16[512,2048]{1,0:T(8,128)(2,1)S(1)}, bf16[512,2048]{1,0:T(8,128)(2,1)}, u32[]{:S(2)}) copy-start(bf16[512,2048]{1,0:T(8,128)(2,1)} %get-tuple-element.509) | copy-start | bytes 6291460
  (82 other events, 335.4 us)
Sparse Core Ops, SparseCore 0:
  531.3 60.2 all-reduce.75
  654.8 62.9 all-reduce.77
  960.9 107.9 all-reduce.79
  1072.6 73.2 reduce-scatter.9
  1149.6 71.8 reduce-scatter.11
  1225.2 71.5 reduce-scatter.13
  1300.6 71.8 reduce-scatter.15
  1376.5 126.0 reduce-scatter.21
  1506.8 126.3 reduce-scatter.17
  1637.1 126.3 reduce-scatter.19

commit v2 on v1

--- a/solution.py
+++ b/solution.py
@@ -224,6 +224,676 @@
     )(*shards)
 
 
+def pick(z, values):
+    out = jnp.int32(values[-1])
+    for k in range(len(values) - 2, -1, -1):
+        out = jnp.where(z == k, values[k], out)
+    return out
+
+
+def far_first(Z):
+    table = []
+    for z in range(Z):
+        ups, dns, mine, turn = list(range(Z - 1, z, -1)), list(range(0, z)), [], z < Z // 2
+        while ups or dns:
+            if (turn and ups) or not dns:
+                mine.append(ups.pop(0))
+            else:
+                mine.append(dns.pop(0))
+            turn = not turn
+        table.append(mine + [z])
+    return table
+
+
+def cross_order(Z):
+    table = []
+    for z in range(Z):
+        zp = z ^ 1
+        table.append([zp] + [k for k in range(Z) if k not in (z, zp)] + [z])
+    return table
+
+
+class Scatter:
+    def __init__(self, Z, parts, rc, xr, zu, zd, hr, outs, xs, zs, stage, fin, sems):
+        self.Z, self.parts, self.rc, self.xr, self.zu, self.zd, self.hr, self.outs = Z, parts, rc, xr, zu, zd, hr, outs
+        self.xs, self.zs, self.stage, self.fin = xs, zs, stage, fin
+        (self.c_s, self.c_r, self.x_s, self.x_r, self.z_s, self.u_r, self.d_r, self.h_s, self.h_r, self.l_s, self.f_s) = sems
+        s, z = lax.axis_index("shard"), lax.axis_index("ctx")
+        q, c = s // 2, lax.rem(s, 2)
+        self.z, self.q, self.c = z, q, c
+        self.even = lax.rem(z, 2) == 0
+        self.zp = jnp.where(self.even, z + 1, z - 1)
+        self.X = {"shard": (1 - q) * 2 + c}
+        self.C = {"shard": q * 2 + (1 - c)}
+        self.UP, self.DN, self.ZP = {"ctx": z + 1}, {"ctx": z - 1}, {"ctx": self.zp}
+        self.R = [p.shape[0] // (4 * Z) for p in parts]
+        self.N = [p.shape[1] for p in parts]
+        self.ffirst = far_first(Z)
+        self.xorder = cross_order(Z)
+
+    def part(self, w, q, c, z, n=1):
+        R = self.R[w]
+        return self.parts[w].at[pl.ds(pl.multiple_of(((2 * q + c) * self.Z + z) * R, R), n * R), :]
+
+    def rows(self, ref, i, w):
+        R = self.R[w]
+        return ref.at[pl.ds(pl.multiple_of(i * R, R), R), :]
+
+    def hrows(self, ref, i, w, h):
+        H = self.R[w] // 2
+        return ref.at[pl.ds(pl.multiple_of(i * 2 * H + h * H, H), H), :]
+
+    def c_copy(self, w, k):
+        Z, R = self.Z, self.R[w]
+        q = self.q if k == 1 else 1 - self.q
+        return remote(self.part(w, q, 1 - self.c, 0, Z), self.rc[w].at[pl.ds(k * Z * R, Z * R), :],
+                      self.c_s.at[w, k], self.c_r.at[w, k], self.C)
+
+    def c_send(self, w):
+        for k in (0, 1):
+            self.c_copy(w, k).start()
+
+    def load(self, w, srcs, slot):
+        cps = []
+        for i, src in enumerate(srcs):
+            if src is None:
+                continue
+            n = src.shape[0]
+            cp = pltpu.make_async_copy(src, self.stage.at[slot, i, pl.ds(0, n), pl.ds(0, self.N[w])], self.l_s.at[slot, i])
+            cp.start()
+            cps.append(cp)
+        return cps
+
+    def add(self, w, slot, idx, store, lo=0, hi=None, off=None):
+        N = self.N[w]
+        hi = self.R[w] if hi is None else hi
+        G = 16
+
+        def go(i, _):
+            r = pl.multiple_of(lo + i * G, G)
+            tot = None
+            for k in idx:
+                rk = r
+                if off is not None and k in off:
+                    rk = pl.multiple_of(r + off[k], G)
+                v = self.stage[slot, k, pl.ds(rk, G), pl.ds(0, N)].astype(jnp.float32)
+                tot = v if tot is None else tot + v
+            store(r, tot)
+            return 0
+
+        lax.fori_loop(0, (hi - lo) // G, go, 0)
+
+    def x_slot(self, w, n):
+        return self.xs.at[w % 2, n, :, pl.ds(0, self.N[w])]
+
+    def x_copy(self, w, n, half=None):
+        zt = pick(self.z, [t[n] for t in self.xorder])
+        src = self.x_slot(w, n)
+        H = self.R[w] // 2
+        if half is None:
+            return remote(src, self.rows(self.xr[w], zt, w), self.x_s.at[w, n], self.x_r.at[w, n], self.X)
+        return remote(src.at[pl.ds(half * H, H), :], self.hrows(self.xr[w], zt, w, half), self.x_s.at[w, n], self.x_r.at[w, n], self.X)
+
+    def h_copy(self, w):
+        H = self.R[w] // 2
+        return remote(self.x_slot(w, 0).at[pl.ds(0, H), :], self.hr[w], self.h_s.at[w], self.h_r.at[w], self.ZP)
+
+    def x_phase(self, w, n):
+        Z, H = self.Z, self.R[w] // 2
+        if n == 0:
+            self.c_copy(w, 0).wait_recv()
+        zt = pick(self.z, [t[n] for t in self.xorder])
+        last = n == Z - 1
+        cps = self.load(w, [self.part(w, 1 - self.q, self.c, zt), self.rows(self.rc[w], zt, w)], 0)
+        if last:
+            self.h_copy(w).wait_recv()
+            cps += self.load(w, [None, None, self.hr[w]], 0)
+        if w >= 2:
+            self.x_wait_send(w - 2, n)
+        for cp in cps:
+            cp.wait()
+        dst = self.x_slot(w, n)
+
+        def store(r, v):
+            dst[pl.ds(r, 16), :] = v.astype(jnp.bfloat16)
+
+        if last:
+            self.add(w, 0, (0, 1, 2), store, 0, H)
+            self.add(w, 0, (0, 1), store, H, 2 * H)
+        else:
+            self.add(w, 0, (0, 1), store)
+        if n == 0:
+            self.h_copy(w).start()
+            self.x_copy(w, 0, 1).start()
+        else:
+            self.x_copy(w, n).start()
+
+    def x_wait_send(self, w, n):
+        if n == 0:
+            self.h_copy(w).wait_send()
+            self.x_copy(w, 0, 1).wait_send()
+        else:
+            self.x_copy(w, n).wait_send()
+
+    def z_copy(self, w, n, dest, up):
+        src = self.zs.at[w % 2, n, :, pl.ds(0, self.N[w])]
+        if up:
+            return remote(src, self.rows(self.zu[w], dest, w), self.z_s.at[w, n], self.u_r.at[w, dest], self.UP)
+        return remote(src, self.rows(self.zd[w], dest, w), self.z_s.at[w, n], self.d_r.at[w, dest], self.DN)
+
+    def x_wait(self, w, zt):
+        for n in range(self.Z):
+            @pl.when(zt == pick(self.z, [t[n] for t in self.xorder]))
+            def _():
+                self.x_copy(w, n, 1 if n == 0 else None).wait_recv()
+
+    def z_phase(self, w, n):
+        Z, H = self.Z, self.R[w] // 2
+        z = self.z
+        last = n == Z - 1
+        dest = z if last else pick(z, [t[n] for t in self.ffirst])
+        if n == 0:
+            self.c_copy(w, 1).wait_recv()
+        self.x_wait(w, dest)
+        cps = self.load(w, [self.part(w, self.q, self.c, dest), self.rows(self.rc[w], dest + Z, w),
+                            self.rows(self.xr[w], dest, w)], 1)
+        if not last:
+            up = dest > z
+            down = dest < z
+            has_in = (up & (z > 0)) | (down & (z < Z - 1))
+
+            @pl.when(up & (z > 0))
+            def _():
+                self.z_copy(w, n, dest, True).wait_recv()
+                cp = self.load(w, [None] * 3 + [self.rows(self.zu[w], dest, w)], 1)
+                cp[0].wait()
+
+            @pl.when(down & (z < Z - 1))
+            def _():
+                self.z_copy(w, n, dest, False).wait_recv()
+                cp = self.load(w, [None] * 3 + [self.rows(self.zd[w], dest, w)], 1)
+                cp[0].wait()
+
+            if w >= 2:
+                self.z_wait_send(w - 2, n)
+            for cp in cps:
+                cp.wait()
+            dst = self.zs.at[w % 2, n, :, pl.ds(0, self.N[w])]
+
+            def store(r, v):
+                dst[pl.ds(r, 16), :] = v.astype(jnp.bfloat16)
+
+            paired = dest == self.zp
+            self.sum_parts(w, paired, has_in, (3,), store)
+
+            @pl.when(up)
+            def _():
+                self.z_copy(w, n, dest, True).start()
+
+            @pl.when(down)
+            def _():
+                self.z_copy(w, n, dest, False).start()
+        else:
+            @pl.when(z > 0)
+            def _():
+                self.z_copy(w, 0, dest, True).wait_recv()
+                cp = self.load(w, [None] * 3 + [self.rows(self.zu[w], dest, w)], 1)
+                cp[0].wait()
+
+            @pl.when(z < Z - 1)
+            def _():
+                self.z_copy(w, 0, dest, False).wait_recv()
+                cp = self.load(w, [None] * 4 + [self.rows(self.zd[w], dest, w)], 1)
+                cp[0].wait()
+
+            for cp in cps:
+                cp.wait()
+            if w >= 1:
+                self.f_copy(w - 1).wait()
+            dst = self.fin.at[:, pl.ds(0, self.N[w])]
+
+            def store(r, v):
+                dst[pl.ds(r, 16), :] = v
+
+            @pl.when((z > 0) & (z < Z - 1))
+            def _():
+                self.add(w, 1, (0, 1, 2, 3, 4), store)
+
+            @pl.when(z == 0)
+            def _():
+                self.add(w, 1, (0, 1, 2, 4), store)
+
+            @pl.when(z == Z - 1)
+            def _():
+                self.add(w, 1, (0, 1, 2, 3), store)
+
+            self.f_copy(w).start()
+
+    def sum_parts(self, w, paired, has_in, extra, store):
+        H = self.R[w] // 2
+        for p in (False, True):
+            for e in (False, True):
+                cond = (paired if p else jnp.logical_not(paired)) & (has_in if e else jnp.logical_not(has_in))
+
+                @pl.when(cond)
+                def _(p=p, e=e):
+                    ex = extra if e else ()
+                    if p:
+                        self.add(w, 1, (0, 1) + ex, store, 0, H)
+                        self.add(w, 1, (0, 1, 2) + ex, store, H, 2 * H)
+                    else:
+                        self.add(w, 1, (0, 1, 2) + ex, store)
+
+    def z_wait_send(self, w, n):
+        z = self.z
+        dest = pick(z, [t[n] for t in self.ffirst])
+        self.z_copy_any(w, n).wait_send()
+
+    def z_copy_any(self, w, n):
+        src = self.zs.at[w % 2, n, :, pl.ds(0, self.N[w])]
+        return remote(src, self.rows(self.zu[w], 0, w), self.z_s.at[w, n], self.u_r.at[w, 0],
+                      {"ctx": jnp.where(pick(self.z, [t[n] for t in self.ffirst]) > self.z, self.z + 1, self.z - 1)})
+
+    def f_copy(self, w):
+        return pltpu.make_async_copy(self.fin.at[:, pl.ds(0, self.N[w])], self.outs[w], self.f_s.at[w])
+
+    def drain(self, w, nw):
+        for k in (0, 1):
+            self.c_copy(w, k).wait_send()
+        if w >= nw - 2:
+            for n in range(self.Z):
+                self.x_wait_send(w, n)
+            for n in range(self.Z - 1):
+                self.z_wait_send(w, n)
+        if w == nw - 1:
+            self.f_copy(w).wait()
+
+
+def scatter_body(nw, Z, *refs):
+    parts = refs[:nw]
+    vec, vec_out = refs[nw], refs[nw + 1]
+    outs = refs[nw + 2:2 * nw + 2]
+    rc, xr, zu, zd, hr = (refs[2 + (2 + k) * nw:2 + (3 + k) * nw] for k in range(5))
+    xs, zs, stage, fin, vsum, vgot, vbox = refs[7 * nw + 2:7 * nw + 9]
+    v_s, v_r, vz_s, vz_r = refs[7 * nw + 9:7 * nw + 13]
+    sems = refs[7 * nw + 13:]
+    sc = Scatter(Z, parts, rc, xr, zu, zd, hr, outs, xs, zs, stage, fin, sems)
+    far = [{"ctx": lax.rem(sc.z + o, Z)} for o in range(1, Z)]
+    barrier = pltpu.get_barrier_semaphore()
+    for d in [sc.X, sc.C] + far:
+        pl.semaphore_signal(barrier, inc=1, device_id=d, device_id_type=MESH)
+    pl.semaphore_wait(barrier, 1 + Z)
+    first = remote(vec, vgot.at[0], v_s.at[0], v_r.at[0], sc.C)
+    first.start()
+    for w in range(nw):
+        sc.c_send(w)
+    first.wait()
+    vsum[...] = vec[...] + vgot[0]
+    for n in range(Z):
+        sc.x_phase(0, n)
+    second = remote(vsum, vgot.at[1], v_s.at[1], v_r.at[1], sc.X)
+    second.start()
+    for n in range(Z):
+        sc.x_phase(1, n)
+    second.wait()
+    vsum[...] = vsum[...] + vgot[1]
+    for n in range(Z):
+        sc.z_phase(0, n)
+    cps = spread(Z, sc.z, vsum, vbox, vz_s, vz_r)
+    for w in range(1, nw):
+        if w + 1 < nw:
+            for n in range(Z):
+                sc.x_phase(w + 1, n)
+        for n in range(Z):
+            sc.z_phase(w, n)
+    spread_wait(Z, sc.z, vsum, vbox, vz_s, vz_r, cps)
+    total = vbox[0]
+    for k in range(1, Z):
+        total = total + vbox[k]
+    vec_out[...] = total
+    for w in range(nw):
+        sc.drain(w, nw)
+
+
+def scatter_all(parts, vec, Z, collective_id=1):
+    nw = len(parts)
+    dma = pltpu.SemaphoreType.DMA
+    bf = jnp.bfloat16
+    R = [p.shape[0] // (4 * Z) for p in parts]
+    N = [p.shape[1] for p in parts]
+    Rm, Nm = max(R), max(N)
+    sh = jax.ShapeDtypeStruct
+    vmem = pl.BlockSpec(memory_space=pltpu.VMEM)
+    anyw = pl.BlockSpec(memory_space=pl.ANY)
+    out_shape = ([sh(vec.shape, jnp.float32)] + [sh((r, n), jnp.float32) for r, n in zip(R, N)]
+                 + [sh((2 * Z * r, n), bf) for r, n in zip(R, N)]
+                 + [sh((Z * r, n), bf) for r, n in zip(R, N)]
+                 + [sh((Z * r, n), bf) for r, n in zip(R, N)]
+                 + [sh((Z * r, n), bf) for r, n in zip(R, N)]
+                 + [sh((r // 2, n), bf) for r, n in zip(R, N)])
+    res = pl.pallas_call(
+        functools.partial(scatter_body, nw, Z),
+        out_shape=out_shape,
+        in_specs=[anyw] * nw + [vmem],
+        out_specs=[vmem] + [anyw] * (len(out_shape) - 1),
+        scratch_shapes=[
+            pltpu.VMEM((2, Z, Rm, Nm), bf), pltpu.VMEM((2, Z - 1, Rm, Nm), bf), pltpu.VMEM((2, 5, Rm, Nm), bf),
+            pltpu.VMEM((Rm, Nm), jnp.float32),
+            pltpu.VMEM(vec.shape, jnp.float32), pltpu.VMEM((2,) + vec.shape, jnp.float32), pltpu.VMEM((Z,) + vec.shape, jnp.float32),
+            dma((2,)), dma((2,)), dma((Z - 1,)), dma((Z,)),
+            dma((nw, 2)), dma((nw, 2)), dma((nw, Z)), dma((nw, Z)), dma((nw, Z - 1)), dma((nw, Z)), dma((nw, Z)),
+            dma((nw,)), dma((nw,)), dma((2, 5)), dma((nw,)),
+        ],
+        compiler_params=pltpu.CompilerParams(collective_id=collective_id, has_side_effects=True),
+        name="grads_out",
+    )(*parts, vec)
+    return res[0], res[1:nw + 1]
+
+
+T8 = 8
+
+
+def spread(Z, z, pay, box, s_sem, r_sem):
+    cps = []
+    for o in range(1, Z):
+        to = lax.rem(z + o, Z)
+        cp = remote(pay, box.at[z], s_sem.at[o - 1], r_sem.at[z], {"ctx": to})
+        cp.start()
+        cps.append(cp)
+    box[z] = pay[...]
+    return cps
+
+
+def spread_wait(Z, z, pay, box, s_sem, r_sem, cps):
+    for o in range(1, Z):
+        frm = lax.rem(z + o, Z)
+        remote(pay, box.at[frm], s_sem.at[o - 1], r_sem.at[frm], {"ctx": frm}).wait_recv()
+    for cp in cps:
+        cp.wait_send()
+
+
+def joined(box, k):
+    last, first = box[k, 6:8, :], box[k + 1, 4:6, :]
+    return jnp.where(last == first, 1.0, 0.0)
+
+
+def prefix_state(Z, z, box):
+    state = jnp.zeros(box.shape[2:][:0] + (2, box.shape[2]), jnp.float32)
+    mine = state
+    for k in range(Z - 1):
+        state = joined(box, k) * (box[k, 2:4, :] + box[k, 0:2, :] * state)
+        mine = jnp.where(z == k + 1, state, mine)
+    return mine
+
+
+def suffix_state(Z, z, box):
+    state = jnp.zeros((2, box.shape[2]), jnp.float32)
+    mine = state
+    for k in range(Z - 2, -1, -1):
+        state = joined(box, k) * (box[k + 1, 2:4, :] + box[k + 1, 0:2, :] * state)
+        mine = jnp.where(z == k, state, mine)
+    return mine
+
+
+def diagonal():
+    return lax.broadcasted_iota(jnp.int32, (128, 128), 0) == lax.broadcasted_iota(jnp.int32, (128, 128), 1)
+
+
+def column_to_rows(col_ref, row_ref, n):
+    eye = diagonal()
+    for k in range(n // 128):
+        col = col_ref[pl.ds(k * 128, 128), :]
+        row_ref[k:k + 1, :] = jnp.sum(jnp.where(eye, jnp.broadcast_to(col, (128, 128)), 0.0), axis=0, keepdims=True)
+
+
+def rows_to_column(row, k):
+    return jnp.sum(jnp.where(diagonal(), jnp.broadcast_to(row, (128, 128)), 0.0), axis=1, keepdims=True)
+
+
+def sigmoid(v):
+    return jax.nn.sigmoid(v)
+
+
+def row_at(ref, t):
+    return pl.ds(pl.multiple_of(t, T8), T8)
+
+
+def forward_scan(seqs, length, pi, pf, lower, link, h, cum):
+    C = pi.shape[1]
+    low = lower[...]
+    iota = lax.broadcasted_iota(jnp.int32, (T8, C), 0)
+    ends = []
+    for sq in range(seqs):
+        def tile(i, carry):
+            hl, pr = carry
+            r = row_at(pi, sq * length + i * T8)
+            s = sigmoid(pf[r, :])
+            forget = low + (1.0 - low) * s
+            x = pi[r, :]
+            b = x * sigmoid(x) * (1.0 - forget)
+            a = forget * link[r, :]
+            for sh in (1, 2, 4):
+                keep = iota >= sh
+                b = b + jnp.where(keep, a * pltpu.roll(b, sh, 0), 0.0)
+                a = jnp.where(keep, a * pltpu.roll(a, sh, 0), a)
+            b = b + a * hl
+            a = a * pr
+            h[r, :] = b
+            cum[r, :] = a
+            return b[T8 - 1:T8, :], a[T8 - 1:T8, :]
+
+        ends.append(lax.fori_loop(0, length // T8, tile, (jnp.zeros((1, C), jnp.float32), jnp.ones((1, C), jnp.float32)), unroll=2))
+    return ends
+
+
+def forward_finish(seqs, length, h, cum, start, col):
+    def tile(i, _, sq):
+        r = row_at(h, sq * length + i * T8)
+        v = h[r, :] + cum[r, :] * start[sq:sq + 1, :]
+        h[r, :] = v
+        col[r, :] = jnp.sum(v * v, axis=1, keepdims=True)
+        return 0
+
+    for sq in range(seqs):
+        lax.fori_loop(0, length // T8, functools.partial(tile, sq=sq), 0, unroll=2)
+
+
+def swap_columns(col, row, got, s_sem, r_sem, other, n):
+    column_to_rows(col, row, n)
+    cp = remote(row, got, s_sem, r_sem, {"tp": other})
+    cp.start()
+    cp.wait()
+
+
+def scale_columns(row, got, col, n, width, fn):
+    for k in range(n // 128):
+        col[pl.ds(k * 128, 128), :] = fn(rows_to_column(row[k:k + 1, :] + got[k:k + 1, :], k))
+
+
+def mixed(h, rh, gain, pg, m, step=16):
+    g = gain[...]
+
+    def tile(i, _):
+        r = pl.ds(pl.multiple_of(i * step, step), step)
+        p = pg[r, :]
+        m[r, :] = (h[r, :] * rh[r, :] * g * (p * sigmoid(p))).astype(m.dtype)
+        return 0
+
+    lax.fori_loop(0, h.shape[0] // step, tile, 0)
+
+
+def mixer_forward_body(Z, seqs, length, width, pi, pf, pg, lower, gain, link, ids, h, m, rh, start,
+                       cum, pay, box, row, got, s_c, r_c, s_t, r_t):
+    z, t = lax.axis_index("ctx"), lax.axis_index("tp")
+    n = seqs * length
+    barrier_all(Z, z, t)
+    ends = forward_scan(seqs, length, pi, pf, lower, link, h, cum)
+    pay[4:8, :] = ids[...]
+    for sq in range(seqs):
+        pay[sq:sq + 1, :] = ends[sq][1]
+        pay[2 + sq:3 + sq, :] = ends[sq][0]
+    cps = spread(Z, z, pay, box, s_c, r_c)
+    spread_wait(Z, z, pay, box, s_c, r_c, cps)
+    start[...] = prefix_state(Z, z, box)
+    forward_finish(seqs, length, h, cum, start, rh)
+    swap_columns(rh, row, got, s_t.at[0], r_t.at[0], 1 - t, n)
+    scale_columns(row, got, rh, n, width, lambda v: lax.rsqrt(v / width + epsilon))
+    mixed(h, rh, gain, pg, m)
+
+
+def barrier_all(Z, z, t):
+    barrier = pltpu.get_barrier_semaphore()
+    for o in range(1, Z):
+        pl.semaphore_signal(barrier, inc=1, device_id={"ctx": lax.rem(z + o, Z)}, device_id_type=MESH)
+    pl.semaphore_signal(barrier, inc=1, device_id={"tp": 1 - t}, device_id_type=MESH)
+    pl.semaphore_wait(barrier, Z)
+
+
+def slope(v):
+    s = sigmoid(v)
+    return s * (1.0 + v * (1.0 - s))
+
+
+def backward_first(n, dm, h, pg, gain, rh, dpg, col, gsum, step=16):
+    g = gain[...]
+
+    def tile(i, acc):
+        r = pl.ds(pl.multiple_of(i * step, step), step)
+        d, hv, p, rv = dm[r, :], h[r, :], pg[r, :], rh[r, :]
+        s = sigmoid(p)
+        sl = p * s
+        q = d * g * sl
+        col[r, :] = jnp.sum(q * hv, axis=1, keepdims=True)
+        hr = d * hv * rv
+        dpg[r, :] = (hr * g * (s * (1.0 + p * (1.0 - s)))).astype(dpg.dtype)
+        return acc + jnp.sum(hr * sl, axis=0, keepdims=True)
+
+    gsum[...] = lax.fori_loop(0, n // step, tile, jnp.zeros(gsum.shape, jnp.float32))
+
+
+def backward_scan(seqs, length, dm, h, pf, pg, lower, gain, link, rh, inner, gl, tail):
+    C = dm.shape[1]
+    low, g = lower[...], gain[...]
+    iota = lax.broadcasted_iota(jnp.int32, (T8, C), 0)
+    ends = []
+    nt = length // T8
+    for sq in range(seqs):
+        def tile(k, carry):
+            vl, pr = carry
+            r = row_at(dm, sq * length + (nt - 1 - k) * T8)
+            rv = rh[r, :]
+            p = pg[r, :]
+            q = dm[r, :] * g * (p * sigmoid(p))
+            dh = q * rv - h[r, :] * (rv * rv * rv) * inner[r, :]
+            a = (low + (1.0 - low) * sigmoid(pf[r, :])) * link[r, :]
+            b = a * dh
+            for sh in (1, 2, 4):
+                keep = iota < T8 - sh
+                b = b + jnp.where(keep, a * pltpu.roll(b, T8 - sh, 0), 0.0)
+                a = jnp.where(keep, a * pltpu.roll(a, T8 - sh, 0), a)
+            v = b + a * vl
+            pa = a * pr
+            last = iota == T8 - 1
+            gl[r, :] = dh + jnp.where(last, vl, pltpu.roll(v, T8 - 1, 0))
+            tail[r, :] = jnp.where(last, pr, pltpu.roll(pa, T8 - 1, 0))
+            return v[0:1, :], pa[0:1, :]
+
+        ends.append(lax.fori_loop(0, nt, tile, (jnp.zeros((1, C), jnp.float32), jnp.ones((1, C), jnp.float32)), unroll=2))
+    return ends
+
+
+def backward_last(seqs, length, gl, tail, end, h, start, pi, pf, lower, link, dpi, dpf, lsum):
+    C = gl.shape[1]
+    low = lower[...]
+    iota = lax.broadcasted_iota(jnp.int32, (T8, C), 0)
+    total = jnp.zeros((1, C), jnp.float32)
+    for sq in range(seqs):
+        def tile(i, carry):
+            acc, hp = carry
+            halves = []
+            for half in (0, 1):
+                r = row_at(gl, sq * length + i * 16 + half * T8)
+                gv = gl[r, :] + tail[r, :] * end[sq:sq + 1, :]
+                hv = h[r, :]
+                prev = jnp.where(iota == 0, hp, pltpu.roll(hv, 1, 0) * link[r, :])
+                if half == 1:
+                    prev = jnp.where(iota == 0, prev * link[r, :], prev)
+                else:
+                    prev = jnp.where((iota == 0) & (i > 0), prev * link[r, :], prev)
+                s = sigmoid(pf[r, :])
+                forget = low + (1.0 - low) * s
+                x = pi[r, :]
+                sx = sigmoid(x)
+                df = gv * (prev - x * sx)
+                halves.append((gv * (1.0 - forget) * (sx * (1.0 + x * (1.0 - sx))), df * (1.0 - low) * s * (1.0 - s)))
+                acc = acc + jnp.sum(df * (1.0 - s), axis=0, keepdims=True)
+                hp = hv[T8 - 1:T8, :]
+            r = pl.ds(pl.multiple_of(sq * length + i * 16, 16), 16)
+            dpi[r, :] = jnp.concatenate([halves[0][0], halves[1][0]], axis=0).astype(dpi.dtype)
+            dpf[r, :] = jnp.concatenate([halves[0][1], halves[1][1]], axis=0).astype(dpf.dtype)
+            return acc, hp
+
+        total, _ = lax.fori_loop(0, length // 16, tile, (total, start[sq:sq + 1, :]))
+    lsum[...] = total
+
+
+def mixer_backward_body(Z, seqs, length, width, dm, h, pi, pf, pg, lower, gain, link, ids, rh, start,
+                        dpi, dpf, dpg, gsum, lsum,
+                        gl, tail, col, end, pay, box, row, got, s_c, r_c, s_t, r_t):
+    z, t = lax.axis_index("ctx"), lax.axis_index("tp")
+    n = seqs * length
+    barrier_all(Z, z, t)
+    backward_first(n, dm, h, pg, gain, rh, dpg, col, gsum)
+    swap_columns(col, row, got, s_t.at[0], r_t.at[0], 1 - t, n)
+    scale_columns(row, got, col, n, width, lambda v: v / width)
+    ends = backward_scan(seqs, length, dm, h, pf, pg, lower, gain, link, rh, col, gl, tail)
+    pay[4:8, :] = ids[...]
+    for sq in range(seqs):
+        pay[sq:sq + 1, :] = ends[sq][1]
+        pay[2 + sq:3 + sq, :] = ends[sq][0]
+    cps = spread(Z, z, pay, box, s_c, r_c)
+    spread_wait(Z, z, pay, box, s_c, r_c, cps)
+    end[...] = suffix_state(Z, z, box)
+    backward_last(seqs, length, gl, tail, end, h, start, pi, pf, lower, link, dpi, dpf, lsum)
+
+
+def mixer_scratch(Z, n, C):
+    dma = pltpu.SemaphoreType.DMA
+    f = jnp.float32
+    return [pltpu.VMEM((8, C), f), pltpu.VMEM((Z, 8, C), f), pltpu.VMEM((n // 128, 128), f), pltpu.VMEM((n // 128, 128), f),
+            dma((Z - 1,)), dma((Z,)), dma((1,)), dma((1,))]
+
+
+def mixer_forward(Z, seqs, length, width, pi, pf, pg, lower, gain, link, ids, cid=2):
+    n, C = pi.shape
+    f = jnp.float32
+    sh = jax.ShapeDtypeStruct
+    vm = pl.BlockSpec(memory_space=pltpu.VMEM)
+    return pl.pallas_call(
+        functools.partial(mixer_forward_body, Z, seqs, length, width),
+        out_shape=[sh((n, C), f), sh((n, C), jnp.bfloat16), sh((n, 1), f), sh((seqs, C), f)],
+        in_specs=[vm] * 7, out_specs=[vm] * 4,
+        scratch_shapes=[pltpu.VMEM((n, C), f)] + mixer_scratch(Z, n, C),
+        compiler_params=pltpu.CompilerParams(collective_id=cid, has_side_effects=True),
+        name="mixer_forward",
+    )(pi, pf, pg, lower, gain, link, ids)
+
+
+def mixer_backward(Z, seqs, length, width, dm, h, pi, pf, pg, lower, gain, link, ids, rh, start, cid=3):
+    n, C = pi.shape
+    f, bf = jnp.float32, jnp.bfloat16
+    sh = jax.ShapeDtypeStruct
+    vm = pl.BlockSpec(memory_space=pltpu.VMEM)
+    return pl.pallas_call(
+        functools.partial(mixer_backward_body, Z, seqs, length, width),
+        out_shape=[sh((n, C), bf), sh((n, C), bf), sh((n, C), bf), sh((1, C), f), sh((1, C), f)],
+        in_specs=[vm] * 11, out_specs=[vm] * 5,
+        scratch_shapes=[pltpu.VMEM((n, C), f), pltpu.VMEM((n, C), f), pltpu.VMEM((n, 1), f), pltpu.VMEM((seqs, C), f)] + mixer_scratch(Z, n, C),
+        compiler_params=pltpu.CompilerParams(collective_id=cid, has_side_effects=True),
+        name="mixer_backward",
+    )(dm, h, pi, pf, pg, lower, gain, link, ids, rh, start)
+
+
 def carried_in(x, axis, combine, identity, reverse):
     size, position = (lax.axis_size(axis), lax.axis_index(axis))
     everything = jax.tree.map(lambda part: lax.all_gather(part, axis), x)
@@ -271,12 +941,12 @@
     return (first_part[0] * second_part[0], second_part[0] * first_part[1] + second_part[1])
 
 
-def joined(last_ids, first_ids):
+def joined_ids(last_ids, first_ids):
     return jnp.where((last_ids == first_ids) | (last_ids < 0.0) | (first_ids < 0.0), 1.0, 0.0)
 
 
 def forward_join(first_part, second_part):
-    linked = joined(first_part[3], second_part[2])[:, None]
+    linked = joined_ids(first_part[3], second_part[2])[:, None]
     return (
         first_part[0] * second_part[0] * linked,
         second_part[0] * linked * first_part[1] + second_part[1],
@@ -286,13 +956,77 @@
 
 
 def backward_join(first_part, second_part):
-    linked = joined(second_part[3], first_part[2])[:, None]
+    linked = joined_ids(second_part[3], first_part[2])[:, None]
     return (
         second_part[0] * linked * first_part[0],
         second_part[0] * linked * first_part[1] + second_part[1],
         jnp.where(second_part[2] < 0.0, first_part[2], second_part[2]),
         jnp.where(first_part[3] < 0.0, second_part[3], first_part[3]),
     )
+
+
+def mixer_forward_plain(seqs, length, width, pi, pf, pg, lower, gain, segs):
+    channels = pi.shape[1]
+    forget = lower + (1.0 - lower) * jax.nn.sigmoid(pf)
+    candidate = jax.nn.silu(pi) * (1.0 - forget)
+    inner_link = jnp.concatenate(
+        [jnp.ones((seqs, 1), jnp.float32), jnp.where(segs[:, 1:] == segs[:, :-1], 1.0, 0.0)], axis=1
+    )
+    decay = forget.reshape(seqs, length, channels) * inner_link[:, :, None]
+    prod, local = lax.associative_scan(
+        linear_step, (decay, candidate.reshape(seqs, length, channels)), axis=1
+    )
+    first, last = segs[:, 0], segs[:, -1]
+    ones, zero = jnp.ones((seqs, channels), jnp.float32), jnp.zeros((seqs, channels), jnp.float32)
+    minus = -jnp.ones((seqs,), jnp.float32)
+    prefix = carried_in(
+        (prod[:, -1], local[:, -1], first, last), "ctx", forward_join, (ones, zero, minus, minus), False
+    )
+    start = joined_ids(prefix[3], first)[:, None] * prefix[1]
+    h = (local + prod * start[:, None, :]).reshape(seqs * length, channels)
+    squares = lax.psum(jnp.sum(h * h, axis=1), "tp")
+    rh = lax.rsqrt(squares / width + epsilon)[:, None]
+    m = (h * rh * gain * jax.nn.silu(pg)).astype(jnp.bfloat16)
+    return h, m, rh, start
+
+
+def mixer_backward_plain(seqs, length, width, dm, h, pi, pf, pg, lower, gain, segs, rh, start):
+    channels = pi.shape[1]
+    s = jax.nn.sigmoid(pf)
+    forget = lower + (1.0 - lower) * s
+    inner_link = jnp.concatenate(
+        [jnp.ones((seqs, 1), jnp.float32), jnp.where(segs[:, 1:] == segs[:, :-1], 1.0, 0.0)], axis=1
+    )
+    forget_seq = forget.reshape(seqs, length, channels)
+    decay = forget_seq * inner_link[:, :, None]
+    silu_gate = jax.nn.silu(pg)
+    weighted = dm * gain * silu_gate
+    inner = lax.psum(jnp.sum(weighted * h, axis=1), "tp")
+    dh = weighted * rh - h * (rh * rh * rh) * (inner / width)[:, None]
+    gain_grad = jnp.sum(dm * h * rh * silu_gate, axis=0)
+    dpg = (dm * h * rh * gain * silu_slope(pg)).astype(jnp.bfloat16)
+    ones_row = jnp.ones((seqs, 1, channels), jnp.float32)
+    following = jnp.concatenate([decay[:, 1:], ones_row], axis=1)
+    tail, local = lax.associative_scan(
+        linear_step, (following, dh.reshape(seqs, length, channels)), reverse=True, axis=1
+    )
+    first, last = segs[:, 0], segs[:, -1]
+    ones, zero = jnp.ones((seqs, channels), jnp.float32), jnp.zeros((seqs, channels), jnp.float32)
+    minus = -jnp.ones((seqs,), jnp.float32)
+    suffix = carried_in(
+        (decay[:, 0] * tail[:, 0], forget_seq[:, 0] * local[:, 0], first, last),
+        "ctx", backward_join, (ones, zero, minus, minus), True,
+    )
+    end = joined_ids(last, suffix[2])[:, None] * suffix[1]
+    g = (local + tail * end[:, None, :]).reshape(seqs * length, channels)
+    states = h.reshape(seqs, length, channels)
+    previous = jnp.concatenate(
+        [start[:, None, :], inner_link[:, 1:, None] * states[:, :-1]], axis=1
+    ).reshape(seqs * length, channels)
+    dforget = g * (previous - jax.nn.silu(pi))
+    dpi = (g * (1.0 - forget) * silu_slope(pi)).astype(jnp.bfloat16)
+    dpf = (dforget * (1.0 - lower) * s * (1.0 - s)).astype(jnp.bfloat16)
+    return dpi, dpf, dpg, gain_grad, jnp.sum(dforget * (1.0 - s), axis=0)
 
 
 def on_device(
@@ -311,169 +1045,114 @@
     w_down,
     cotangent,
 ):
-    bfloat = jnp.bfloat16
-    seq_count, span_len, model_width = block_input.shape
-    rows_all = seq_count * span_len
+    bfloat, f32 = jnp.bfloat16, jnp.float32
+    seqs, length, width = block_input.shape
+    rows_all = seqs * length
+    small = lax.axis_size("shard") == 4
+    Z = lax.axis_size("ctx")
     shards = [
         w.astype(bfloat) for w in (w_input, w_forget, w_gate, w_out, w_mlp_gate, w_mlp_up, w_down)
     ]
-    if lax.axis_size("shard") == 4:
-        wide = gather_all(shards, 4, lax.axis_size("ctx"))
+    if small:
+        wide = gather_all(shards, 4, Z)
     else:
         wide = [lax.all_gather(w, ("shard", "ctx"), axis=0, tiled=True) for w in shards]
     wide_input, wide_forget, wide_gate, wide_out, wide_mgate, wide_mup, wide_down = wide
-    residual_in = block_input.reshape(rows_all, model_width)
+    segs = segment_ids.astype(f32)
+    link = jnp.concatenate(
+        [jnp.ones((seqs, 1), f32), jnp.where(segs[:, 1:] == segs[:, :-1], 1.0, 0.0)], axis=1
+    ).reshape(rows_all, 1)
+    residual_in = block_input.reshape(rows_all, width)
     scale_one = inverse_rms(residual_in)
     normed_one = (residual_in * scale_one * norm_gain).astype(bfloat)
-    proj_input = jnp.dot(normed_one, wide_input, preferred_element_type=jnp.float32)
-    proj_forget = jnp.dot(normed_one, wide_forget, preferred_element_type=jnp.float32)
-    proj_gate = jnp.dot(normed_one, wide_gate, preferred_element_type=jnp.float32)
-    channels = proj_input.shape[1]
-    sigmoid_f = jax.nn.sigmoid(proj_forget)
-    forget = lower + (1.0 - lower) * sigmoid_f
-    silu_in = jax.nn.silu(proj_input)
-    candidate = silu_in * (1.0 - forget)
-    seg_float = segment_ids.astype(jnp.float32)
-    inner_link = jnp.concatenate(
-        [
-            jnp.ones((seq_count, 1), jnp.float32),
-            jnp.where(seg_float[:, 1:] == seg_float[:, :-1], 1.0, 0.0),
-        ],
-        axis=1,
-    )
-    forget_seq = forget.reshape(seq_count, span_len, channels)
-    decay_rate = forget_seq * inner_link[:, :, None]
-    decay_prod, local_state = lax.associative_scan(
-        linear_step, (decay_rate, candidate.reshape(seq_count, span_len, channels)), axis=1
-    )
-    first_ids = seg_float[:, 0]
-    last_ids = seg_float[:, -1]
-    ones_state = jnp.ones((seq_count, channels), jnp.float32)
-    zero_state = jnp.zeros((seq_count, channels), jnp.float32)
-    minus_ids = -jnp.ones((seq_count,), jnp.float32)
-    prefix = carried_in(
-        (decay_prod[:, -1], local_state[:, -1], first_ids, last_ids),
-        "ctx",
-        forward_join,
-        (ones_state, zero_state, minus_ids, minus_ids),
-        False,
-    )
-    start_state = joined(prefix[3], first_ids)[:, None] * prefix[1]
-    state_seq = local_state + decay_prod * start_state[:, None, :]
-    hidden_state = state_seq.reshape(rows_all, channels)
-    squares = lax.psum(jnp.sum(hidden_state * hidden_state, axis=1), "tp")
-    scale_mid = lax.rsqrt(squares / model_width + epsilon)[:, None]
-    silu_gate = jax.nn.silu(proj_gate)
-    mixed_in = (hidden_state * scale_mid * hidden_gain * silu_gate).astype(bfloat)
-    mixer_out = lax.psum(times_back(mixed_in, wide_out).astype(jnp.bfloat16), "tp").astype(
-        jnp.float32
-    )
+    pi = jnp.dot(normed_one, wide_input, preferred_element_type=f32)
+    pf = jnp.dot(normed_one, wide_forget, preferred_element_type=f32)
+    pg = jnp.dot(normed_one, wide_gate, preferred_element_type=f32)
+    channels = pi.shape[1]
+    ids = jnp.broadcast_to(
+        jnp.concatenate([segs[:, 0], segs[:, -1]])[:, None], (2 * seqs, channels)
+    )
+    low_row, gain_row = lower[None, :], hidden_gain[None, :]
+    if small:
+        h, mixed_in, rh, start = mixer_forward(
+            Z, seqs, length, width, pi, pf, pg, low_row, gain_row, link, ids
+        )
+    else:
+        h, mixed_in, rh, start = mixer_forward_plain(
+            seqs, length, width, pi, pf, pg, lower, hidden_gain, segs
+        )
+    mixer_out = lax.psum(times_back(mixed_in, wide_out).astype(bfloat), "tp").astype(f32)
     middle = residual_in + mixer_out
     scale_two = inverse_rms(middle)
     normed_two = (middle * scale_two * mlp_gain).astype(bfloat)
-    gate_pre = jnp.dot(normed_two, wide_mgate, preferred_element_type=jnp.float32)
-    up_pre = jnp.dot(normed_two, wide_mup, preferred_element_type=jnp.float32)
+    gate_pre = jnp.dot(normed_two, wide_mgate, preferred_element_type=f32)
+    up_pre = jnp.dot(normed_two, wide_mup, preferred_element_type=f32)
     silu_mlp = jax.nn.silu(gate_pre)
     activated = (silu_mlp * up_pre).astype(bfloat)
-    mlp_out = lax.psum(times_back(activated, wide_down).astype(jnp.bfloat16), "tp").astype(
-        jnp.float32
-    )
+    mlp_out = lax.psum(times_back(activated, wide_down).astype(bfloat), "tp").astype(f32)
     output = middle + mlp_out
-    upstream = cotangent.reshape(rows_all, model_width)
+    upstream = cotangent.reshape(rows_all, width)
     upstream_low = upstream.astype(bfloat)
-    grad_activ = jnp.dot(upstream_low, wide_down, preferred_element_type=jnp.float32)
-    grad_down = outer_sum(upstream_low, activated)
+    grad_activ = jnp.dot(upstream_low, wide_down, preferred_element_type=f32)
+    grad_down = outer_sum(upstream_low, activated).astype(bfloat)
     grad_gate_pre = (grad_activ * up_pre * silu_slope(gate_pre)).astype(bfloat)
     grad_up_pre = (grad_activ * silu_mlp).astype(bfloat)
-    grad_mgate = outer_sum(normed_two, grad_gate_pre)
-    grad_mup = outer_sum(normed_two, grad_up_pre)
+    grad_mgate = outer_sum(normed_two, grad_gate_pre).astype(bfloat)
+    grad_mup = outer_sum(normed_two, grad_up_pre).astype(bfloat)
     grad_normed_two = lax.psum(
-        (times_back(grad_gate_pre, wide_mgate) + times_back(grad_up_pre, wide_mup)).astype(
-            jnp.bfloat16
-        ),
+        (times_back(grad_gate_pre, wide_mgate) + times_back(grad_up_pre, wide_mup)).astype(bfloat),
         "tp",
-    ).astype(jnp.float32)
+    ).astype(f32)
     grad_mlp_gain = jnp.sum(grad_normed_two * middle * scale_two, axis=0)
     grad_middle = upstream + rms_backward(middle, scale_two, mlp_gain, grad_normed_two)
     middle_low = grad_middle.astype(bfloat)
-    grad_mixed_in = jnp.dot(middle_low, wide_out, preferred_element_type=jnp.float32)
-    grad_out = outer_sum(middle_low, mixed_in)
-    weighted = grad_mixed_in * hidden_gain * silu_gate
-    inner_sum = lax.psum(jnp.sum(weighted * hidden_state, axis=1), "tp")
-    grad_state = (
-        weighted * scale_mid
-        - hidden_state * (scale_mid * scale_mid * scale_mid) * (inner_sum / model_width)[:, None]
-    )
-    grad_hidden_gain = jnp.sum(grad_mixed_in * hidden_state * scale_mid * silu_gate, axis=0)
-    grad_gate_proj = (
-        grad_mixed_in * hidden_state * scale_mid * hidden_gain * silu_slope(proj_gate)
-    ).astype(bfloat)
-    next_decay = jnp.concatenate(
-        [decay_rate[:, 1:], jnp.ones((seq_count, 1, channels), jnp.float32)], axis=1
-    )
-    tail_prod, local_grad = lax.associative_scan(
-        linear_step,
-        (next_decay, grad_state.reshape(seq_count, span_len, channels)),
-        reverse=True,
-        axis=1,
-    )
-    suffix = carried_in(
-        (decay_prod[:, -1], forget_seq[:, 0] * local_grad[:, 0], first_ids, last_ids),
-        "ctx",
-        backward_join,
-        (ones_state, zero_state, minus_ids, minus_ids),
-        True,
-    )
-    end_grad = joined(last_ids, suffix[2])[:, None] * suffix[1]
-    total_grad = (local_grad + tail_prod * end_grad[:, None, :]).reshape(rows_all, channels)
-    previous = jnp.concatenate(
-        [start_state[:, None, :], inner_link[:, 1:, None] * state_seq[:, :-1]], axis=1
-    ).reshape(rows_all, channels)
-    grad_forget = total_grad * (previous - silu_in)
-    grad_input_proj = (total_grad * (1.0 - forget) * silu_slope(proj_input)).astype(bfloat)
-    grad_forget_proj = (grad_forget * (1.0 - lower) * sigmoid_f * (1.0 - sigmoid_f)).astype(bfloat)
-    grad_lower = jnp.sum(grad_forget * (1.0 - sigmoid_f), axis=0)
-    grad_w_input = outer_sum(normed_one, grad_input_proj)
-    grad_w_forget = outer_sum(normed_one, grad_forget_proj)
-    grad_w_gate = outer_sum(normed_one, grad_gate_proj)
+    dm = jnp.dot(middle_low, wide_out, preferred_element_type=f32)
+    grad_out = outer_sum(middle_low, mixed_in).astype(bfloat)
+    if small:
+        dpi, dpf, dpg, grad_hidden_gain, grad_lower = mixer_backward(
+            Z, seqs, length, width, dm, h, pi, pf, pg, low_row, gain_row, link, ids, rh, start
+        )
+        grad_hidden_gain, grad_lower = grad_hidden_gain[0], grad_lower[0]
+    else:
+        dpi, dpf, dpg, grad_hidden_gain, grad_lower = mixer_backward_plain(
+            seqs, length, width, dm, h, pi, pf, pg, lower, hidden_gain, segs, rh, start
+        )
+    grad_w_input = outer_sum(normed_one, dpi).astype(bfloat)
+    grad_w_forget = outer_sum(normed_one, dpf).astype(bfloat)
+    grad_w_gate = outer_sum(normed_one, dpg).astype(bfloat)
     grad_normed_one = lax.psum(
         (
-            times_back(grad_input_proj, wide_input)
-            + times_back(grad_forget_proj, wide_forget)
-            + times_back(grad_gate_proj, wide_gate)
-        ).astype(jnp.bfloat16),
+            times_back(dpi, wide_input) + times_back(dpf, wide_forget) + times_back(dpg, wide_gate)
+        ).astype(bfloat),
         "tp",
-    ).astype(jnp.float32)
+    ).astype(f32)
     grad_norm_gain = jnp.sum(grad_normed_one * residual_in * scale_one, axis=0)
     grad_resid = grad_middle + rms_backward(residual_in, scale_one, norm_gain, grad_normed_one)
-    mlp_grads = (
-        lax.psum_scatter(grad_mgate.astype(bfloat), ("shard", "ctx"), scatter_dimension=0, tiled=True).astype(jnp.float32),
-        lax.psum_scatter(grad_mup.astype(bfloat), ("shard", "ctx"), scatter_dimension=0, tiled=True).astype(jnp.float32),
-        lax.psum_scatter(grad_down.astype(bfloat), ("shard", "ctx"), scatter_dimension=0, tiled=True).astype(jnp.float32),
-    )
-    mixer_grads = (
-        lax.psum_scatter(grad_w_input.astype(bfloat), ("shard", "ctx"), scatter_dimension=0, tiled=True).astype(jnp.float32),
-        lax.psum_scatter(grad_w_forget.astype(bfloat), ("shard", "ctx"), scatter_dimension=0, tiled=True).astype(jnp.float32),
-        lax.psum_scatter(grad_w_gate.astype(bfloat), ("shard", "ctx"), scatter_dimension=0, tiled=True).astype(jnp.float32),
-        lax.psum_scatter(grad_out.astype(bfloat), ("shard", "ctx"), scatter_dimension=0, tiled=True).astype(jnp.float32),
-    )
-    gain_grads = lax.psum(
-        (grad_norm_gain, grad_lower, grad_hidden_gain, grad_mlp_gain), ("shard", "ctx")
-    )
+    parts = (grad_down, grad_mgate, grad_mup, grad_out, grad_w_input, grad_w_forget, grad_w_gate)
+    vectors = jnp.concatenate([grad_norm_gain, grad_mlp_gain, grad_lower, grad_hidden_gain])
+    if small:
+        vectors, sums = scatter_all(parts, vectors.reshape(-1, 128), Z)
+        vectors = vectors.reshape(-1)
+    else:
+        vectors = lax.psum(vectors, ("shard", "ctx"))
+        sums = [
+            lax.psum_scatter(p, ("shard", "ctx"), scatter_dimension=0, tiled=True).astype(f32)
+            for p in parts
+        ]
     return (
         output.reshape(block_input.shape),
         grad_resid.reshape(block_input.shape),
-        gain_grads[0],
-        gain_grads[1],
-        mixer_grads[0],
-        mixer_grads[1],
-        mixer_grads[2],
-        gain_grads[2],
-        mixer_grads[3],
-        gain_grads[3],
-        mlp_grads[0],
-        mlp_grads[1],
-        mlp_grads[2],
+        vectors[:width],
+        vectors[2 * width : 2 * width + channels],
+        sums[4],
+        sums[5],
+        sums[6],
+        vectors[2 * width + channels :],
+        sums[3],
+        vectors[width : 2 * width],
+        sums[1],
+        sums[2],
+        sums[0],
     )
 
 

time: 1790 us -> 1090 us (0.61)
  waiting for transfers between devices: 714 us -> 171 us
  Pallas kernels: 271 us -> 691 us
  local copies, waits for them, and re-layouts: 333 us -> 13.6 us
  blocking collectives: 123 us -> 0 us
  other arithmetic: 157 us -> 41.2 us
    reduce_scatter x6 -> x0, waiting for transfers between devices: 477 us -> none  [the longest x1 128 us: on_device(): lax.psum_scatter(grad_mup.astype(bfloat), ('shard', 'ctx'), scatter_dimen...]
    pallas_call x0 -> x3, Pallas kernels: none -> 419 us  [the longest x1 368 us: scatter_all(): pl.pallas_call(functools.partial(scatter_body, nw, Z), out_shape=out_shap...]
    slice x111 -> x3, local copies, waits for them, and re-layouts: 209 us -> 2.77 us  [the longest x1 1.32 us: on_device(): vectors[width:2 * width]]
    unnamed x11 -> x3, waiting for transfers between devices: 129 us -> 0.05 us
    psum x3 -> x0, blocking collectives: 72.2 us -> none  [the longest x1 62.4 us: on_device(): lax.psum((grad_norm_gain, grad_lower, grad_hidden_gain, grad_mlp_gain), (...]
    add x47 -> x0, other arithmetic: 54.2 us -> none  [the longest x14 21.7 us: linear_step(): second_part[0] * first_part[1] + second_part[1]]
    pad x56 -> x0, local copies, waits for them, and re-layouts: 51.4 us -> none  [the longest x28 34 us: on_device(): lax.associative_scan(linear_step, (decay_rate, candidate.reshape(seq_coun...]
    psum x2, waiting for transfers between devices: 87.6 us -> 130 us  [the longest x1 71 us: on_device(): lax.psum(times_back(activated, wide_down).astype(bfloat), 'tp').astype(f32)]
  transfers between devices with their start and end apart: 10 -> 3, of which waited for: 10 -> 3; matrix products, arithmetic and copies ran while one was open for 8% -> 6% of each run, Pallas kernels for 0% -> 0%
where the time goes in v2:
time: 1090 us; the launch traced here: 1080 us
  Pallas kernels  691 us (63%)
  waiting for transfers between devices  171 us (16%)
  matrix products  147 us (13%)
  other arithmetic  41.2 us (4%)
  between operations  14.7 us (1%)
  local copies, waits for them, and re-layouts  13.6 us (1%)
    pallas_call x1, Pallas kernels, scatter_all(): pl.pallas_call(functools.partial(scatter_body, nw, Z), out_shape=out_shap...  368 us
    pallas_call x1, Pallas kernels, gather_all(): pl.pallas_call(functools.partial(gather_body, nw, Z, ahead, relay), out_s...  271 us
    psum x1, waiting for transfers between devices, on_device(): lax.psum(times_back(activated, wide_down).astype(bfloat), 'tp').astype(f32)  71 us
    psum x1, waiting for transfers between devices, on_device(): lax.psum(times_back(mixed_in, wide_out).astype(bfloat), 'tp').astype(f32)  59 us
    dot_general x7, matrix products, outer_sum(): lax.dot_general(left_mat, right_mat, (((0,), (0,)), ((), ())), preferred_...  49.2 us
    dot_general x7, matrix products, times_back(): lax.dot_general(left_mat, right_mat, (((1,), (1,)), ((), ())), preferred_...  47.3 us
    psum x1, waiting for transfers between devices, on_device(): lax.psum((times_back(grad_gate_pre, wide_mgate) + times_back(grad_up_pre,...  41.4 us
    pallas_call x1, Pallas kernels, mixer_backward(): pl.pallas_call(functools.partial(mixer_backward_body, Z, seqs, length, wi...  27.3 us
  transfers between devices with their start and end apart: 3, of which 3 were waited for; matrix products, arithmetic and copies ran while one was open for 6% of the time, Pallas kernels for 0%

profile of v2, /device:TPU:0, one launch (start us, length us, event | category | flops | bytes accessed | tf_op | source)
XLA Modules:
  0.0 1078.5 jit_solution(10130710307886357704)
XLA Ops:
  8.4 2.7 multiply_reduce_fusion.1
  11.1 0.9 copy.37
  12.7 1.8 convert_element_type.94.refs_1_
  14.5 1.9 convert_element_type.95.refs_2_
  16.4 1.8 convert_element_type.96.refs_3_
  18.2 0.9 convert_element_type.97.refs_4_
  19.1 0.9 convert_element_type.98.refs_5_
  20.1 0.9 convert_element_type.99.refs_6_
  21.4 271.3 %weights_in.1 = (bf16[2048,1024]{1,0:T(8,128)(2,1)}, bf16[2048,1024]{1,0:T(8,128)(2,1)}, bf16[2048,1024]{1,0:T(8,128)(2,1)}, bf16[2048,1024]{1,0:T(8,128)(2,1)},...) custom-call(bf16[128,1024]{1,0:T(8,128)(2,1)} %convert_element_type.93.refs_0_, ...), custom_call_target="tpu_custom_call" | custom-call | tf_op jit(solution)/shard_map/weights_in/pallas_call | solution.py:212
  292.7 6.0 fusion.24.pi
  298.7 3.7 fusion.25.pf
  302.4 3.7 fusion.26.pg
  306.9 24.2 %mixer_forward.1 = (f32[512,1024]{1,0:T(8,128)}, bf16[512,1024]{1,0:T(8,128)(2,1)}, f32[512,1]{1,0:T(8,128)}, f32[2,1024]{1,0:T(2,128)}) custom-call(f32[512,1024]{1,0:T(8,128)} %fusion.24.pi, f32[512,1024]{1,0:T(8,128)} %fusion.25.pf, f32[512,1024]{1,0:T(8,128)} %fusion.26.pg, f32[1,1024]{1,0:T(1,128)} %bitcast.101, f32[1,1024]{1,0:T(1,128)} %bitcast.103, ...), custom_call_target="tpu_custom_call" | custom-call | tf_op jit(solution)/shard_map/mixer_forward/pallas_call | solution.py:872
  331.1 6.2 convolution_convert_fusion.6
  338.0 2.5 bitcast_convert_fusion
  340.5 59.0 %all-reduce.6.cloned.1.call-done = bf16[512,2048]{1,0:T(8,128)(2,1)} async-done(((bf16[512,2048]{1,0:T(8,128)(2,1)}), bf16[512,2048]{1,0:T(8,128)(2,1)}) %all-reduce.6.cloned.1.call-update) | async-done | bytes 2097168 | tf_op jit(solution)/shard_map/psum | solution.py:1084
  399.5 3.4 multiply_reduce_fusion
  403.0 2.0 copy-done.1
  405.4 12.4 %fusion.28 = f32[512,2816]{1,0:T(8,128)} fusion(bf16[512,2048]{1,0:T(8,128)(2,1)S(1)} %multiply_convert_fusion.1, bf16[2048,2816]{1,0:T(8,128)(2,1)} %get-tuple-element.43), kind=kOutput, calls=%fused_computation.71 | convolution fusion | flops 5905580032 | bytes 19398656 | tf_op jit(solution)/shard_map/dot_general | solution.py:1089
  417.9 7.9 fusion.27
  425.8 12.6 %fusion.2 = (bf16[512,2816]{1,0:T(8,128)(2,1)}, bf16[512,2816]{1,0:T(8,128)(2,1)}, bf16[512,2816]{1,0:T(8,128)(2,1)}) fusion(f32[512,2816]{1,0:T(8,128)} %fusion.27, f32[512,2816]{1,0:T(8,128)} %fusion.28, bf16[512,2048]{1,0:T(8,128)(2,1)S(1)} %bitcast_convert_fusion, bf16[2048,2816]{1,0:T(8,128)(2,1)S(1)} %bitcast.109), kind=kOutput, calls=%fused_computation.7 | convolution fusion | flops 5927206912 | bytes 33816576 | tf_op jit(solution)/shard_map/dot_general | solution.py:1096
  438.4 10.0 fusion.29
  448.4 10.0 add_convert_fusion.1
  458.5 11.7 %convolution_convert_fusion.refs_2_ = bf16[2048,2816]{1,0:T(8,128)(2,1)} fusion(bf16[512,2048]{1,0:T(8,128)(2,1)} %copy-done.9, bf16[512,2816]{1,0:T(8,128)(2,1)} %get-tuple-element.71), kind=kOutput, calls=%fused_computation.1 | convolution fusion | flops 5911347200 | bytes 16515072 | tf_op jit(solution)/shard_map/dot_general | solution.py:935
  470.2 10.0 convolution_convert_fusion.7
  480.2 41.4 %all-reduce.8.cloned.1.call-done = bf16[512,2048]{1,0:T(8,128)(2,1)} async-done(((bf16[512,2048]{1,0:T(8,128)(2,1)}), bf16[512,2048]{1,0:T(8,128)(2,1)}) %all-reduce.8.cloned.1.call-update) | async-done | bytes 2097168 | tf_op jit(solution)/shard_map/psum | solution.py:1102
  521.6 4.3 fusion.15
  526.3 3.4 fusion.12
  529.8 3.8 fusion.22.dm
  533.5 27.3 %mixer_backward.1 = (bf16[512,1024]{1,0:T(8,128)(2,1)}, bf16[512,1024]{1,0:T(8,128)(2,1)}, bf16[512,1024]{1,0:T(8,128)(2,1)}, f32[1,1024]{1,0:T(1,128)}, f32[1,1024]{1,0:T(1,128)}) custom-call(f32[512,1024]{1,0:T(8,128)} %fusion.22.dm, f32[512,1024]{1,0:T(8,128)} %get-tuple-element.45.h, f32[512,1024]{1,0:T(8,128)} %fusion.24.pi, f32[512,1024]{1,0:T(8,128)} %fusion.25.pf, ...), custom_call_target="tpu_custom_call" | custom-call | tf_op jit(solution)/shard_map/mixer_backward/pallas_call | solution.py:887
  560.9 5.0 fusion.30
  565.9 2.4 fusion.31
  568.4 3.7 add_convert_fusion
  572.1 10.9 %convert_bitcast_fusion.refs_0_ = bf16[2048,2816]{1,0:T(8,128)(2,1)} fusion(bf16[512,2816]{1,0:T(8,128)(2,1)} %get-tuple-element.73, bf16[512,2048]{1,0:T(8,128)(2,1)S(1)} %bitcast_convert_fusion), kind=kOutput, calls=%fused_computation | convolution fusion | flops 5911347200 | bytes 16515072 | tf_op jit(solution)/shard_map/dot_general | solution.py:935
  583.1 9.1 convolution_convert_fusion.1.refs_1_
  592.2 4.3 convolution_convert_fusion.4.refs_4_
  596.5 4.4 convolution_convert_fusion.3.refs_5_
  600.9 4.5 convolution_convert_fusion.2.refs_6_
  605.4 4.4 convolution_convert_fusion.5.refs_3_
  609.8 71.0 %all-reduce.10.cloned.1.call-done = (bf16[512,2048]{1,0:T(8,128)(2,1)}, bf16[512,2048]{1,0:T(8,128)(2,1)}) async-done(((bf16[512,2048]{1,0:T(8,128)(2,1)}, bf16[512,2048]{1,0:T(8,128)(2,1)}), (bf16[512,2048]{1,0:T(8,128)(2,1)}, bf16[512,2048]{1,0:T(8,128)(2,1)})) %all-reduce.10.cloned.1.call-update) | async-done | bytes 4194320 | tf_op jit(solution)/shard_map/psum | solution.py:1092
  680.9 4.1 fusion.17
  685.6 368.0 %grads_out.1 = (f32[48,128]{1,0:T(8,128)}, f32[128,2816]{1,0:T(8,128)}, f32[128,2816]{1,0:T(8,128)}, f32[128,2816]{1,0:T(8,128)}, f32[128,1024]{1,0:T(8,128)}, /...) custom-call(bf16[2048,2816]{1,0:T(8,128)(2,1)} %convert_bitcast_fusi, ...), custom_call_target="tpu_custom_call" | custom-call | tf_op jit(solution)/shard_map/grads_out/pallas_call | solution.py:574
  1053.6 1.3 slice_bitcast_fusion.2
  1054.9 1.3 slice_bitcast_fusion
  1056.2 8.8 fusion.9
  1068.2 1.1 copy.53
  1069.3 1.1 copy.54
  1070.4 1.1 copy.55
  (126 shorter events, 8.8 us)
Async XLA Ops:
  7.2 4.8 copy-start.17
  7.2 11.0 %copy-start.11 = (f32[128,2816]{1,0:T(8,128)S(1)}, f32[128,2816]{1,0:T(8,128)}, u32[]{:S(2)}) copy-start(f32[128,2816]{1,0:T(8,128)} %param.24) | copy-start | bytes 4325380
  7.2 392.3 %all-reduce.6.cloned.1.call-start = ((), (), s32[]{:S(2)}) async-start(), calls=%async_computation | async-start | bytes 4194304 | tf_op jit(solution)/shard_map/psum | solution.py:1084
  8.4 10.7 copy-start.12
  11.1 326.3 %copy-start.25 = (f32[1,2,2,128]{3,1,2,0:T(2,128)}, f32[1,2,2,128]{3,1,2,0:T(2,128)S(1)}, u32[]{:S(2)}) copy-start(f32[1,2,2,128]{3,1,2,0:T(2,128)S(1)} %copy.35) | copy-start | bytes 6148
  11.9 8.1 copy-start.13
  14.5 6.5 copy-start
  14.5 6.5 copy-start.22
  21.4 281.0 %copy-start.7 = (bf16[512,2048]{1,0:T(8,128)(2,1)}, bf16[512,2048]{1,0:T(8,128)(2,1)S(1)}, u32[]{:S(2)}) copy-start(bf16[512,2048]{1,0:T(8,128)(2,1)S(1)} %fusion.19) | copy-start | bytes 6291460
  292.7 6.0 copy-start.32
  298.7 3.7 copy-start.30
  337.3 184.2 %all-reduce.8.cloned.1.call-start = ((), (), s32[]{:S(2)}) async-start(), calls=%async_computation.1 | async-start | bytes 4194304 | tf_op jit(solution)/shard_map/psum | solution.py:1102
  340.5 64.5 %copy-start.24 = (f32[2048]{0:T(1024)S(1)}, f32[2048]{0:T(1024)}, u32[]{:S(2)}) copy-start(f32[2048]{0:T(1024)} %param.23) | copy-start | bytes 24580
  404.9 12.9 %slice-start.3 = ((s8[11534336]{0:T(1024)(128)(4,1)}), s8[4194304]{0:T(1024)(128)(4,1)S(1)}, s32[]{:S(2)}) async-start(s8[11534336]{0:T(1024)(128)(4,1)} %bitcast.110), calls=%async_computation.6 | async-start | bytes 8388608
  405.4 12.5 %copy-start.9 = (bf16[512,2048]{1,0:T(8,128)(2,1)}, bf16[512,2048]{1,0:T(8,128)(2,1)S(1)}, u32[]{:S(2)}) copy-start(bf16[512,2048]{1,0:T(8,128)(2,1)S(1)} %multiply_convert_fusion.1) | copy-start | bytes 6291460
  405.4 12.5 %slice-start.4 = ((s8[11534336]{0:T(1024)(128)(4,1)}), s8[4194304]{0:T(1024)(128)(4,1)S(1)}, s32[]{:S(2)}) async-start(s8[11534336]{0:T(1024)(128)(4,1)} %bitcast.110), calls=%async_computation.7 | async-start | bytes 8388608
  405.4 12.4 %slice-start.5 = ((s8[11534336]{0:T(1024)(128)(4,1)}), s8[3145728]{0:T(1024)(128)(4,1)S(1)}, s32[]{:S(2)}) async-start(s8[11534336]{0:T(1024)(128)(4,1)} %bitcast.110), calls=%async_computation.8 | async-start | bytes 6291456
  405.4 20.4 %slice-start = ((s8[11534336]{0:T(1024)(128)(4,1)}), s8[4194304]{0:T(1024)(128)(4,1)S(1)}, s32[]{:S(2)}) async-start(s8[11534336]{0:T(1024)(128)(4,1)} %bitcast.108), calls=%async_computation.3 | async-start | bytes 8388608
  405.4 20.4 %slice-start.1 = ((s8[11534336]{0:T(1024)(128)(4,1)}), s8[4194304]{0:T(1024)(128)(4,1)S(1)}, s32[]{:S(2)}) async-start(s8[11534336]{0:T(1024)(128)(4,1)} %bitcast.108), calls=%async_computation.4 | async-start | bytes 8388608
  417.9 7.9 slice-start.2
  438.4 10.0 copy-start.41
  458.4 222.4 %all-reduce.10.cloned.1.call-start = ((), (), s32[]{:S(2)}) async-start(), calls=%async_computation.2 | async-start | bytes 8388608 | tf_op jit(solution)/shard_map/psum | solution.py:1092
  458.5 11.7 %copy-start.42 = (bf16[512,2816]{1,0:T(8,128)(2,1)S(1)}, bf16[512,2816]{1,0:T(8,128)(2,1)}, u32[]{:S(2)}) copy-start(bf16[512,2816]{1,0:T(8,128)(2,1)} %get-tuple-element.73) | copy-start | bytes 8650756
  521.6 4.3 copy-start.2
  521.6 4.7 copy-start.6
  526.3 3.4 copy-start.34
  529.8 3.8 copy-start.3
  560.8 5.1 copy-start.33
  560.8 5.1 copy-start.37
  572.1 10.9 %copy-start.10 = (bf16[512,2048]{1,0:T(8,128)(2,1)S(1)}, bf16[512,2048]{1,0:T(8,128)(2,1)}, u32[]{:S(2)}) copy-start(bf16[512,2048]{1,0:T(8,128)(2,1)} %copy-done.9) | copy-start | bytes 6291460
  572.1 10.9 %copy-start.40 = (bf16[512,2816]{1,0:T(8,128)(2,1)S(1)}, bf16[512,2816]{1,0:T(8,128)(2,1)}, u32[]{:S(2)}) copy-start(bf16[512,2816]{1,0:T(8,128)(2,1)} %get-tuple-element.72) | copy-start | bytes 8650756
  583.1 9.1 copy-start.8
  583.1 9.1 copy-start.39
  592.2 4.4 copy-start.38
  600.9 4.5 copy-start.4
  600.9 4.5 copy-start.35
  605.4 75.4 %copy-start.23 = (f32[2048]{0:T(1024)S(1)}, f32[2048]{0:T(1024)}, u32[]{:S(2)}) copy-start(f32[2048]{0:T(1024)} %param.16) | copy-start | bytes 24580
  605.4 75.4 %copy-start.26 = (f32[1,2,2,128]{3,1,2,0:T(2,128)S(1)}, f32[1,2,2,128]{3,1,2,0:T(2,128)}, u32[]{:S(2)}) copy-start(f32[1,2,2,128]{3,1,2,0:T(2,128)} %copy-done.25) | copy-start | bytes 6148
  609.8 75.2 %copy-start.28 = (f32[1,1024]{1,0:T(1,128)S(1)}, f32[1,1024]{1,0:T(1,128)}, u32[]{:S(2)}) copy-start(f32[1,1024]{1,0:T(1,128)} %get-tuple-element.52) | copy-start | bytes 12292
  609.8 75.2 %copy-start.29 = (f32[1,1024]{1,0:T(1,128)S(1)}, f32[1,1024]{1,0:T(1,128)}, u32[]{:S(2)}) copy-start(f32[1,1024]{1,0:T(1,128)} %get-tuple-element.51) | copy-start | bytes 12292
  685.6 370.6 %copy-start.5 = (bf16[512,2048]{1,0:T(8,128)(2,1)S(1)}, bf16[512,2048]{1,0:T(8,128)(2,1)}, u32[]{:S(2)}) copy-start(bf16[512,2048]{1,0:T(8,128)(2,1)} %get-tuple-element.68) | copy-start | bytes 6291460
  685.6 370.6 %copy-start.27 = (f32[512]{0:T(512)S(1)}, f32[512]{0:T(512)}, u32[]{:S(2)}) copy-start(f32[512]{0:T(512)} %multiply_multiply_fusion) | copy-start | bytes 6148
  1056.2 8.8 copy-start.21
  1056.2 9.6 copy-start.20
  1056.2 10.4 copy-start.19
  1056.2 11.2 %copy-start.18 = (f32[128,1024]{1,0:T(8,128)S(1)}, f32[128,1024]{1,0:T(8,128)}, u32[]{:S(2)}) copy-start(f32[128,1024]{1,0:T(8,128)} %get-tuple-element.103) | copy-start | bytes 1572868
  1065.0 4.3 copy-start.15
  1066.6 3.8 copy-start.14
  (4 other events, 10.1 us)
Sparse Core Ops, SparseCore 0:
  337.5 61.9 all-reduce.5
  458.6 62.9 all-reduce.7
  572.2 108.5 all-reduce.9

commit v3 on v2

--- a/solution.py
+++ b/solution.py
@@ -245,14 +245,6 @@
     return table
 
 
-def cross_order(Z):
-    table = []
-    for z in range(Z):
-        zp = z ^ 1
-        table.append([zp] + [k for k in range(Z) if k not in (z, zp)] + [z])
-    return table
-
-
 class Scatter:
     def __init__(self, Z, parts, rc, xr, zu, zd, hr, outs, xs, zs, stage, fin, sems):
         self.Z, self.parts, self.rc, self.xr, self.zu, self.zd, self.hr, self.outs = Z, parts, rc, xr, zu, zd, hr, outs
@@ -269,7 +261,6 @@
         self.R = [p.shape[0] // (4 * Z) for p in parts]
         self.N = [p.shape[1] for p in parts]
         self.ffirst = far_first(Z)
-        self.xorder = cross_order(Z)
 
     def part(self, w, q, c, z, n=1):
         R = self.R[w]
@@ -293,15 +284,22 @@
         for k in (0, 1):
             self.c_copy(w, k).start()
 
-    def load(self, w, srcs, slot):
+    def stage_of(self, slot):
+        return self.stage[0].at[slot] if slot < 2 else self.stage[1]
+
+    def load_waits(self, w, srcs, slot):
         cps = []
         for i, src in enumerate(srcs):
-            if src is None:
-                continue
-            n = src.shape[0]
-            cp = pltpu.make_async_copy(src, self.stage.at[slot, i, pl.ds(0, n), pl.ds(0, self.N[w])], self.l_s.at[slot, i])
+            if src is not None:
+                n = src.shape[0]
+                cps.append(pltpu.make_async_copy(
+                    src, self.stage_of(slot).at[i, pl.ds(0, n), pl.ds(0, self.N[w])], self.l_s.at[slot, i]))
+        return cps
+
+    def load(self, w, srcs, slot):
+        cps = self.load_waits(w, srcs, slot)
+        for cp in cps:
             cp.start()
-            cps.append(cp)
         return cps
 
     def add(self, w, slot, idx, store, lo=0, hi=None, off=None):
@@ -316,7 +314,7 @@
                 rk = r
                 if off is not None and k in off:
                     rk = pl.multiple_of(r + off[k], G)
-                v = self.stage[slot, k, pl.ds(rk, G), pl.ds(0, N)].astype(jnp.float32)
+                v = self.stage_of(slot)[k, pl.ds(rk, G), pl.ds(0, N)].astype(jnp.float32)
                 tot = v if tot is None else tot + v
             store(r, tot)
             return 0
@@ -326,31 +324,55 @@
     def x_slot(self, w, n):
         return self.xs.at[w % 2, n, :, pl.ds(0, self.N[w])]
 
+    def order(self, n):
+        return pick(self.z, [t[n] for t in self.ffirst])
+
     def x_copy(self, w, n, half=None):
-        zt = pick(self.z, [t[n] for t in self.xorder])
+        zt = self.order(n)
         src = self.x_slot(w, n)
         H = self.R[w] // 2
         if half is None:
             return remote(src, self.rows(self.xr[w], zt, w), self.x_s.at[w, n], self.x_r.at[w, n], self.X)
         return remote(src.at[pl.ds(half * H, H), :], self.hrows(self.xr[w], zt, w, half), self.x_s.at[w, n], self.x_r.at[w, n], self.X)
 
-    def h_copy(self, w):
+    def h_copy(self, w, n=0):
         H = self.R[w] // 2
-        return remote(self.x_slot(w, 0).at[pl.ds(0, H), :], self.hr[w], self.h_s.at[w], self.h_r.at[w], self.ZP)
+        return remote(self.x_slot(w, n).at[pl.ds(0, H), :], self.hr[w], self.h_s.at[w], self.h_r.at[w], self.ZP)
+
+    def on_pair(self, n, yes, no):
+        if n == self.Z - 1:
+            no()
+            return
+        paired = self.order(n) == self.zp
+
+        @pl.when(paired)
+        def _():
+            yes()
+
+        @pl.when(jnp.logical_not(paired))
+        def _():
+            no()
+
+    def x_load(self, w, n):
+        zt = self.order(n)
+        return self.load(w, [self.part(w, 1 - self.q, self.c, zt), self.rows(self.rc[w], zt, w)], n % 2)
 
     def x_phase(self, w, n):
         Z, H = self.Z, self.R[w] // 2
+        last = n == Z - 1
         if n == 0:
             self.c_copy(w, 0).wait_recv()
-        zt = pick(self.z, [t[n] for t in self.xorder])
-        last = n == Z - 1
-        cps = self.load(w, [self.part(w, 1 - self.q, self.c, zt), self.rows(self.rc[w], zt, w)], 0)
+            self.x_load(w, 0)
+        if not last:
+            self.x_load(w, n + 1)
         if last:
             self.h_copy(w).wait_recv()
-            cps += self.load(w, [None, None, self.hr[w]], 0)
+            for cp in self.load(w, [None, None, self.hr[w]], n % 2):
+                cp.wait()
         if w >= 2:
             self.x_wait_send(w - 2, n)
-        for cp in cps:
+        zt = self.order(n)
+        for cp in self.load_waits(w, [self.part(w, 1 - self.q, self.c, zt), self.rows(self.rc[w], zt, w)], n % 2):
             cp.wait()
         dst = self.x_slot(w, n)
 
@@ -358,22 +380,24 @@
             dst[pl.ds(r, 16), :] = v.astype(jnp.bfloat16)
 
         if last:
-            self.add(w, 0, (0, 1, 2), store, 0, H)
-            self.add(w, 0, (0, 1), store, H, 2 * H)
+            self.add(w, n % 2, (0, 1, 2), store, 0, H)
+            self.add(w, n % 2, (0, 1), store, H, 2 * H)
+            self.x_copy(w, n).start()
         else:
-            self.add(w, 0, (0, 1), store)
-        if n == 0:
-            self.h_copy(w).start()
-            self.x_copy(w, 0, 1).start()
-        else:
-            self.x_copy(w, n).start()
+            self.add(w, n % 2, (0, 1), store)
+
+            def yes():
+                self.h_copy(w, n).start()
+                self.x_copy(w, n, 1).start()
+
+            self.on_pair(n, yes, lambda: self.x_copy(w, n).start())
 
     def x_wait_send(self, w, n):
-        if n == 0:
-            self.h_copy(w).wait_send()
-            self.x_copy(w, 0, 1).wait_send()
-        else:
-            self.x_copy(w, n).wait_send()
+        def yes():
+            self.h_copy(w, n).wait_send()
+            self.x_copy(w, n, 1).wait_send()
+
+        self.on_pair(n, yes, lambda: self.x_copy(w, n).wait_send())
 
     def z_copy(self, w, n, dest, up):
         src = self.zs.at[w % 2, n, :, pl.ds(0, self.N[w])]
@@ -381,11 +405,8 @@
             return remote(src, self.rows(self.zu[w], dest, w), self.z_s.at[w, n], self.u_r.at[w, dest], self.UP)
         return remote(src, self.rows(self.zd[w], dest, w), self.z_s.at[w, n], self.d_r.at[w, dest], self.DN)
 
-    def x_wait(self, w, zt):
-        for n in range(self.Z):
-            @pl.when(zt == pick(self.z, [t[n] for t in self.xorder]))
-            def _():
-                self.x_copy(w, n, 1 if n == 0 else None).wait_recv()
+    def x_wait(self, w, n):
+        self.on_pair(n, lambda: self.x_copy(w, n, 1).wait_recv(), lambda: self.x_copy(w, n).wait_recv())
 
     def z_phase(self, w, n):
         Z, H = self.Z, self.R[w] // 2
@@ -394,9 +415,9 @@
         dest = z if last else pick(z, [t[n] for t in self.ffirst])
         if n == 0:
             self.c_copy(w, 1).wait_recv()
-        self.x_wait(w, dest)
+        self.x_wait(w, n)
         cps = self.load(w, [self.part(w, self.q, self.c, dest), self.rows(self.rc[w], dest + Z, w),
-                            self.rows(self.xr[w], dest, w)], 1)
+                            self.rows(self.xr[w], dest, w)], 2)
         if not last:
             up = dest > z
             down = dest < z
@@ -405,13 +426,13 @@
             @pl.when(up & (z > 0))
             def _():
                 self.z_copy(w, n, dest, True).wait_recv()
-                cp = self.load(w, [None] * 3 + [self.rows(self.zu[w], dest, w)], 1)
+                cp = self.load(w, [None] * 3 + [self.rows(self.zu[w], dest, w)], 2)
                 cp[0].wait()
 
             @pl.when(down & (z < Z - 1))
             def _():
                 self.z_copy(w, n, dest, False).wait_recv()
-                cp = self.load(w, [None] * 3 + [self.rows(self.zd[w], dest, w)], 1)
+                cp = self.load(w, [None] * 3 + [self.rows(self.zd[w], dest, w)], 2)
                 cp[0].wait()
 
             if w >= 2:
@@ -437,13 +458,13 @@
             @pl.when(z > 0)
             def _():
                 self.z_copy(w, 0, dest, True).wait_recv()
-                cp = self.load(w, [None] * 3 + [self.rows(self.zu[w], dest, w)], 1)
+                cp = self.load(w, [None] * 3 + [self.rows(self.zu[w], dest, w)], 2)
                 cp[0].wait()
 
             @pl.when(z < Z - 1)
             def _():
                 self.z_copy(w, 0, dest, False).wait_recv()
-                cp = self.load(w, [None] * 4 + [self.rows(self.zd[w], dest, w)], 1)
+                cp = self.load(w, [None] * 4 + [self.rows(self.zd[w], dest, w)], 2)
                 cp[0].wait()
 
             for cp in cps:
@@ -457,15 +478,15 @@
 
             @pl.when((z > 0) & (z < Z - 1))
             def _():
-                self.add(w, 1, (0, 1, 2, 3, 4), store)
+                self.add(w, 2, (0, 1, 2, 3, 4), store)
 
             @pl.when(z == 0)
             def _():
-                self.add(w, 1, (0, 1, 2, 4), store)
+                self.add(w, 2, (0, 1, 2, 4), store)
 
             @pl.when(z == Z - 1)
             def _():
-                self.add(w, 1, (0, 1, 2, 3), store)
+                self.add(w, 2, (0, 1, 2, 3), store)
 
             self.f_copy(w).start()
 
@@ -479,10 +500,10 @@
                 def _(p=p, e=e):
                     ex = extra if e else ()
                     if p:
-                        self.add(w, 1, (0, 1) + ex, store, 0, H)
-                        self.add(w, 1, (0, 1, 2) + ex, store, H, 2 * H)
+                        self.add(w, 2, (0, 1) + ex, store, 0, H)
+                        self.add(w, 2, (0, 1, 2) + ex, store, H, 2 * H)
                     else:
-                        self.add(w, 1, (0, 1, 2) + ex, store)
+                        self.add(w, 2, (0, 1, 2) + ex, store)
 
     def z_wait_send(self, w, n):
         z = self.z
@@ -507,87 +528,6 @@
                 self.z_wait_send(w, n)
         if w == nw - 1:
             self.f_copy(w).wait()
-
-
-def scatter_body(nw, Z, *refs):
-    parts = refs[:nw]
-    vec, vec_out = refs[nw], refs[nw + 1]
-    outs = refs[nw + 2:2 * nw + 2]
-    rc, xr, zu, zd, hr = (refs[2 + (2 + k) * nw:2 + (3 + k) * nw] for k in range(5))
-    xs, zs, stage, fin, vsum, vgot, vbox = refs[7 * nw + 2:7 * nw + 9]
-    v_s, v_r, vz_s, vz_r = refs[7 * nw + 9:7 * nw + 13]
-    sems = refs[7 * nw + 13:]
-    sc = Scatter(Z, parts, rc, xr, zu, zd, hr, outs, xs, zs, stage, fin, sems)
-    far = [{"ctx": lax.rem(sc.z + o, Z)} for o in range(1, Z)]
-    barrier = pltpu.get_barrier_semaphore()
-    for d in [sc.X, sc.C] + far:
-        pl.semaphore_signal(barrier, inc=1, device_id=d, device_id_type=MESH)
-    pl.semaphore_wait(barrier, 1 + Z)
-    first = remote(vec, vgot.at[0], v_s.at[0], v_r.at[0], sc.C)
-    first.start()
-    for w in range(nw):
-        sc.c_send(w)
-    first.wait()
-    vsum[...] = vec[...] + vgot[0]
-    for n in range(Z):
-        sc.x_phase(0, n)
-    second = remote(vsum, vgot.at[1], v_s.at[1], v_r.at[1], sc.X)
-    second.start()
-    for n in range(Z):
-        sc.x_phase(1, n)
-    second.wait()
-    vsum[...] = vsum[...] + vgot[1]
-    for n in range(Z):
-        sc.z_phase(0, n)
-    cps = spread(Z, sc.z, vsum, vbox, vz_s, vz_r)
-    for w in range(1, nw):
-        if w + 1 < nw:
-            for n in range(Z):
-                sc.x_phase(w + 1, n)
-        for n in range(Z):
-            sc.z_phase(w, n)
-    spread_wait(Z, sc.z, vsum, vbox, vz_s, vz_r, cps)
-    total = vbox[0]
-    for k in range(1, Z):
-        total = total + vbox[k]
-    vec_out[...] = total
-    for w in range(nw):
-        sc.drain(w, nw)
-
-
-def scatter_all(parts, vec, Z, collective_id=1):
-    nw = len(parts)
-    dma = pltpu.SemaphoreType.DMA
-    bf = jnp.bfloat16
-    R = [p.shape[0] // (4 * Z) for p in parts]
-    N = [p.shape[1] for p in parts]
-    Rm, Nm = max(R), max(N)
-    sh = jax.ShapeDtypeStruct
-    vmem = pl.BlockSpec(memory_space=pltpu.VMEM)
-    anyw = pl.BlockSpec(memory_space=pl.ANY)
-    out_shape = ([sh(vec.shape, jnp.float32)] + [sh((r, n), jnp.float32) for r, n in zip(R, N)]
-                 + [sh((2 * Z * r, n), bf) for r, n in zip(R, N)]
-                 + [sh((Z * r, n), bf) for r, n in zip(R, N)]
-                 + [sh((Z * r, n), bf) for r, n in zip(R, N)]
-                 + [sh((Z * r, n), bf) for r, n in zip(R, N)]
-                 + [sh((r // 2, n), bf) for r, n in zip(R, N)])
-    res = pl.pallas_call(
-        functools.partial(scatter_body, nw, Z),
-        out_shape=out_shape,
-        in_specs=[anyw] * nw + [vmem],
-        out_specs=[vmem] + [anyw] * (len(out_shape) - 1),
-        scratch_shapes=[
-            pltpu.VMEM((2, Z, Rm, Nm), bf), pltpu.VMEM((2, Z - 1, Rm, Nm), bf), pltpu.VMEM((2, 5, Rm, Nm), bf),
-            pltpu.VMEM((Rm, Nm), jnp.float32),
-            pltpu.VMEM(vec.shape, jnp.float32), pltpu.VMEM((2,) + vec.shape, jnp.float32), pltpu.VMEM((Z,) + vec.shape, jnp.float32),
-            dma((2,)), dma((2,)), dma((Z - 1,)), dma((Z,)),
-            dma((nw, 2)), dma((nw, 2)), dma((nw, Z)), dma((nw, Z)), dma((nw, Z - 1)), dma((nw, Z)), dma((nw, Z)),
-            dma((nw,)), dma((nw,)), dma((2, 5)), dma((nw,)),
-        ],
-        compiler_params=pltpu.CompilerParams(collective_id=collective_id, has_side_effects=True),
-        name="grads_out",
-    )(*parts, vec)
-    return res[0], res[1:nw + 1]
 
 
 T8 = 8
@@ -771,35 +711,36 @@
     gsum[...] = lax.fori_loop(0, n // step, tile, jnp.zeros(gsum.shape, jnp.float32))
 
 
-def backward_scan(seqs, length, dm, h, pf, pg, lower, gain, link, rh, inner, gl, tail):
+def backward_scan(seqs, length, *a):
+    return [backward_scan_one(sq, length, *a) for sq in range(seqs)]
+
+
+def backward_scan_one(sq, length, dm, h, pf, pg, lower, gain, link, rh, inner, gl, tail):
     C = dm.shape[1]
     low, g = lower[...], gain[...]
     iota = lax.broadcasted_iota(jnp.int32, (T8, C), 0)
-    ends = []
     nt = length // T8
-    for sq in range(seqs):
-        def tile(k, carry):
-            vl, pr = carry
-            r = row_at(dm, sq * length + (nt - 1 - k) * T8)
-            rv = rh[r, :]
-            p = pg[r, :]
-            q = dm[r, :] * g * (p * sigmoid(p))
-            dh = q * rv - h[r, :] * (rv * rv * rv) * inner[r, :]
-            a = (low + (1.0 - low) * sigmoid(pf[r, :])) * link[r, :]
-            b = a * dh
-            for sh in (1, 2, 4):
-                keep = iota < T8 - sh
-                b = b + jnp.where(keep, a * pltpu.roll(b, T8 - sh, 0), 0.0)
-                a = jnp.where(keep, a * pltpu.roll(a, T8 - sh, 0), a)
-            v = b + a * vl
-            pa = a * pr
-            last = iota == T8 - 1
-            gl[r, :] = dh + jnp.where(last, vl, pltpu.roll(v, T8 - 1, 0))
-            tail[r, :] = jnp.where(last, pr, pltpu.roll(pa, T8 - 1, 0))
-            return v[0:1, :], pa[0:1, :]
-
-        ends.append(lax.fori_loop(0, nt, tile, (jnp.zeros((1, C), jnp.float32), jnp.ones((1, C), jnp.float32)), unroll=2))
-    return ends
+    def tile(k, carry):
+        vl, pr = carry
+        r = row_at(dm, sq * length + (nt - 1 - k) * T8)
+        rv = rh[r, :]
+        p = pg[r, :]
+        q = dm[r, :] * g * (p * sigmoid(p))
+        dh = q * rv - h[r, :] * (rv * rv * rv) * inner[r, :]
+        a = (low + (1.0 - low) * sigmoid(pf[r, :])) * link[r, :]
+        b = a * dh
+        for sh in (1, 2, 4):
+            keep = iota < T8 - sh
+            b = b + jnp.where(keep, a * pltpu.roll(b, T8 - sh, 0), 0.0)
+            a = jnp.where(keep, a * pltpu.roll(a, T8 - sh, 0), a)
+        v = b + a * vl
+        pa = a * pr
+        last = iota == T8 - 1
+        gl[r, :] = dh + jnp.where(last, vl, pltpu.roll(v, T8 - 1, 0))
+        tail[r, :] = jnp.where(last, pr, pltpu.roll(pa, T8 - 1, 0))
+        return v[0:1, :], pa[0:1, :]
+
+    return lax.fori_loop(0, nt, tile, (jnp.zeros((1, C), jnp.float32), jnp.ones((1, C), jnp.float32)), unroll=2)
 
 
 def backward_last(seqs, length, gl, tail, end, h, start, pi, pf, lower, link, dpi, dpf, lsum):
@@ -837,26 +778,6 @@
     lsum[...] = total
 
 
-def mixer_backward_body(Z, seqs, length, width, dm, h, pi, pf, pg, lower, gain, link, ids, rh, start,
-                        dpi, dpf, dpg, gsum, lsum,
-                        gl, tail, col, end, pay, box, row, got, s_c, r_c, s_t, r_t):
-    z, t = lax.axis_index("ctx"), lax.axis_index("tp")
-    n = seqs * length
-    barrier_all(Z, z, t)
-    backward_first(n, dm, h, pg, gain, rh, dpg, col, gsum)
-    swap_columns(col, row, got, s_t.at[0], r_t.at[0], 1 - t, n)
-    scale_columns(row, got, col, n, width, lambda v: v / width)
-    ends = backward_scan(seqs, length, dm, h, pf, pg, lower, gain, link, rh, col, gl, tail)
-    pay[4:8, :] = ids[...]
-    for sq in range(seqs):
-        pay[sq:sq + 1, :] = ends[sq][1]
-        pay[2 + sq:3 + sq, :] = ends[sq][0]
-    cps = spread(Z, z, pay, box, s_c, r_c)
-    spread_wait(Z, z, pay, box, s_c, r_c, cps)
-    end[...] = suffix_state(Z, z, box)
-    backward_last(seqs, length, gl, tail, end, h, start, pi, pf, lower, link, dpi, dpf, lsum)
-
-
 def mixer_scratch(Z, n, C):
     dma = pltpu.SemaphoreType.DMA
     f = jnp.float32
@@ -879,19 +800,421 @@
     )(pi, pf, pg, lower, gain, link, ids)
 
 
-def mixer_backward(Z, seqs, length, width, dm, h, pi, pf, pg, lower, gain, link, ids, rh, start, cid=3):
-    n, C = pi.shape
-    f, bf = jnp.float32, jnp.bfloat16
+TR = 64
+TC = 256
+
+
+def dot_t(a, b):
+    return lax.dot_general(a, b, (((1,), (1,)), ((), ())), preferred_element_type=jnp.float32)
+
+
+def dot_o(a, b):
+    return lax.dot_general(a, b, (((0,), (0,)), ((), ())), preferred_element_type=jnp.float32)
+
+
+def back_body(Z, seqs, length, *refs):
+    (gd, gg, gu, pn, po, x, mid, cot, n1, m, w_out, w_in, w_f, w_g, pi_h, pf_h, pg_h, h_h,
+     rh, start, ids, link, gain1, gain2, low, hgain) = refs[:26]
+    out, dx, vec_out = refs[26:29]
+    grads = refs[29:36]
+    mparts = refs[36:40]
+    rn, ro = refs[40:42]
+    k0 = 42
+    rc, xr, zu, zd, hr = (refs[k0 + 7 * i:k0 + 7 * (i + 1)] for i in range(5))
+    k0 += 35
+    (xs, zs, stage, stage_z, fin, dmid, gm, dm, h, pi, pf, pg, gl, tail, dpi, dpf, dpg, n1v, mv, wbuf, wbuf3, stg, sn, rn1,
+     e_f, e_b, vec, vgot, vbox, col, end, pay, box, row, got, acc) = refs[k0:k0 + 36]
+    k0 += 36
+    (l_h, l_n, w_s, g_s, n_s, n_r, o_s, o_r, t_s, t_r, e_s, eo_s, v_s, v_r, vz_s, vz_r, s_c, r_c, s_t, r_t) = refs[k0:k0 + 20]
+    sems = refs[k0 + 20:]
+    n, width = x.shape
+    C = dm.shape[1]
+    parts = (gd, gg, gu) + tuple(mparts)
+    sc = Scatter(Z, parts, rc, xr, zu, zd, hr, grads, xs, zs, (stage, stage_z), fin, sems)
+    z = sc.z
+    t = lax.axis_index("tp")
+    OTHER = {"tp": 1 - t}
+
+    barrier = pltpu.get_barrier_semaphore()
+    for d in [sc.X, sc.C, OTHER] + [{"ctx": lax.rem(z + o, Z)} for o in range(1, Z)]:
+        pl.semaphore_signal(barrier, inc=1, device_id=d, device_id_type=MESH)
+    pl.semaphore_wait(barrier, 2 + Z)
+
+    for w in range(3):
+        sc.c_send(w)
+
+    NP = n // TR
+    NC = width // TC
+
+    def rows_of(k):
+        return pl.ds(k * TR, TR)
+
+    def pn_copy(k):
+        return remote(pn.at[rows_of(k), :], rn.at[rows_of(k), :], n_s.at[k], n_r.at[k], OTHER)
+
+    def po_copy(k):
+        return remote(po.at[rows_of(k), :], ro.at[rows_of(k), :], o_s.at[k], o_r.at[k], OTHER)
+
+    for k in range(NP):
+        pn_copy(k).start()
+    for k in range(NP):
+        po_copy(k).start()
+    early = [pltpu.make_async_copy(a, b, l_h.at[i]) for i, (a, b) in enumerate(
+        ((pi_h, pi), (pf_h, pf), (pg_h, pg), (h_h, h), (n1, n1v), (m, mv)))]
+    for cp in early:
+        cp.start()
+    vec[...] = jnp.zeros_like(vec)
+
+    steps = []
+
+    def X(w):
+        return [functools.partial(sc.x_phase, w, k) for k in range(Z)]
+
+    def Zs(w):
+        return [functools.partial(sc.z_phase, w, k) for k in range(Z)]
+
+    def tick(*todo):
+        for s in todo:
+            s()
+
+    def piece(k, s, f_src, b_src):
+        r = rows_of(k)
+        return ([pltpu.make_async_copy(a.at[r, :], e_f.at[s, i], e_s.at[s, i]) for i, a in enumerate(f_src)]
+                + [pltpu.make_async_copy(a.at[r, :], e_b.at[s, i], e_s.at[s, 2 + i]) for i, a in enumerate(b_src)])
+
+    def p1_load(k):
+        pn_copy(k).wait_recv()
+        for cp in piece(k, k % 2, (mid, cot), (pn, rn)):
+            cp.start()
+
+    def p1(k):
+        s = k % 2
+        for cp in piece(k, s, (mid, cot), (pn, rn)):
+            cp.wait()
+        g = gain2[...]
+
+        def go(i, a):
+            r = pl.ds(pl.multiple_of(i * 16, 16), 16)
+            v, ct = e_f[s, 0, r, :], e_f[s, 1, r, :]
+            d = e_b[s, 0, r, :].astype(jnp.float32) + e_b[s, 1, r, :].astype(jnp.float32)
+            r2 = lax.rsqrt(jnp.mean(v * v, axis=1, keepdims=True) + epsilon)
+            gdn = d * g
+            inner = jnp.mean(gdn * v, axis=1, keepdims=True)
+            o = ct + gdn * r2 - v * (r2 * r2 * r2 * inner)
+            rr = pl.ds(pl.multiple_of(k * TR + i * 16, 16), 16)
+            dmid[rr, :] = o
+            gm[rr, :] = o.astype(jnp.bfloat16)
+            return a + jnp.sum(d * v * r2, axis=0, keepdims=True)
+
+        vec[1:2, :] = vec[1:2, :] + lax.fori_loop(0, TR // 16, go, jnp.zeros((1, width), jnp.float32))
+
+    def po_load(k):
+        po_copy(k).wait_recv()
+        for cp in piece(k, k % 2, (mid,), (po, ro)):
+            if cp is not None:
+                cp.start()
+
+    def o_store(k):
+        return pltpu.make_async_copy(e_f.at[k % 2, 1], out.at[rows_of(k), :], eo_s.at[k % 2])
+
+    def p_out(k):
+        s = k % 2
+        for cp in piece(k, s, (mid,), (po, ro)):
+            cp.wait()
+        if k >= 2:
+            o_store(k - 2).wait()
+
+        def go(i, _):
+            r = pl.ds(pl.multiple_of(i * 16, 16), 16)
+            e_f[s, 1, r, :] = e_f[s, 0, r, :] + (e_b[s, 0, r, :].astype(jnp.float32) + e_b[s, 1, r, :].astype(jnp.float32))
+            return 0
+
+        lax.fori_loop(0, TR // 16, go, 0)
+        o_store(k).start()
+
+    NW = C // TC
+
+    def w_load(j, s):
+        return pltpu.make_async_copy(w_out.at[:, pl.ds(pl.multiple_of(j * TC, TC), TC)], wbuf.at[s], w_s.at[s, 0])
+
+    def p2():
+        w_load(0, 0).start()
+
+        def go(j, _):
+            s = lax.rem(j, 2)
+
+            @pl.when(j + 1 < NW)
+            def _():
+                w_load(j + 1, 1 - s).start()
+
+            w_load(j, s).wait()
+            dm[:, pl.ds(pl.multiple_of(j * TC, TC), TC)] = jnp.dot(gm[...], wbuf[s], preferred_element_type=jnp.float32)
+            return 0
+
+        lax.fori_loop(0, NW, go, 0)
+
+    def g_copy(dst, j, s):
+        return pltpu.make_async_copy(stg.at[s], dst.at[pl.ds(pl.multiple_of(j * TC, TC), TC), :], g_s.at[s])
+
+    def p4(w, lhs, rhs):
+        dst = mparts[w - 3]
+
+        def go(j, _):
+            s = lax.rem(j, 2)
+
+            @pl.when(j >= 2)
+            def _():
+                g_copy(dst, j - 2, s).wait()
+
+            stg[s] = dot_o(lhs[:, pl.ds(pl.multiple_of(j * TC, TC), TC)], rhs[...]).astype(jnp.bfloat16)
+            g_copy(dst, j, s).start()
+            return 0
+
+        lax.fori_loop(0, NC, go, 0)
+        g_copy(dst, NC - 2, NC % 2).wait()
+        g_copy(dst, NC - 1, (NC - 1) % 2).wait()
+        sc.c_send(w)
+
+    def w3_start(j, s):
+        for i, a in enumerate((w_in, w_f, w_g)):
+            pltpu.make_async_copy(a.at[pl.ds(pl.multiple_of(j * TC, TC), TC), :], wbuf3.at[s, i], w_s.at[2 + s, i]).start()
+
+    def w3_wait(j, s):
+        for i, a in enumerate((w_in, w_f, w_g)):
+            pltpu.make_async_copy(a.at[pl.ds(pl.multiple_of(j * TC, TC), TC), :], wbuf3.at[s, i], w_s.at[2 + s, i]).wait()
+
+    def n_copy(j):
+        return remote(sn.at[j], rn1.at[j], t_s.at[j], t_r.at[j], OTHER)
+
+    def p5(j0, j1):
+        def go(j, _):
+            s = lax.rem(j, 2)
+
+            @pl.when(j + 1 < NC)
+            def _():
+                w3_start(j + 1, 1 - s)
+
+            w3_wait(j, s)
+            o = dot_t(dpi[...], wbuf3[s, 0]) + dot_t(dpf[...], wbuf3[s, 1]) + dot_t(dpg[...], wbuf3[s, 2])
+            sn[j] = o.astype(jnp.bfloat16)
+            n_copy(j).start()
+            return 0
+
+        lax.fori_loop(j0, j1, go, 0)
+
+    def x_load(j, s):
+        return pltpu.make_async_copy(x.at[:, pl.ds(j * TC, TC)], tail.at[:, pl.ds(s * TC, TC)], e_s.at[s, 0])
+
+    def p6a(j):
+        s = j % 2
+        if j == 0:
+            x_load(0, 0).start()
+        if j + 1 < NC:
+            x_load(j + 1, 1 - s).start()
+        x_load(j, s).wait()
+        n_copy(j).wait_recv()
+        g = gain1[:, j * TC:(j + 1) * TC]
+
+        def go(i, _):
+            r = pl.ds(pl.multiple_of(i * 16, 16), 16)
+            v = tail[r, s * TC:(s + 1) * TC]
+            d = sn[j, r, :].astype(jnp.float32) + rn1[j, r, :].astype(jnp.float32)
+            a, b = v * v, d * g * v
+            a, b = a[:, :128] + a[:, 128:], b[:, :128] + b[:, 128:]
+            if j == 0:
+                acc[0, r, :] = a
+                acc[1, r, :] = b
+            else:
+                acc[0, r, :] = acc[0, r, :] + a
+                acc[1, r, :] = acc[1, r, :] + b
+            return 0
+
+        lax.fori_loop(0, n // 16, go, 0, unroll=2)
+
+    def p6b():
+        def go(i, _):
+            r = pl.ds(pl.multiple_of(i * 16, 16), 16)
+            r1 = lax.rsqrt(jnp.sum(acc[0, r, :], axis=1, keepdims=True) / width + epsilon)
+            inner = jnp.sum(acc[1, r, :], axis=1, keepdims=True) / width
+            acc[0, r, :] = jnp.broadcast_to(r1, (16, 128))
+            acc[1, r, :] = jnp.broadcast_to(r1 * r1 * r1 * inner, (16, 128))
+            return 0
+
+        lax.fori_loop(0, n // 16, go, 0, unroll=2)
+
+    def dx_copy(j):
+        s = j % 2
+        return pltpu.make_async_copy(gl.at[:, pl.ds(s * TC, TC)], dx.at[:, pl.ds(j * TC, TC)], eo_s.at[s])
+
+    def p6c(j):
+        s = j % 2
+        if j == 0:
+            x_load(0, 0).start()
+        if j + 1 < NC:
+            x_load(j + 1, 1 - s).start()
+        x_load(j, s).wait()
+        if j >= 2:
+            dx_copy(j - 2).wait()
+        g = gain1[:, j * TC:(j + 1) * TC]
+
+        def go(i, total):
+            r = pl.ds(pl.multiple_of(i * 16, 16), 16)
+            v = tail[r, s * TC:(s + 1) * TC]
+            d = sn[j, r, :].astype(jnp.float32) + rn1[j, r, :].astype(jnp.float32)
+            r1 = jnp.concatenate([acc[0, r, :], acc[0, r, :]], axis=1)
+            ri = jnp.concatenate([acc[1, r, :], acc[1, r, :]], axis=1)
+            gl[r, s * TC:(s + 1) * TC] = dmid[r, j * TC:(j + 1) * TC] + d * g * r1 - v * ri
+            return total + jnp.sum(d * v * r1, axis=0, keepdims=True)
+
+        vec[0:1, j * TC:(j + 1) * TC] = lax.fori_loop(0, n // 16, go, jnp.zeros((1, TC), jnp.float32), unroll=2)
+        dx_copy(j).start()
+
+    x0, x1, x2, z0, z1, z2 = X(0), X(1), X(2), Zs(0), Zs(1), Zs(2)
+    x3, x4, x5, x6 = X(3), X(4), X(5), X(6)
+    z3, z4, z5, z6 = Zs(3), Zs(4), Zs(5), Zs(6)
+    tick(*x0, x1[0])
+    p1_load(0)
+    tick(x1[1])
+    between = [[z0[0], x1[2]], [x1[3]], [z0[1]], [], [z0[2], x2[0]], [], [z0[3], x2[1]], [x2[2]]]
+    for k in range(NP):
+        if k + 1 < NP:
+            p1_load(k + 1)
+        p1(k)
+        tick(*(between[k] if k < len(between) else []))
+    p2()
+    tick(x2[3], z1[0])
+    for cp in early:
+        cp.wait()
+    p4(3, gm, mv)
+    tick(z1[1])
+    backward_first(n, dm, h, pg, hgain, rh, dpg, col, acc_row(vec, 2, C))
+    column_to_rows(col, row, n)
+    swap = remote(row, got, s_t.at[0], r_t.at[0], OTHER)
+    swap.start()
+    tick(x3[0], x3[1])
+    swap.wait()
+    scale_columns(row, got, col, n, width, lambda v: v / width)
+    ends = []
+    for sq in range(seqs):
+        ends.append(backward_scan_one(sq, length, dm, h, pf, pg, low, hgain, link, rh, col, gl, tail))
+        tick(z1[2 + sq] if sq < 2 else (lambda: None))
+    pay[4:8, :] = ids[...]
+    for sq in range(seqs):
+        pay[sq:sq + 1, :] = ends[sq][1]
+        pay[2 + sq:3 + sq, :] = ends[sq][0]
+    cps = spread(Z, z, pay, box, s_c, r_c)
+    tick(x3[2], x3[3])
+    spread_wait(Z, z, pay, box, s_c, r_c, cps)
+    end[...] = suffix_state(Z, z, box)
+    backward_last(seqs, length, gl, tail, end, h, start, pi, pf, low, link, dpi, dpf, acc_row(vec, 3, C))
+    tick(z2[0])
+    w3_start(0, 0)
+    p4(4, n1v, dpi)
+    tick(x4[0], x4[1], z2[1])
+    p4(5, n1v, dpf)
+    tick(x4[2], x4[3], z2[2])
+    p4(6, n1v, dpg)
+    tick(z2[3], x5[0], x5[1])
+    p5(0, NC // 2)
+    tick(x5[2], x5[3], z3[0], z3[1])
+    p5(NC // 2, NC)
+    tick(z3[2], z3[3], *x6)
+    po_load(0)
+    outs = [[z4[0]], [], [z4[1]], [], [z4[2]], [], [z4[3]], []]
+    for k in range(NP):
+        if k + 1 < NP:
+            po_load(k + 1)
+        p_out(k)
+        tick(*(outs[k] if k < len(outs) else []))
+    for k in (NP - 2, NP - 1):
+        o_store(k).wait()
+    for j in range(NC):
+        p6a(j)
+        if j % 4 == 3 and j // 4 < 2:
+            tick(z5[j // 4])
+    p6b()
+    for j in range(NC):
+        p6c(j)
+        if j % 4 == 3 and j // 4 < 2:
+            tick(z5[2 + j // 4])
+    for j in (NC - 2, NC - 1):
+        dx_copy(j).wait()
+    first = remote(vec, vgot.at[0], v_s.at[0], v_r.at[0], sc.C)
+    first.start()
+    tick(z6[0])
+    first.wait()
+    vec[...] = vec[...] + vgot[0]
+    second = remote(vec, vgot.at[1], v_s.at[1], v_r.at[1], sc.X)
+    second.start()
+    tick(z6[1])
+    second.wait()
+    vec[...] = vec[...] + vgot[1]
+    cps = spread(Z, z, vec, vbox, vz_s, vz_r)
+    tick(z6[2], z6[3])
+    spread_wait(Z, z, vec, vbox, vz_s, vz_r, cps)
+    total = vbox[0]
+    for k in range(1, Z):
+        total = total + vbox[k]
+    vec_out[...] = total
+    for k in range(NP):
+        pn_copy(k).wait_send()
+        po_copy(k).wait_send()
+    for j in range(NC):
+        n_copy(j).wait_send()
+    for w in range(7):
+        sc.drain(w, 7)
+
+
+def acc_row(vec, k, C):
+    return vec.at[k:k + 1, pl.ds(0, C)]
+
+
+def back_all(Z, seqs, length, gd, gg, gu, pn, po, x, mid, cot, n1, m, w_out, w_in, w_f, w_g, pi, pf, pg, h,
+             rh, start, ids, link, gain1, gain2, low, hgain, cid=1):
+    n, width = x.shape
+    C = pi.shape[1]
+    dma = pltpu.SemaphoreType.DMA
+    bf, f = jnp.bfloat16, jnp.float32
     sh = jax.ShapeDtypeStruct
-    vm = pl.BlockSpec(memory_space=pltpu.VMEM)
-    return pl.pallas_call(
-        functools.partial(mixer_backward_body, Z, seqs, length, width),
-        out_shape=[sh((n, C), bf), sh((n, C), bf), sh((n, C), bf), sh((1, C), f), sh((1, C), f)],
-        in_specs=[vm] * 11, out_specs=[vm] * 5,
-        scratch_shapes=[pltpu.VMEM((n, C), f), pltpu.VMEM((n, C), f), pltpu.VMEM((n, 1), f), pltpu.VMEM((seqs, C), f)] + mixer_scratch(Z, n, C),
-        compiler_params=pltpu.CompilerParams(collective_id=cid, has_side_effects=True),
-        name="mixer_backward",
-    )(dm, h, pi, pf, pg, lower, gain, link, ids, rh, start)
+    anyw, vmem = pl.BlockSpec(memory_space=pl.ANY), pl.BlockSpec(memory_space=pltpu.VMEM)
+    shapes = [gd.shape, gg.shape, gu.shape] + [(width, C)] * 4
+    R = [s[0] // (4 * Z) for s in shapes]
+    N = [s[1] for s in shapes]
+    Rm, Nm = max(R), max(N)
+    NP, NC = n // TR, width // TC
+    out_shape = ([sh((n, width), f), sh((n, width), f), sh((8, width), f)]
+                 + [sh((r, k), f) for r, k in zip(R, N)]
+                 + [sh((width, C), bf)] * 4
+                 + [sh((n, width), bf)] * 2
+                 + [sh((2 * Z * r, k), bf) for r, k in zip(R, N)]
+                 + [sh((Z * r, k), bf) for r, k in zip(R, N)]
+                 + [sh((Z * r, k), bf) for r, k in zip(R, N)]
+                 + [sh((Z * r, k), bf) for r, k in zip(R, N)]
+                 + [sh((r // 2, k), bf) for r, k in zip(R, N)])
+    V = pltpu.VMEM
+    scratch = [
+        V((2, Z, Rm, Nm), bf), V((2, Z - 1, Rm, Nm), bf), V((2, 3, Rm, Nm), bf), V((5, Rm, Nm), bf), V((Rm, Nm), f),
+        V((n, width), f), V((n, width), bf), V((n, C), f), V((n, C), f), V((n, C), f), V((n, C), f), V((n, C), f),
+        V((n, C), f), V((n, C), f), V((n, C), bf), V((n, C), bf), V((n, C), bf), V((n, width), bf), V((n, C), bf),
+        V((2, width, TC), bf), V((2, 3, TC, C), bf), V((2, TC, C), bf), V((NC, n, TC), bf), V((NC, n, TC), bf),
+        V((2, 2, TR, width), f), V((2, 2, TR, width), bf), V((8, width), f), V((2, 8, width), f), V((Z, 8, width), f),
+        V((n, 1), f), V((seqs, C), f), V((8, C), f), V((Z, 8, C), f), V((n // 128, 128), f), V((n // 128, 128), f),
+        V((2, n, 128), f),
+        dma((6,)), dma((1,)), dma((4, 3)), dma((2,)), dma((NP,)), dma((NP,)), dma((NP,)), dma((NP,)), dma((NC,)), dma((NC,)),
+        dma((2, 4)), dma((2,)), dma((2,)), dma((2,)), dma((Z - 1,)), dma((Z,)), dma((Z - 1,)), dma((Z,)), dma((1,)), dma((1,)),
+        dma((7, 2)), dma((7, 2)), dma((7, Z)), dma((7, Z)), dma((7, Z - 1)), dma((7, Z)), dma((7, Z)),
+        dma((7,)), dma((7,)), dma((3, 5)), dma((7,)),
+    ]
+    res = pl.pallas_call(
+        functools.partial(back_body, Z, seqs, length),
+        out_shape=out_shape,
+        in_specs=[anyw] * 18 + [vmem] * 8,
+        out_specs=[anyw, anyw, vmem] + [anyw] * (len(out_shape) - 3),
+        scratch_shapes=scratch,
+        compiler_params=pltpu.CompilerParams(collective_id=cid, has_side_effects=True, vmem_limit_bytes=66_000_000),
+        name="backward",
+    )(gd, gg, gu, pn, po, x, mid, cot, n1, m, w_out, w_in, w_f, w_g, pi, pf, pg, h, rh, start, ids, link, gain1, gain2, low, hgain)
+    return res[0], res[1], res[2], res[3:10]
 
 
 def carried_in(x, axis, combine, identity, reverse):
@@ -1089,8 +1412,6 @@
     up_pre = jnp.dot(normed_two, wide_mup, preferred_element_type=f32)
     silu_mlp = jax.nn.silu(gate_pre)
     activated = (silu_mlp * up_pre).astype(bfloat)
-    mlp_out = lax.psum(times_back(activated, wide_down).astype(bfloat), "tp").astype(f32)
-    output = middle + mlp_out
     upstream = cotangent.reshape(rows_all, width)
     upstream_low = upstream.astype(bfloat)
     grad_activ = jnp.dot(upstream_low, wide_down, preferred_element_type=f32)
@@ -1099,57 +1420,59 @@
     grad_up_pre = (grad_activ * silu_mlp).astype(bfloat)
     grad_mgate = outer_sum(normed_two, grad_gate_pre).astype(bfloat)
     grad_mup = outer_sum(normed_two, grad_up_pre).astype(bfloat)
-    grad_normed_two = lax.psum(
-        (times_back(grad_gate_pre, wide_mgate) + times_back(grad_up_pre, wide_mup)).astype(bfloat),
-        "tp",
-    ).astype(f32)
-    grad_mlp_gain = jnp.sum(grad_normed_two * middle * scale_two, axis=0)
-    grad_middle = upstream + rms_backward(middle, scale_two, mlp_gain, grad_normed_two)
-    middle_low = grad_middle.astype(bfloat)
-    dm = jnp.dot(middle_low, wide_out, preferred_element_type=f32)
-    grad_out = outer_sum(middle_low, mixed_in).astype(bfloat)
+    down_part = times_back(activated, wide_down).astype(bfloat)
+    normed_part = (times_back(grad_gate_pre, wide_mgate) + times_back(grad_up_pre, wide_mup)).astype(bfloat)
     if small:
-        dpi, dpf, dpg, grad_hidden_gain, grad_lower = mixer_backward(
-            Z, seqs, length, width, dm, h, pi, pf, pg, low_row, gain_row, link, ids, rh, start
+        output, grad_resid, vectors, sums = back_all(
+            Z, seqs, length, grad_down, grad_mgate, grad_mup, normed_part, down_part, residual_in, middle, upstream,
+            normed_one, mixed_in, wide_out, wide_input, wide_forget, wide_gate, pi, pf, pg, h,
+            rh, start, ids, link, norm_gain[None, :], mlp_gain[None, :], low_row, gain_row
         )
-        grad_hidden_gain, grad_lower = grad_hidden_gain[0], grad_lower[0]
+        grad_norm_gain, grad_mlp_gain = vectors[0], vectors[1]
+        grad_hidden_gain, grad_lower = vectors[2, :channels], vectors[3, :channels]
     else:
+        output = middle + lax.psum(down_part, "tp").astype(f32)
+        grad_normed_two = lax.psum(normed_part, "tp").astype(f32)
+        grad_mlp_gain = jnp.sum(grad_normed_two * middle * scale_two, axis=0)
+        grad_middle = upstream + rms_backward(middle, scale_two, mlp_gain, grad_normed_two)
+        middle_low = grad_middle.astype(bfloat)
+        dm = jnp.dot(middle_low, wide_out, preferred_element_type=f32)
+        grad_out = outer_sum(middle_low, mixed_in).astype(bfloat)
         dpi, dpf, dpg, grad_hidden_gain, grad_lower = mixer_backward_plain(
             seqs, length, width, dm, h, pi, pf, pg, lower, hidden_gain, segs, rh, start
         )
-    grad_w_input = outer_sum(normed_one, dpi).astype(bfloat)
-    grad_w_forget = outer_sum(normed_one, dpf).astype(bfloat)
-    grad_w_gate = outer_sum(normed_one, dpg).astype(bfloat)
-    grad_normed_one = lax.psum(
-        (
-            times_back(dpi, wide_input) + times_back(dpf, wide_forget) + times_back(dpg, wide_gate)
-        ).astype(bfloat),
-        "tp",
-    ).astype(f32)
-    grad_norm_gain = jnp.sum(grad_normed_one * residual_in * scale_one, axis=0)
-    grad_resid = grad_middle + rms_backward(residual_in, scale_one, norm_gain, grad_normed_one)
-    parts = (grad_down, grad_mgate, grad_mup, grad_out, grad_w_input, grad_w_forget, grad_w_gate)
-    vectors = jnp.concatenate([grad_norm_gain, grad_mlp_gain, grad_lower, grad_hidden_gain])
-    if small:
-        vectors, sums = scatter_all(parts, vectors.reshape(-1, 128), Z)
-        vectors = vectors.reshape(-1)
-    else:
-        vectors = lax.psum(vectors, ("shard", "ctx"))
+        grad_w_input = outer_sum(normed_one, dpi).astype(bfloat)
+        grad_w_forget = outer_sum(normed_one, dpf).astype(bfloat)
+        grad_w_gate = outer_sum(normed_one, dpg).astype(bfloat)
+        grad_normed_one = lax.psum(
+            (
+                times_back(dpi, wide_input) + times_back(dpf, wide_forget) + times_back(dpg, wide_gate)
+            ).astype(bfloat),
+            "tp",
+        ).astype(f32)
+        grad_norm_gain = jnp.sum(grad_normed_one * residual_in * scale_one, axis=0)
+        grad_resid = grad_middle + rms_backward(residual_in, scale_one, norm_gain, grad_normed_one)
+        vectors = lax.psum(
+            jnp.concatenate([grad_norm_gain, grad_mlp_gain, grad_lower, grad_hidden_gain]), ("shard", "ctx")
+        )
+        grad_norm_gain, grad_mlp_gain = vectors[:width], vectors[width : 2 * width]
+        grad_lower = vectors[2 * width : 2 * width + channels]
+        grad_hidden_gain = vectors[2 * width + channels :]
         sums = [
             lax.psum_scatter(p, ("shard", "ctx"), scatter_dimension=0, tiled=True).astype(f32)
-            for p in parts
+            for p in (grad_down, grad_mgate, grad_mup, grad_out, grad_w_input, grad_w_forget, grad_w_gate)
         ]
     return (
         output.reshape(block_input.shape),
         grad_resid.reshape(block_input.shape),
-        vectors[:width],
-        vectors[2 * width : 2 * width + channels],
+        grad_norm_gain,
+        grad_lower,
         sums[4],
         sums[5],
         sums[6],
-        vectors[2 * width + channels :],
+        grad_hidden_gain,
         sums[3],
-        vectors[width : 2 * width],
+        grad_mlp_gain,
         sums[1],
         sums[2],
         sums[0],

time: 1090 us -> 897 us (0.82)
  waiting for transfers between devices: 171 us -> 62.1 us
  matrix products: 147 us -> 111 us
  Pallas kernels: 691 us -> 662 us
  other arithmetic: 41.2 us -> 16.9 us
    psum x2 -> x0, waiting for transfers between devices: 112 us -> none  [the longest x1 71 us: on_device(): lax.psum(times_back(activated, wide_down).astype(bfloat), 'tp').astype(f32)]
    pallas_call x2 -> x1, Pallas kernels: 395 us -> 366 us  [back_all(): pl.pallas_call(functools.partial(back_body, Z, seqs, length), out_shape=o...]
    dot_general x7 -> x3, matrix products: 49.2 us -> 27.3 us  [outer_sum(): lax.dot_general(left_mat, right_mat, (((0,), (0,)), ((), ())), preferred_...]
    add x2 -> x0, other arithmetic: 12.2 us -> none  [the longest x1 8.77 us: on_device(): grad_middle + rms_backward(residual_in, scale_one, norm_gain, grad_normed...]
    dot_general x7 -> x4, matrix products: 47.3 us -> 37.6 us  [times_back(): lax.dot_general(left_mat, right_mat, (((1,), (1,)), ((), ())), preferred_...]
  transfers between devices with their start and end apart: 3 -> 1, of which waited for: 3 -> 1; matrix products, arithmetic and copies ran while one was open for 6% -> 0% of each run, Pallas kernels for 0% -> 0%
where the time goes in v3:
time: 897 us; the launch traced here: 887 us
  Pallas kernels  662 us (74%)
  matrix products  111 us (12%)
  waiting for transfers between devices  62.1 us (7%)
  local copies, waits for them, and re-layouts  20.3 us (2%)
  other arithmetic  16.9 us (2%)
  between operations  14.7 us (2%)
    pallas_call x1, Pallas kernels, back_all(): pl.pallas_call(functools.partial(back_body, Z, seqs, length), out_shape=o...  366 us
    pallas_call x1, Pallas kernels, gather_all(): pl.pallas_call(functools.partial(gather_body, nw, Z, ahead, relay), out_s...  271 us
    psum x1, waiting for transfers between devices, on_device(): lax.psum(times_back(mixed_in, wide_out).astype(bfloat), 'tp').astype(f32)  62.1 us
    dot_general x4, matrix products, times_back(): lax.dot_general(left_mat, right_mat, (((1,), (1,)), ((), ())), preferred_...  37.6 us
    dot_general x3, matrix products, outer_sum(): lax.dot_general(left_mat, right_mat, (((0,), (0,)), ((), ())), preferred_...  27.3 us
    pallas_call x1, Pallas kernels, mixer_forward(): pl.pallas_call(functools.partial(mixer_forward_body, Z, seqs, length, wid...  24.6 us
  transfers between devices with their start and end apart: 1, of which 1 were waited for; matrix products, arithmetic and copies ran while one was open for 0% of the time, Pallas kernels for 0%

profile of v3, /device:TPU:0, one launch (start us, length us, event | category | flops | bytes accessed | tf_op | source)
XLA Modules:
  0.0 887.1 jit_solution(4773953207161506540)
XLA Ops:
  7.2 0.0 all-reduce.3.cloned.1.call-start
  7.2 0.8 convert_element_type.73
  8.1 0.2 slice_reduce_fusion.1
  8.2 0.1 compare_select_fusion
  8.3 0.1 pad_bitcast_fusion
  8.4 2.7 multiply_reduce_fusion.1
  11.1 0.9 copy.37
  12.0 0.7 convert_element_type.66.refs_0_
  12.7 1.8 convert_element_type.67.refs_1_
  14.5 1.9 convert_element_type.68.refs_2_
  16.4 1.8 convert_element_type.69.refs_3_
  18.2 0.9 convert_element_type.70.refs_4_
  19.1 0.9 convert_element_type.71.refs_5_
  20.1 0.9 convert_element_type.72.refs_6_
  21.0 0.4 multiply_convert_fusion.2.refs_8_
  21.4 271.3 %weights_in.1 = (bf16[2048,1024]{1,0:T(8,128)(2,1)}, bf16[2048,1024]{1,0:T(8,128)(2,1)}, bf16[2048,1024]{1,0:T(8,128)(2,1)}, bf16[2048,1024]{1,0:T(8,128)(2,1)},...) custom-call(bf16[128,1024]{1,0:T(8,128)(2,1)} %convert_element_type.66.refs_0_, ...), custom_call_target="tpu_custom_call" | custom-call | tf_op jit(solution)/shard_map/weights_in/pallas_call | solution.py:212
  292.7 6.0 fusion.9.pi.refs_14_
  298.7 3.7 fusion.10.pf.refs_15_
  302.4 3.7 fusion.11.pg.refs_16_
  306.1 0.1 pad_maximum_fusion
  306.2 0.7 broadcast_in_dim.34.ids.refs_20_
  306.9 24.6 %mixer_forward.1 = (f32[512,1024]{1,0:T(8,128)}, bf16[512,1024]{1,0:T(8,128)(2,1)}, f32[512,1]{1,0:T(8,128)}, f32[2,1024]{1,0:T(2,128)}) custom-call(f32[512,1024]{1,0:T(8,128)} %fusion.9.pi.refs_14_, f32[512,1024]{1,0:T(8,128)} %fusion.10.pf.refs_15_, f32[512,1024]{1,0:T(8,128)} %fusion.11.pg.refs_16_, f32[1,1024]{1,0:T(1,128)} %bitcast.68, ...), custom_call_target="tpu_custom_call" | custom-call | tf_op jit(solution)/shard_map/mixer_forward/pallas_call | solution.py:793
  331.5 6.2 convolution_convert_fusion.2
  337.8 62.1 %all-reduce.3.cloned.1.call-done = bf16[512,2048]{1,0:T(8,128)(2,1)} async-done(((bf16[512,2048]{1,0:T(8,128)(2,1)}), bf16[512,2048]{1,0:T(8,128)(2,1)}) %all-reduce.3.cloned.1.call-update) | async-done | bytes 2097168 | tf_op jit(solution)/shard_map/psum | solution.py:1407
  399.9 3.4 multiply_reduce_fusion
  403.3 2.0 copy-done.1
  405.3 0.4 multiply_convert_fusion.1
  405.8 9.7 %fusion.13 = f32[512,2816]{1,0:T(8,128)S(1)} fusion(bf16[512,2048]{1,0:T(8,128)(2,1)S(1)} %multiply_convert_fusion.1, bf16[2048,2816]{1,0:T(8,128)(2,1)} %get-tuple-element.40), kind=kOutput, calls=%fused_computation.35 | convolution fusion | flops 5905580032 | bytes 19398656 | tf_op jit(solution)/shard_map/dot_general | solution.py:1412
  415.6 8.0 fusion.12
  423.6 14.7 %fusion.2 = (bf16[512,2816]{1,0:T(8,128)(2,1)}, bf16[512,2816]{1,0:T(8,128)(2,1)}, bf16[512,2816]{1,0:T(8,128)(2,1)}) fusion(f32[512,2816]{1,0:T(8,128)} %fusion.12, f32[512,2816]{1,0:T(8,128)S(1)} %fusion.13, bf16[2048,2816]{1,0:T(8,128)(2,1)} %get-tuple-element.41, f32[512,2048]{1,0:T(8,128)S(1)} %bitcast.60), kind=kOutput, calls=%fused_computation.7 | convolution fusion | flops 5928255488 | bytes 35913728 | tf_op jit(solution)/shard_map/dot_general | solution.py:1417
  438.3 11.4 %fusion.14 = f32[512,2048]{1,0:T(8,128)S(1)} fusion(bf16[512,2816]{1,0:T(8,128)(2,1)} %get-tuple-element.60, bf16[2048,2816]{1,0:T(8,128)(2,1)} %get-tuple-element.39), kind=kOutput, calls=%fused_computation.36 | convolution fusion | flops 5905580032 | bytes 18612224 | tf_op jit(solution)/shard_map/dot_general | solution.py:1252
  449.7 9.0 %convolution_convert_fusion.1.refs_1_ = bf16[2048,2816]{1,0:T(8,128)(2,1)} fusion(bf16[512,2048]{1,0:T(8,128)(2,1)S(1)} %multiply_convert_fusion.1, bf16[512,2816]{1,0:T(8,128)(2,1)S(1)} %copy-done.22), kind=kOutput, calls=%fused_computation.2 | convolution fusion | flops 5911347200 | bytes 16515072 | tf_op jit(solution)/shard_map/dot_general | solution.py:1258
  458.8 10.0 %convolution_convert_fusion.3.refs_4_ = bf16[512,2048]{1,0:T(8,128)(2,1)} fusion(bf16[512,2816]{1,0:T(8,128)(2,1)S(1)} %copy-done.20, bf16[2048,2816]{1,0:T(8,128)(2,1)} %get-tuple-element.41), kind=kOutput, calls=%fused_computation.18 | convolution fusion | flops 5906628608 | bytes 16515072 | tf_op jit(solution)/shard_map/dot_general | solution.py:1252
  468.8 9.0 %convert_bitcast_fusion.refs_0_ = bf16[2048,2816]{1,0:T(8,128)(2,1)} fusion(bf16[512,2816]{1,0:T(8,128)(2,1)S(1)} %copy-done.20, f32[512,2048]{1,0:T(8,128)S(1)} %bitcast.61), kind=kOutput, calls=%fused_computation | convolution fusion | flops 5912395776 | bytes 18612224 | tf_op jit(solution)/shard_map/dot_general | solution.py:1258
  477.8 9.3 %convolution_convert_fusion.refs_2_ = bf16[2048,2816]{1,0:T(8,128)(2,1)} fusion(bf16[512,2048]{1,0:T(8,128)(2,1)S(1)} %multiply_convert_fusion.1, bf16[512,2816]{1,0:T(8,128)(2,1)S(1)} %copy-done.21), kind=kOutput, calls=%fused_computation.1 | convolution fusion | flops 5911347200 | bytes 16515072 | tf_op jit(solution)/shard_map/dot_general | solution.py:1258
  487.0 10.0 %add_convert_fusion.refs_3_ = bf16[512,2048]{1,0:T(8,128)(2,1)} fusion(f32[512,2048]{1,0:T(8,128)S(1)} %fusion.14, bf16[512,2816]{1,0:T(8,128)(2,1)S(1)} %copy-done.21, bf16[2048,2816]{1,0:T(8,128)(2,1)} %get-tuple-element.40), kind=kOutput, calls=%fused_computation.11 | convolution fusion | flops 5907677184 | bytes 20709376 | tf_op jit(solution)/shard_map/dot_general | solution.py:1252
  497.0 366.3 %backward.1 = (f32[512,2048]{1,0:T(8,128)}, f32[512,2048]{1,0:T(8,128)}, f32[8,2048]{1,0:T(8,128)}, f32[128,2816]{1,0:T(8,128)}, f32[128,2816]{1,0:T(8,128)}, /*...) custom-call(bf16[2048,2816]{1,0:T(8,128)(2,1)} %convert_bitcast_fusi, ...), custom_call_target="tpu_custom_call" | custom-call | tf_op jit(solution)/shard_map/backward/pallas_call | solution.py:1208
  863.3 1.4 fusion.8
  864.8 1.5 fusion.7
  866.3 4.8 copy.48
  871.2 2.1 copy.49
  873.3 0.8 copy.50
  874.1 0.8 copy.51
  874.9 0.8 copy.52
  875.7 0.8 copy.53
  876.5 1.1 copy.54
  877.6 1.1 copy.55
  878.7 1.1 copy.56
  (57 shorter events, 0.1 us)
Async XLA Ops:
  7.2 4.8 copy-start.13
  7.2 11.0 %copy-start.7 = (f32[128,2816]{1,0:T(8,128)S(1)}, f32[128,2816]{1,0:T(8,128)}, u32[]{:S(2)}) copy-start(f32[128,2816]{1,0:T(8,128)} %param.24) | copy-start | bytes 4325380
  7.2 392.7 %all-reduce.3.cloned.1.call-start = ((), (), s32[]{:S(2)}) async-start(), calls=%async_computation | async-start | bytes 4194304 | tf_op jit(solution)/shard_map/psum | solution.py:1407
  8.4 10.7 %copy-start.8 = (f32[128,2816]{1,0:T(8,128)S(1)}, f32[128,2816]{1,0:T(8,128)}, u32[]{:S(2)}) copy-start(f32[128,2816]{1,0:T(8,128)} %param.25) | copy-start | bytes 4325380
  11.9 8.1 copy-start.9
  14.5 6.5 copy-start
  14.5 6.5 copy-start.18
  21.4 281.0 %copy-start.2 = (bf16[512,2048]{1,0:T(8,128)(2,1)}, bf16[512,2048]{1,0:T(8,128)(2,1)S(1)}, u32[]{:S(2)}) copy-start(bf16[512,2048]{1,0:T(8,128)(2,1)S(1)} %multiply_convert_fusion.2.refs_8_) | copy-start | bytes 6291460
  292.7 6.0 copy-start.4
  298.7 3.7 copy-start.5
  337.7 67.6 %copy-start.19 = (f32[2048]{0:T(1024)S(1)}, f32[2048]{0:T(1024)}, u32[]{:S(2)}) copy-start(f32[2048]{0:T(1024)} %param.23) | copy-start | bytes 24580
  403.3 2.0 copy-start.1
  405.3 10.2 %slice-start = ((s8[11534336]{0:T(1024)(128)(4,1)}), s8[3145728]{0:T(1024)(128)(4,1)S(1)}, s32[]{:S(2)}) async-start(s8[11534336]{0:T(1024)(128)(4,1)} %bitcast.78), calls=%async_computation.1 | async-start | bytes 6291456
  405.8 9.8 %slice-start.1 = ((s8[11534336]{0:T(1024)(128)(4,1)}), s8[4194304]{0:T(1024)(128)(4,1)S(1)}, s32[]{:S(2)}) async-start(s8[11534336]{0:T(1024)(128)(4,1)} %bitcast.78), calls=%async_computation.2 | async-start | bytes 8388608
  405.8 9.8 %slice-start.2 = ((s8[11534336]{0:T(1024)(128)(4,1)}), s8[4194304]{0:T(1024)(128)(4,1)S(1)}, s32[]{:S(2)}) async-start(s8[11534336]{0:T(1024)(128)(4,1)} %bitcast.78), calls=%async_computation.3 | async-start | bytes 8388608
  415.6 8.0 copy-start.3
  438.3 11.4 %copy-start.22 = (bf16[512,2816]{1,0:T(8,128)(2,1)S(1)}, bf16[512,2816]{1,0:T(8,128)(2,1)}, u32[]{:S(2)}) copy-start(bf16[512,2816]{1,0:T(8,128)(2,1)} %get-tuple-element.60) | copy-start | bytes 8650756
  449.7 9.0 %copy-start.20 = (bf16[512,2816]{1,0:T(8,128)(2,1)S(1)}, bf16[512,2816]{1,0:T(8,128)(2,1)}, u32[]{:S(2)}) copy-start(bf16[512,2816]{1,0:T(8,128)(2,1)} %get-tuple-element.61) | copy-start | bytes 8650756
  468.8 9.0 %copy-start.21 = (bf16[512,2816]{1,0:T(8,128)(2,1)S(1)}, bf16[512,2816]{1,0:T(8,128)(2,1)}, u32[]{:S(2)}) copy-start(bf16[512,2816]{1,0:T(8,128)(2,1)} %get-tuple-element.59) | copy-start | bytes 8650756
  866.3 4.9 copy-start.6
  871.1 2.1 copy-start.17
  871.1 2.9 copy-start.16
  871.1 3.7 copy-start.15
  871.1 4.5 copy-start.14
  873.3 3.2 copy-start.12
  873.3 4.3 copy-start.11
  874.9 3.8 copy-start.10
Sparse Core Ops, SparseCore 0:
  337.9 61.9 all-reduce.2

commit v4 on v3

--- a/solution.py
+++ b/solution.py
@@ -14,214 +14,6 @@
     return pltpu.make_async_remote_copy(
         src_ref=src, dst_ref=dst, send_sem=send_sem, recv_sem=recv_sem,
         device_id=device, device_id_type=MESH)
-
-
-def gather_body(nw, Z, ahead, relay, *refs):
-    own, out = refs[:nw], refs[nw:2 * nw]
-    (s_up, r_up, s_dn, r_dn, s_x, r_x, s_c, r_c, s_h, r_h, l_sem) = refs[2 * nw:]
-    s, z = lax.axis_index("shard"), lax.axis_index("ctx")
-    q, c = s // 2, lax.rem(s, 2)
-    sx, sc = (1 - q) * 2 + c, q * 2 + (1 - c)
-    sxc = (1 - q) * 2 + (1 - c)
-    even = lax.rem(z, 2) == 0
-    zp = jnp.where(even, z + 1, z - 1)
-    rows = [r.shape[0] for r in own]
-
-    def block(w, s_, z_, part=0):
-        R = rows[w]
-        start = pl.multiple_of((s_ * Z + z_) * R, R)
-        if part == 0:
-            return out[w].at[pl.ds(start, R), :]
-        H = R // 2
-        return out[w].at[pl.ds(pl.multiple_of(start + (part - 1) * H, H), H), :]
-
-    UP, DN, XX, CC, ZP = {"ctx": z + 1}, {"ctx": z - 1}, {"shard": sx}, {"shard": sc}, {"ctx": zp}
-
-    def up(w, k, src=None):
-        b = block(w, s, z - k)
-        return remote(b if src is None else src, b, s_up.at[w, k], r_up.at[w, k], UP)
-
-    def dn(w, k, src=None):
-        b = block(w, s, z + k)
-        return remote(b if src is None else src, b, s_dn.at[w, k], r_dn.at[w, k], DN)
-
-    def origin(j):
-        return z if j == 0 else (z - j if j < Z else z + j - Z + 1)
-
-    def valid(j):
-        return (z >= j) if j < Z else (z + j - Z + 1 <= Z - 1)
-
-    def xx(w, j, part, src=None):
-        b = block(w, s, origin(j), part)
-        return remote(b if src is None else src, b, s_x.at[w, j], r_x.at[w, j], XX)
-
-    def xx_in(w, j, part):
-        b = block(w, sx, origin(j), part)
-        return remote(b, b, s_x.at[w, j], r_x.at[w, j], XX)
-
-    def cc(w, j, src=None):
-        b = block(w, s if j < 2 * Z - 1 else sx, origin(j % (2 * Z - 1)))
-        return remote(b if src is None else src, b, s_c.at[w, j], r_c.at[w, j], CC)
-
-    def cc_in(w, j):
-        b = block(w, sc if j < 2 * Z - 1 else sxc, origin(j % (2 * Z - 1)))
-        return remote(b, b, s_c.at[w, j], r_c.at[w, j], CC)
-
-    def half(w):
-        b = block(w, sx, z, 1)
-        return remote(b, b, s_h.at[w], r_h.at[w], ZP)
-
-    def half_in(w):
-        b = block(w, sx, zp, 1)
-        return remote(b, b, s_h.at[w], r_h.at[w], ZP)
-
-    barrier = pltpu.get_barrier_semaphore()
-    for d in (XX, CC):
-        pl.semaphore_signal(barrier, inc=1, device_id=d, device_id_type=MESH)
-
-    @pl.when(z < Z - 1)
-    def _():
-        pl.semaphore_signal(barrier, inc=1, device_id=UP, device_id_type=MESH)
-
-    @pl.when(z > 0)
-    def _():
-        pl.semaphore_signal(barrier, inc=1, device_id=DN, device_id_type=MESH)
-
-    pl.semaphore_wait(barrier, 2 + (z < Z - 1).astype(jnp.int32) + (z > 0).astype(jnp.int32))
-
-    local = []
-    for w in range(nw):
-        cp = pltpu.make_async_copy(own[w], block(w, s, z), l_sem.at[w])
-        cp.start()
-        local.append(cp)
-
-    def begin(w):
-        @pl.when(z < Z - 1)
-        def _():
-            up(w, 0, own[w]).start()
-
-        @pl.when(z > 0)
-        def _():
-            dn(w, 0, own[w]).start()
-
-        xx(w, 0, 0, own[w]).start()
-        cc(w, 0, own[w]).start()
-
-    def is_pair(j):
-        if j == 1:
-            return jnp.logical_not(even)
-        if j == Z:
-            return even
-        return None
-
-    def for_part(w, j, fn):
-        pair = is_pair(j) if relay else None
-        if pair is None:
-            fn(0)
-        else:
-            @pl.when(pair)
-            def _():
-                fn(2)
-
-            @pl.when(jnp.logical_not(pair))
-            def _():
-                fn(0)
-
-    def step(w, k):
-        @pl.when(z >= k)
-        def _():
-            remote(block(w, s, z - k), block(w, s, z - k), s_up.at[w, k - 1], r_up.at[w, k - 1], UP).wait_recv()
-            if k < Z - 1:
-                @pl.when(z < Z - 1)
-                def _():
-                    up(w, k).start()
-            for_part(w, k, lambda p: xx(w, k, p).start())
-            cc(w, k).start()
-
-        @pl.when(z + k <= Z - 1)
-        def _():
-            remote(block(w, s, z + k), block(w, s, z + k), s_dn.at[w, k - 1], r_dn.at[w, k - 1], DN).wait_recv()
-            if k < Z - 1:
-                @pl.when(z > 0)
-                def _():
-                    dn(w, k).start()
-            for_part(w, Z - 1 + k, lambda p: xx(w, Z - 1 + k, p).start())
-            cc(w, Z - 1 + k).start()
-
-    def xstep(w, j):
-        @pl.when(valid(j))
-        def _():
-            for_part(w, j, lambda p: xx_in(w, j, p).wait_recv())
-            if j == 0:
-                if relay:
-                    half(w).start()
-                cc(w, 2 * Z - 1).start()
-            else:
-                if relay and is_pair(j) is not None:
-                    @pl.when(is_pair(j))
-                    def _():
-                        half_in(w).wait_recv()
-                cc(w, 2 * Z - 1 + j).start()
-
-    def finish(w):
-        for j in range(4 * Z - 2):
-            @pl.when(valid(j % (2 * Z - 1)))
-            def _():
-                cc_in(w, j).wait_recv()
-                cc(w, j).wait_send()
-        for j in range(2 * Z - 1):
-            @pl.when(valid(j))
-            def _():
-                for_part(w, j, lambda p: xx(w, j, p).wait_send())
-        for k in range(Z - 1):
-            @pl.when((z >= k) & (z < Z - 1))
-            def _():
-                up(w, k).wait_send()
-
-            @pl.when((z + k <= Z - 1) & (z > 0))
-            def _():
-                dn(w, k).wait_send()
-        if relay:
-            half(w).wait_send()
-        local[w].wait()
-
-    for w in range(min(ahead, nw)):
-        begin(w)
-    for w in range(nw):
-        for k in range(1, Z):
-            step(w, k)
-            if k == 1:
-                xstep(w, 0)
-                if w + ahead < nw:
-                    begin(w + ahead)
-            else:
-                xstep(w, k - 1)
-                xstep(w, Z - 1 + k - 1)
-            if w > 0 and k == 1:
-                xstep(w - 1, Z - 1)
-                xstep(w - 1, 2 * Z - 2)
-    xstep(nw - 1, Z - 1)
-    xstep(nw - 1, 2 * Z - 2)
-    for w in range(nw):
-        finish(w)
-
-
-def gather_all(shards, S, Z, collective_id=0, ahead=2, relay=True):
-    nw = len(shards)
-    dma = pltpu.SemaphoreType.DMA
-    return pl.pallas_call(
-        functools.partial(gather_body, nw, Z, ahead, relay),
-        out_shape=[jax.ShapeDtypeStruct((a.shape[0] * S * Z, a.shape[1]), a.dtype) for a in shards],
-        in_specs=[pl.BlockSpec(memory_space=pltpu.VMEM)] * nw,
-        out_specs=[pl.BlockSpec(memory_space=pl.ANY)] * nw,
-        scratch_shapes=[
-            dma((nw, Z - 1)), dma((nw, Z - 1)), dma((nw, Z - 1)), dma((nw, Z - 1)),
-            dma((nw, 2 * Z - 1)), dma((nw, 2 * Z - 1)),
-            dma((nw, 4 * Z - 2)), dma((nw, 4 * Z - 2)), dma((nw,)), dma((nw,)), dma((nw,)),
-        ],
-        compiler_params=pltpu.CompilerParams(collective_id=collective_id, has_side_effects=True),
-        name="weights_in",
-    )(*shards)
 
 
 def pick(z, values):
@@ -598,32 +390,30 @@
     return pl.ds(pl.multiple_of(t, T8), T8)
 
 
-def forward_scan(seqs, length, pi, pf, lower, link, h, cum):
+def forward_scan_one(sq, length, pi, pf, lower, link, h, cum):
     C = pi.shape[1]
     low = lower[...]
     iota = lax.broadcasted_iota(jnp.int32, (T8, C), 0)
-    ends = []
-    for sq in range(seqs):
-        def tile(i, carry):
-            hl, pr = carry
-            r = row_at(pi, sq * length + i * T8)
-            s = sigmoid(pf[r, :])
-            forget = low + (1.0 - low) * s
-            x = pi[r, :]
-            b = x * sigmoid(x) * (1.0 - forget)
-            a = forget * link[r, :]
-            for sh in (1, 2, 4):
-                keep = iota >= sh
-                b = b + jnp.where(keep, a * pltpu.roll(b, sh, 0), 0.0)
-                a = jnp.where(keep, a * pltpu.roll(a, sh, 0), a)
-            b = b + a * hl
-            a = a * pr
-            h[r, :] = b
-            cum[r, :] = a
-            return b[T8 - 1:T8, :], a[T8 - 1:T8, :]
-
-        ends.append(lax.fori_loop(0, length // T8, tile, (jnp.zeros((1, C), jnp.float32), jnp.ones((1, C), jnp.float32)), unroll=2))
-    return ends
+
+    def tile(i, carry):
+        hl, pr = carry
+        r = row_at(pi, sq * length + i * T8)
+        s = sigmoid(pf[r, :])
+        forget = low + (1.0 - low) * s
+        x = pi[r, :]
+        b = x * sigmoid(x) * (1.0 - forget)
+        a = forget * link[r, :]
+        for sh in (1, 2, 4):
+            keep = iota >= sh
+            b = b + jnp.where(keep, a * pltpu.roll(b, sh, 0), 0.0)
+            a = jnp.where(keep, a * pltpu.roll(a, sh, 0), a)
+        b = b + a * hl
+        a = a * pr
+        h[r, :] = b
+        cum[r, :] = a
+        return b[T8 - 1:T8, :], a[T8 - 1:T8, :]
+
+    return lax.fori_loop(0, length // T8, tile, (jnp.zeros((1, C), jnp.float32), jnp.ones((1, C), jnp.float32)), unroll=2)
 
 
 def forward_finish(seqs, length, h, cum, start, col):
@@ -660,38 +450,6 @@
         return 0
 
     lax.fori_loop(0, h.shape[0] // step, tile, 0)
-
-
-def mixer_forward_body(Z, seqs, length, width, pi, pf, pg, lower, gain, link, ids, h, m, rh, start,
-                       cum, pay, box, row, got, s_c, r_c, s_t, r_t):
-    z, t = lax.axis_index("ctx"), lax.axis_index("tp")
-    n = seqs * length
-    barrier_all(Z, z, t)
-    ends = forward_scan(seqs, length, pi, pf, lower, link, h, cum)
-    pay[4:8, :] = ids[...]
-    for sq in range(seqs):
-        pay[sq:sq + 1, :] = ends[sq][1]
-        pay[2 + sq:3 + sq, :] = ends[sq][0]
-    cps = spread(Z, z, pay, box, s_c, r_c)
-    spread_wait(Z, z, pay, box, s_c, r_c, cps)
-    start[...] = prefix_state(Z, z, box)
-    forward_finish(seqs, length, h, cum, start, rh)
-    swap_columns(rh, row, got, s_t.at[0], r_t.at[0], 1 - t, n)
-    scale_columns(row, got, rh, n, width, lambda v: lax.rsqrt(v / width + epsilon))
-    mixed(h, rh, gain, pg, m)
-
-
-def barrier_all(Z, z, t):
-    barrier = pltpu.get_barrier_semaphore()
-    for o in range(1, Z):
-        pl.semaphore_signal(barrier, inc=1, device_id={"ctx": lax.rem(z + o, Z)}, device_id_type=MESH)
-    pl.semaphore_signal(barrier, inc=1, device_id={"tp": 1 - t}, device_id_type=MESH)
-    pl.semaphore_wait(barrier, Z)
-
-
-def slope(v):
-    s = sigmoid(v)
-    return s * (1.0 + v * (1.0 - s))
 
 
 def backward_first(n, dm, h, pg, gain, rh, dpg, col, gsum, step=16):
@@ -709,10 +467,6 @@
         return acc + jnp.sum(hr * sl, axis=0, keepdims=True)
 
     gsum[...] = lax.fori_loop(0, n // step, tile, jnp.zeros(gsum.shape, jnp.float32))
-
-
-def backward_scan(seqs, length, *a):
-    return [backward_scan_one(sq, length, *a) for sq in range(seqs)]
 
 
 def backward_scan_one(sq, length, dm, h, pf, pg, lower, gain, link, rh, inner, gl, tail):
@@ -778,26 +532,433 @@
     lsum[...] = total
 
 
-def mixer_scratch(Z, n, C):
+def gather_steps(nw, Z, ahead, relay, own, out, sems):
+    (s_up, r_up, s_dn, r_dn, s_x, r_x, s_c, r_c, s_h, r_h, l_sem) = sems
+    s, z = lax.axis_index("shard"), lax.axis_index("ctx")
+    q, c = s // 2, lax.rem(s, 2)
+    sx, sc = (1 - q) * 2 + c, q * 2 + (1 - c)
+    sxc = (1 - q) * 2 + (1 - c)
+    even = lax.rem(z, 2) == 0
+    zp = jnp.where(even, z + 1, z - 1)
+    rows = [r.shape[0] for r in own]
+
+    def block(w, s_, z_, part=0):
+        R = rows[w]
+        start = pl.multiple_of((s_ * Z + z_) * R, R)
+        if part == 0:
+            return out[w].at[pl.ds(start, R), :]
+        H = R // 2
+        return out[w].at[pl.ds(pl.multiple_of(start + (part - 1) * H, H), H), :]
+
+    UP, DN, XX, CC, ZP = {"ctx": z + 1}, {"ctx": z - 1}, {"shard": sx}, {"shard": sc}, {"ctx": zp}
+
+    def up(w, k, src=None):
+        b = block(w, s, z - k)
+        return remote(b if src is None else src, b, s_up.at[w, k], r_up.at[w, k], UP)
+
+    def dn(w, k, src=None):
+        b = block(w, s, z + k)
+        return remote(b if src is None else src, b, s_dn.at[w, k], r_dn.at[w, k], DN)
+
+    def origin(j):
+        return z if j == 0 else (z - j if j < Z else z + j - Z + 1)
+
+    def valid(j):
+        return (z >= j) if j < Z else (z + j - Z + 1 <= Z - 1)
+
+    def xx(w, j, part, src=None):
+        b = block(w, s, origin(j), part)
+        return remote(b if src is None else src, b, s_x.at[w, j], r_x.at[w, j], XX)
+
+    def xx_in(w, j, part):
+        b = block(w, sx, origin(j), part)
+        return remote(b, b, s_x.at[w, j], r_x.at[w, j], XX)
+
+    def cc(w, j, src=None):
+        b = block(w, s if j < 2 * Z - 1 else sx, origin(j % (2 * Z - 1)))
+        return remote(b if src is None else src, b, s_c.at[w, j], r_c.at[w, j], CC)
+
+    def cc_in(w, j):
+        b = block(w, sc if j < 2 * Z - 1 else sxc, origin(j % (2 * Z - 1)))
+        return remote(b, b, s_c.at[w, j], r_c.at[w, j], CC)
+
+    def half(w):
+        b = block(w, sx, z, 1)
+        return remote(b, b, s_h.at[w], r_h.at[w], ZP)
+
+    def half_in(w):
+        b = block(w, sx, zp, 1)
+        return remote(b, b, s_h.at[w], r_h.at[w], ZP)
+
+    local = []
+    for w in range(nw):
+        local.append(pltpu.make_async_copy(own[w], block(w, s, z), l_sem.at[w]))
+
+    def begin(w):
+        local[w].start()
+
+        @pl.when(z < Z - 1)
+        def _():
+            up(w, 0, own[w]).start()
+
+        @pl.when(z > 0)
+        def _():
+            dn(w, 0, own[w]).start()
+
+        xx(w, 0, 0, own[w]).start()
+        cc(w, 0, own[w]).start()
+
+    def is_pair(j):
+        if j == 1:
+            return jnp.logical_not(even)
+        if j == Z:
+            return even
+        return None
+
+    def for_part(w, j, fn):
+        pair = is_pair(j) if relay else None
+        if pair is None:
+            fn(0)
+        else:
+            @pl.when(pair)
+            def _():
+                fn(2)
+
+            @pl.when(jnp.logical_not(pair))
+            def _():
+                fn(0)
+
+    def step(w, k):
+        @pl.when(z >= k)
+        def _():
+            remote(block(w, s, z - k), block(w, s, z - k), s_up.at[w, k - 1], r_up.at[w, k - 1], UP).wait_recv()
+            if k < Z - 1:
+                @pl.when(z < Z - 1)
+                def _():
+                    up(w, k).start()
+            for_part(w, k, lambda p: xx(w, k, p).start())
+            cc(w, k).start()
+
+        @pl.when(z + k <= Z - 1)
+        def _():
+            remote(block(w, s, z + k), block(w, s, z + k), s_dn.at[w, k - 1], r_dn.at[w, k - 1], DN).wait_recv()
+            if k < Z - 1:
+                @pl.when(z > 0)
+                def _():
+                    dn(w, k).start()
+            for_part(w, Z - 1 + k, lambda p: xx(w, Z - 1 + k, p).start())
+            cc(w, Z - 1 + k).start()
+
+    def xstep(w, j):
+        @pl.when(valid(j))
+        def _():
+            for_part(w, j, lambda p: xx_in(w, j, p).wait_recv())
+            if j == 0:
+                if relay:
+                    half(w).start()
+                cc(w, 2 * Z - 1).start()
+            else:
+                if relay and is_pair(j) is not None:
+                    @pl.when(is_pair(j))
+                    def _():
+                        half_in(w).wait_recv()
+                cc(w, 2 * Z - 1 + j).start()
+
+    def finish(w):
+        for j in range(4 * Z - 2):
+            @pl.when(valid(j % (2 * Z - 1)))
+            def _():
+                cc_in(w, j).wait_recv()
+                cc(w, j).wait_send()
+        for j in range(2 * Z - 1):
+            @pl.when(valid(j))
+            def _():
+                for_part(w, j, lambda p: xx(w, j, p).wait_send())
+        for k in range(Z - 1):
+            @pl.when((z >= k) & (z < Z - 1))
+            def _():
+                up(w, k).wait_send()
+
+            @pl.when((z + k <= Z - 1) & (z > 0))
+            def _():
+                dn(w, k).wait_send()
+        if relay:
+            half(w).wait_send()
+        local[w].wait()
+
+    def tick(w, k):
+        step(w, k)
+        if k == 1:
+            xstep(w, 0)
+            if w + ahead < nw:
+                begin(w + ahead)
+        else:
+            xstep(w, k - 1)
+            xstep(w, Z - 1 + k - 1)
+        if w > 0 and k == 1:
+            xstep(w - 1, Z - 1)
+            xstep(w - 1, 2 * Z - 2)
+
+    def last():
+        xstep(nw - 1, Z - 1)
+        xstep(nw - 1, 2 * Z - 2)
+
+    return begin, tick, last, finish
+
+
+def front_body(Z, seqs, length, ahead, *refs):
+    nw = 7
+    own = refs[:nw]
+    x, cot, gain1, gain2, low, hgain, link, ids = refs[nw:nw + 8]
+    k0 = nw + 8
+    wide = refs[k0:k0 + nw]
+    k0 += nw
+    n1_o, pi_o, pf_o, pg_o, h_o, m_o, mid_o, n2_o, gate_o, up_o, act_o, gy_o, gd_o, rh, start = refs[k0:k0 + 15]
+    k0 += 15
+    (xv, n1, n2, pi, pf, pg, h, cum, m, wbuf, wob, pn, rn, gate, up, act, gy, stg, e_f,
+     pay, box, row, got) = refs[k0:k0 + 23]
+    k0 += 23
+    s_c, r_c, s_t, r_t, n_s, n_r, w_s, o_s, e_s, g_s, x_s = refs[k0:k0 + 11]
+    sems = refs[k0 + 11:]
+    w_in, w_f, w_g, w_out, w_mg, w_mu, w_dn = wide
+    n, width = x.shape
+    C, F = pi.shape[1], gate.shape[1]
+    s, z, t = lax.axis_index("shard"), lax.axis_index("ctx"), lax.axis_index("tp")
+    q, c = s // 2, lax.rem(s, 2)
+    OTHER = {"tp": 1 - t}
+    begin, tick, last, finish = gather_steps(nw, Z, ahead, True, own, wide, sems)
+    NP, NF, NW, NC = n // TR, F // TC, C // TC, width // TC
+
+    barrier = pltpu.get_barrier_semaphore()
+    for d in [{"shard": (1 - q) * 2 + c}, {"shard": q * 2 + (1 - c)}, OTHER] + [{"ctx": lax.rem(z + o, Z)} for o in range(1, Z)]:
+        pl.semaphore_signal(barrier, inc=1, device_id=d, device_id_type=MESH)
+    pl.semaphore_wait(barrier, 2 + Z)
+
+    for w in range(ahead):
+        begin(w)
+    load_x = pltpu.make_async_copy(x, xv, x_s.at[0])
+    load_x.start()
+    done = []
+
+    def put(src, dst, k):
+        cp = pltpu.make_async_copy(src, dst, o_s.at[k])
+        cp.start()
+        done.append(cp)
+
+    def norm_in():
+        load_x.wait()
+        g = gain1[...]
+
+        def go(i, _):
+            r = pl.ds(pl.multiple_of(i * 16, 16), 16)
+            v = xv[r, :]
+            n1[r, :] = (v * lax.rsqrt(jnp.mean(v * v, axis=1, keepdims=True) + epsilon) * g).astype(jnp.bfloat16)
+            return 0
+
+        lax.fori_loop(0, n // 16, go, 0, unroll=2)
+        put(n1, n1_o, 0)
+
+    def times(lhs, w, dst, tiles, after=None):
+        def load(j, s):
+            return pltpu.make_async_copy(w.at[:, pl.ds(pl.multiple_of(j * TC, TC), TC)], wbuf.at[s], w_s.at[s])
+
+        load(0, 0).start()
+
+        def go(j, _):
+            s = lax.rem(j, 2)
+
+            @pl.when(j + 1 < tiles)
+            def _():
+                load(j + 1, 1 - s).start()
+
+            load(j, s).wait()
+            dst[:, pl.ds(pl.multiple_of(j * TC, TC), TC)] = jnp.dot(lhs[...], wbuf[s], preferred_element_type=jnp.float32)
+            if after is not None:
+                after(j)
+            return 0
+
+        lax.fori_loop(0, tiles, go, 0)
+
+    def rows_of(k):
+        return pl.ds(k * TR, TR)
+
+    def pn_copy(k):
+        return remote(pn.at[rows_of(k), :], rn.at[rows_of(k), :], n_s.at[k], n_r.at[k], OTHER)
+
+    def out_product():
+        def load(j, s):
+            return pltpu.make_async_copy(w_out.at[pl.ds(pl.multiple_of(j * TC, TC), TC), :], wob.at[s], w_s.at[s])
+
+        load(0, 0).start()
+
+        def go(j, _):
+            s = lax.rem(j, 2)
+
+            @pl.when(j + 1 < NC)
+            def _():
+                load(j + 1, 1 - s).start()
+
+            load(j, s).wait()
+            pn[:, pl.ds(pl.multiple_of(j * TC, TC), TC)] = dot_t(m[...], wob[s]).astype(jnp.bfloat16)
+            return 0
+
+        lax.fori_loop(0, NC, go, 0)
+        for k in range(NP):
+            pn_copy(k).start()
+
+    def middle(k):
+        pn_copy(k).wait_recv()
+        g = gain2[...]
+
+        def go(i, _):
+            r = pl.ds(pl.multiple_of(k * TR + i * 16, 16), 16)
+            v = xv[r, :] + (pn[r, :].astype(jnp.float32) + rn[r, :].astype(jnp.float32))
+            xv[r, :] = v
+            n2[r, :] = (v * lax.rsqrt(jnp.mean(v * v, axis=1, keepdims=True) + epsilon) * g).astype(jnp.bfloat16)
+            return 0
+
+        lax.fori_loop(0, TR // 16, go, 0)
+
+    def cot_load(k):
+        return pltpu.make_async_copy(cot.at[rows_of(k), :], e_f.at[k % 2], e_s.at[k % 2])
+
+    def cot_low():
+        cot_load(0).start()
+        for k in range(NP):
+            if k + 1 < NP:
+                cot_load(k + 1).start()
+            cot_load(k).wait()
+            gy[rows_of(k), :] = e_f[k % 2].astype(jnp.bfloat16)
+
+    def activate(j):
+        cols = pl.ds(pl.multiple_of(j * TC, TC), TC)
+
+        def go(i, _):
+            r = pl.ds(pl.multiple_of(i * 32, 32), 32)
+            v = gate[r, cols]
+            act[r, cols] = (v * sigmoid(v) * up[r, cols]).astype(jnp.bfloat16)
+            return 0
+
+        lax.fori_loop(0, n // 32, go, 0)
+
+    def gd_copy(j, s):
+        return pltpu.make_async_copy(stg.at[s], gd_o.at[pl.ds(pl.multiple_of(j * TC, TC), TC), :], g_s.at[s])
+
+    def down_grad(j0, j1):
+        def go(j, _):
+            s = lax.rem(j, 2)
+
+            @pl.when(j >= 2)
+            def _():
+                gd_copy(j - 2, s).wait()
+
+            stg[s] = dot_o(gy[:, pl.ds(pl.multiple_of(j * TC, TC), TC)], act[...]).astype(jnp.bfloat16)
+            gd_copy(j, s).start()
+            return 0
+
+        lax.fori_loop(j0, j1, go, 0)
+
+    norm_in()
+    for w, src, dst, o, k in ((0, w_in, pi, pi_o, 1), (1, w_f, pf, pf_o, 2), (2, w_g, pg, pg_o, 3)):
+        if w == 0:
+            tick(0, 1)
+            tick(0, 2)
+            tick(0, 3)
+        tick(w + 1, 1)
+        tick(w + 1, 2)
+        finish(w)
+        times(n1, src, dst, NW)
+        put(dst, o, k)
+        if w < 2:
+            tick(w + 1, 3)
+    ends = [forward_scan_one(0, length, pi, pf, low, link, h, cum)]
+    tick(3, 3)
+    for sq in range(1, seqs):
+        ends.append(forward_scan_one(sq, length, pi, pf, low, link, h, cum))
+    pay[4:8, :] = ids[...]
+    for sq in range(seqs):
+        pay[sq:sq + 1, :] = ends[sq][1]
+        pay[2 + sq:3 + sq, :] = ends[sq][0]
+    cps = spread(Z, z, pay, box, s_c, r_c)
+    tick(4, 1)
+    cot_low()
+    put(gy, gy_o, 4)
+    spread_wait(Z, z, pay, box, s_c, r_c, cps)
+    start[...] = prefix_state(Z, z, box)
+    forward_finish(seqs, length, h, cum, start, rh)
+    put(h, h_o, 5)
+    swap_columns(rh, row, got, s_t.at[0], r_t.at[0], 1 - t, n)
+    scale_columns(row, got, rh, n, width, lambda v: lax.rsqrt(v / width + epsilon))
+    mixed(h, rh, hgain, pg, m)
+    put(m, m_o, 6)
+    tick(4, 2)
+    finish(3)
+    out_product()
+    tick(4, 3)
+    for k in range(NP // 2):
+        middle(k)
+    tick(5, 1)
+    for k in range(NP // 2, NP):
+        middle(k)
+    put(xv, mid_o, 7)
+    put(n2, n2_o, 8)
+    tick(5, 2)
+    finish(4)
+    times(n2, w_mg, gate, NF)
+    put(gate, gate_o, 9)
+    tick(5, 3)
+    tick(6, 1)
+    finish(5)
+    times(n2, w_mu, up, NF, activate)
+    put(up, up_o, 10)
+    put(act, act_o, 11)
+    tick(6, 2)
+    down_grad(0, NC // 2)
+    tick(6, 3)
+    down_grad(NC // 2, NC)
+    last()
+    finish(6)
+    gd_copy(NC - 2, NC % 2).wait()
+    gd_copy(NC - 1, (NC - 1) % 2).wait()
+    for k in range(NP):
+        pn_copy(k).wait_send()
+    for cp in done:
+        cp.wait()
+
+
+def front_all(Z, seqs, length, shards, x, cot, gain1, gain2, low, hgain, link, ids, cid=0, ahead=2):
+    nw = len(shards)
+    n, width = x.shape
+    C, F = shards[0].shape[1], shards[4].shape[1]
     dma = pltpu.SemaphoreType.DMA
-    f = jnp.float32
-    return [pltpu.VMEM((8, C), f), pltpu.VMEM((Z, 8, C), f), pltpu.VMEM((n // 128, 128), f), pltpu.VMEM((n // 128, 128), f),
-            dma((Z - 1,)), dma((Z,)), dma((1,)), dma((1,))]
-
-
-def mixer_forward(Z, seqs, length, width, pi, pf, pg, lower, gain, link, ids, cid=2):
-    n, C = pi.shape
-    f = jnp.float32
+    bf, f = jnp.bfloat16, jnp.float32
     sh = jax.ShapeDtypeStruct
-    vm = pl.BlockSpec(memory_space=pltpu.VMEM)
-    return pl.pallas_call(
-        functools.partial(mixer_forward_body, Z, seqs, length, width),
-        out_shape=[sh((n, C), f), sh((n, C), jnp.bfloat16), sh((n, 1), f), sh((seqs, C), f)],
-        in_specs=[vm] * 7, out_specs=[vm] * 4,
-        scratch_shapes=[pltpu.VMEM((n, C), f)] + mixer_scratch(Z, n, C),
-        compiler_params=pltpu.CompilerParams(collective_id=cid, has_side_effects=True),
-        name="mixer_forward",
-    )(pi, pf, pg, lower, gain, link, ids)
+    anyw, vmem = pl.BlockSpec(memory_space=pl.ANY), pl.BlockSpec(memory_space=pltpu.VMEM)
+    NP = n // TR
+    V = pltpu.VMEM
+    out_shape = ([sh((a.shape[0] * 4 * Z, a.shape[1]), bf) for a in shards]
+                 + [sh((n, width), bf)] + [sh((n, C), f)] * 4 + [sh((n, C), bf)] + [sh((n, width), f), sh((n, width), bf)]
+                 + [sh((n, F), f)] * 2 + [sh((n, F), bf), sh((n, width), bf), sh((width, F), bf), sh((n, 1), f), sh((seqs, C), f)])
+    scratch = [
+        V((n, width), f), V((n, width), bf), V((n, width), bf), V((n, C), f), V((n, C), f), V((n, C), f), V((n, C), f), V((n, C), f),
+        V((n, C), bf), V((2, width, TC), bf), V((2, TC, C), bf), V((n, width), bf), V((n, width), bf), V((n, F), f), V((n, F), f),
+        V((n, F), bf), V((n, width), bf), V((2, TC, F), bf), V((2, TR, width), f),
+        V((8, C), f), V((Z, 8, C), f), V((n // 128, 128), f), V((n // 128, 128), f),
+        dma((Z - 1,)), dma((Z,)), dma((1,)), dma((1,)), dma((NP,)), dma((NP,)), dma((2,)), dma((12,)), dma((2,)), dma((2,)), dma((1,)),
+        dma((nw, Z - 1)), dma((nw, Z - 1)), dma((nw, Z - 1)), dma((nw, Z - 1)),
+        dma((nw, 2 * Z - 1)), dma((nw, 2 * Z - 1)),
+        dma((nw, 4 * Z - 2)), dma((nw, 4 * Z - 2)), dma((nw,)), dma((nw,)), dma((nw,)),
+    ]
+    res = pl.pallas_call(
+        functools.partial(front_body, Z, seqs, length, ahead),
+        out_shape=out_shape,
+        in_specs=[vmem] * nw + [anyw] * 2 + [vmem] * 6,
+        out_specs=[anyw] * (len(out_shape) - 2) + [vmem] * 2,
+        scratch_shapes=scratch,
+        compiler_params=pltpu.CompilerParams(collective_id=cid, has_side_effects=True, vmem_limit_bytes=66_000_000),
+        name="forward",
+    )(*shards, x, cot, gain1, gain2, low, hgain, link, ids)
+    return res[:nw], res[nw:]
 
 
 TR = 64
@@ -1376,46 +1537,48 @@
     shards = [
         w.astype(bfloat) for w in (w_input, w_forget, w_gate, w_out, w_mlp_gate, w_mlp_up, w_down)
     ]
+    segs = segment_ids.astype(f32)
+    residual_in = block_input.reshape(rows_all, width)
+    upstream = cotangent.reshape(rows_all, width)
+    channels = lower.shape[0]
     if small:
-        wide = gather_all(shards, 4, Z)
+        link = jnp.concatenate(
+            [jnp.ones((seqs, 1), f32), jnp.where(segs[:, 1:] == segs[:, :-1], 1.0, 0.0)], axis=1
+        ).reshape(rows_all, 1)
+        ids = jnp.broadcast_to(
+            jnp.concatenate([segs[:, 0], segs[:, -1]])[:, None], (2 * seqs, channels)
+        )
+        low_row, gain_row = lower[None, :], hidden_gain[None, :]
+        gain_one, gain_two = norm_gain[None, :], mlp_gain[None, :]
+        wide, kept = front_all(
+            Z, seqs, length, shards, residual_in, upstream, gain_one, gain_two, low_row, gain_row, link, ids
+        )
+        (normed_one, pi, pf, pg, h, mixed_in, middle, normed_two, gate_pre, up_pre, activated, upstream_low,
+         grad_down, rh, start) = kept
+        wide_input, wide_forget, wide_gate, wide_out, wide_mgate, wide_mup, wide_down = wide
+        silu_mlp = jax.nn.silu(gate_pre)
     else:
         wide = [lax.all_gather(w, ("shard", "ctx"), axis=0, tiled=True) for w in shards]
-    wide_input, wide_forget, wide_gate, wide_out, wide_mgate, wide_mup, wide_down = wide
-    segs = segment_ids.astype(f32)
-    link = jnp.concatenate(
-        [jnp.ones((seqs, 1), f32), jnp.where(segs[:, 1:] == segs[:, :-1], 1.0, 0.0)], axis=1
-    ).reshape(rows_all, 1)
-    residual_in = block_input.reshape(rows_all, width)
-    scale_one = inverse_rms(residual_in)
-    normed_one = (residual_in * scale_one * norm_gain).astype(bfloat)
-    pi = jnp.dot(normed_one, wide_input, preferred_element_type=f32)
-    pf = jnp.dot(normed_one, wide_forget, preferred_element_type=f32)
-    pg = jnp.dot(normed_one, wide_gate, preferred_element_type=f32)
-    channels = pi.shape[1]
-    ids = jnp.broadcast_to(
-        jnp.concatenate([segs[:, 0], segs[:, -1]])[:, None], (2 * seqs, channels)
-    )
-    low_row, gain_row = lower[None, :], hidden_gain[None, :]
-    if small:
-        h, mixed_in, rh, start = mixer_forward(
-            Z, seqs, length, width, pi, pf, pg, low_row, gain_row, link, ids
-        )
-    else:
+        wide_input, wide_forget, wide_gate, wide_out, wide_mgate, wide_mup, wide_down = wide
+        scale_one = inverse_rms(residual_in)
+        normed_one = (residual_in * scale_one * norm_gain).astype(bfloat)
+        pi = jnp.dot(normed_one, wide_input, preferred_element_type=f32)
+        pf = jnp.dot(normed_one, wide_forget, preferred_element_type=f32)
+        pg = jnp.dot(normed_one, wide_gate, preferred_element_type=f32)
         h, mixed_in, rh, start = mixer_forward_plain(
             seqs, length, width, pi, pf, pg, lower, hidden_gain, segs
         )
-    mixer_out = lax.psum(times_back(mixed_in, wide_out).astype(bfloat), "tp").astype(f32)
-    middle = residual_in + mixer_out
-    scale_two = inverse_rms(middle)
-    normed_two = (middle * scale_two * mlp_gain).astype(bfloat)
-    gate_pre = jnp.dot(normed_two, wide_mgate, preferred_element_type=f32)
-    up_pre = jnp.dot(normed_two, wide_mup, preferred_element_type=f32)
-    silu_mlp = jax.nn.silu(gate_pre)
-    activated = (silu_mlp * up_pre).astype(bfloat)
-    upstream = cotangent.reshape(rows_all, width)
-    upstream_low = upstream.astype(bfloat)
+        mixer_out = lax.psum(times_back(mixed_in, wide_out).astype(bfloat), "tp").astype(f32)
+        middle = residual_in + mixer_out
+        scale_two = inverse_rms(middle)
+        normed_two = (middle * scale_two * mlp_gain).astype(bfloat)
+        gate_pre = jnp.dot(normed_two, wide_mgate, preferred_element_type=f32)
+        up_pre = jnp.dot(normed_two, wide_mup, preferred_element_type=f32)
+        silu_mlp = jax.nn.silu(gate_pre)
+        activated = (silu_mlp * up_pre).astype(bfloat)
+        upstream_low = upstream.astype(bfloat)
+        grad_down = outer_sum(upstream_low, activated).astype(bfloat)
     grad_activ = jnp.dot(upstream_low, wide_down, preferred_element_type=f32)
-    grad_down = outer_sum(upstream_low, activated).astype(bfloat)
     grad_gate_pre = (grad_activ * up_pre * silu_slope(gate_pre)).astype(bfloat)
     grad_up_pre = (grad_activ * silu_mlp).astype(bfloat)
     grad_mgate = outer_sum(normed_two, grad_gate_pre).astype(bfloat)
@@ -1426,7 +1589,7 @@
         output, grad_resid, vectors, sums = back_all(
             Z, seqs, length, grad_down, grad_mgate, grad_mup, normed_part, down_part, residual_in, middle, upstream,
             normed_one, mixed_in, wide_out, wide_input, wide_forget, wide_gate, pi, pf, pg, h,
-            rh, start, ids, link, norm_gain[None, :], mlp_gain[None, :], low_row, gain_row
+            rh, start, ids, link, gain_one, gain_two, low_row, gain_row
         )
         grad_norm_gain, grad_mlp_gain = vectors[0], vectors[1]
         grad_hidden_gain, grad_lower = vectors[2, :channels], vectors[3, :channels]

time: 897 us -> 752 us (0.84)
  waiting for transfers between devices: 62.1 us -> 0 us
  matrix products: 111 us -> 63 us
  Pallas kernels: 662 us -> 647 us
  between operations: 14.7 us -> 1.22 us
    psum x1 -> x0, waiting for transfers between devices: 62.1 us -> none  [on_device(): lax.psum(times_back(mixed_in, wide_out).astype(bfloat), 'tp').astype(f32)]
    dot_general x5 -> x0, matrix products: 31.1 us -> none  [the longest x1 9.71 us: on_device(): up_pre = jnp.dot(normed_two, wide_mup, preferred_element_type=f32)]
    pallas_call x1, Pallas kernels: 366 us -> 356 us  [back_all(): pl.pallas_call(functools.partial(back_body, Z, seqs, length), out_shape=o...]
    dot_general x3 -> x2, matrix products: 27.3 us -> 18.2 us  [outer_sum(): lax.dot_general(left_mat, right_mat, (((0,), (0,)), ((), ())), preferred_...]
    dot_general x4 -> x3, matrix products: 37.6 us -> 30.6 us  [times_back(): lax.dot_general(left_mat, right_mat, (((1,), (1,)), ((), ())), preferred_...]
    pallas_call x2 -> x1, Pallas kernels: 296 us -> 291 us  [front_all(): pl.pallas_call(functools.partial(front_body, Z, seqs, length, ahead), out...]
  transfers between devices with their start and end apart: 1 -> 0, of which waited for: 1 -> 0; matrix products, arithmetic and copies ran while one was open for 0% -> 0% of each run, Pallas kernels for 0% -> 0%
where the time goes in v4:
time: 752 us; the launch traced here: 740 us
  Pallas kernels  647 us (86%)
  matrix products  63 us (8%)
  local copies, waits for them, and re-layouts  18.3 us (2%)
  other arithmetic  11 us (1%)
    pallas_call x1, Pallas kernels, back_all(): pl.pallas_call(functools.partial(back_body, Z, seqs, length), out_shape=o...  356 us
    pallas_call x1, Pallas kernels, front_all(): pl.pallas_call(functools.partial(front_body, Z, seqs, length, ahead), out...  291 us
    dot_general x3, matrix products, times_back(): lax.dot_general(left_mat, right_mat, (((1,), (1,)), ((), ())), preferred_...  30.6 us
    dot_general x2, matrix products, outer_sum(): lax.dot_general(left_mat, right_mat, (((0,), (0,)), ((), ())), preferred_...  18.2 us

profile of v4, /device:TPU:0, one launch (start us, length us, event | category | flops | bytes accessed | tf_op | source)
XLA Modules:
  0.0 740.2 jit_solution(17132614152235810141)
XLA Ops:
  0.6 0.0 copy-start.2
  0.7 0.0 copy-start.1
  0.7 0.8 convert_element_type.49
  1.5 0.2 slice_reduce_fusion.1
  1.7 0.1 compare_select_fusion
  1.8 0.1 pad_bitcast_fusion
  1.8 0.1 pad_maximum_fusion
  1.9 0.7 broadcast_in_dim.32.refs_14_.refs_20_
  2.6 0.8 copy.30
  3.4 1.9 convert_element_type.42.refs_0_
  5.3 1.8 convert_element_type.43.refs_1_
  7.1 1.8 convert_element_type.44.refs_2_
  8.9 1.8 convert_element_type.45.refs_3_
  10.7 0.0 copy-done.1
  10.7 0.9 convert_element_type.46.refs_4_
  11.6 0.0 copy-done.2
  11.6 0.9 convert_element_type.47.refs_5_
  12.5 0.0 copy-done.3
  12.5 0.9 convert_element_type.48.refs_6_
  13.5 291.1 %forward.1 = (bf16[2048,1024]{1,0:T(8,128)(2,1)}, bf16[2048,1024]{1,0:T(8,128)(2,1)}, bf16[2048,1024]{1,0:T(8,128)(2,1)}, bf16[2048,1024]{1,0:T(8,128)(2,1)}, bf...) custom-call(bf16[128,1024]{1,0:T(8,128)(2,1)} %convert_element_type., ...), custom_call_target="tpu_custom_call" | custom-call | tf_op jit(solution)/shard_map/forward/pallas_call | solution.py:952
  304.6 0.0 copy-start.11
  304.6 0.0 copy-start.13
  304.6 11.0 %convolution_convert_fusion.2.refs_4_ = bf16[512,2048]{1,0:T(8,128)(2,1)} fusion(bf16[512,2816]{1,0:T(8,128)(2,1)} %get-tuple-element.53, bf16[2048,2816]{1,0:T(8,128)(2,1)} %get-tuple-element.48), kind=kOutput, calls=%fused_computation.6 | convolution fusion | flops 5906628608 | bytes 16515072 | tf_op jit(solution)/shard_map/dot_general | solution.py:1413
  315.6 0.0 copy-done.11
  315.6 0.0 copy-done.13
  315.6 0.0 slice-start.1
  315.6 14.2 %multiply_convert_fusion = (bf16[512,2816]{1,0:T(8,128)(2,1)}, bf16[512,2816]{1,0:T(8,128)(2,1)S(1)}) fusion(f32[512,2816]{1,0:T(8,128)S(1)} %copy-done.11, f32[512,2816]{1,0:T(8,128)} %get-tuple-element.49, bf16[512,2048]{1,0:T(8,128)(2,1)S(1)} %copy-done.13, bf16[2048,2816]{1,0:T(8,128)(2,1)} %get-tuple-element.48), kind=kOutput, calls=%fused_computation.2 | convolution fusion | flops 5924323328 | bytes 30932992 | tf_op jit(solution)/shard_map/dot_general | solution.py:1581
  329.8 10.5 %fusion.2 = f32[512,2048]{1,0:T(8,128)} fusion(bf16[512,2816]{1,0:T(8,128)(2,1)S(1)} %get-tuple-element.80, bf16[2048,2816]{1,0:T(8,128)(2,1)} %get-tuple-element.51), kind=kOutput, calls=%fused_computation.14 | convolution fusion | flops 5905580032 | bytes 18612224 | tf_op jit(solution)/shard_map/dot_general | solution.py:1413
  340.3 0.0 slice-done.2
  340.3 9.1 %add_convert_fusion.refs_3_ = bf16[512,2048]{1,0:T(8,128)(2,1)} fusion(f32[512,2048]{1,0:T(8,128)} %fusion.2, bf16[512,2816]{1,0:T(8,128)(2,1)S(1)} %copy-done.14, bf16[2048,2816]{1,0:T(8,128)(2,1)S(1)} %bitcast.51), kind=kOutput, calls=%fused_computation.5 | convolution fusion | flops 5907677184 | bytes 20709376 | tf_op jit(solution)/shard_map/dot_general | solution.py:1413
  349.4 0.0 copy-done.12
  349.4 9.0 %convolution_convert_fusion.refs_2_ = bf16[2048,2816]{1,0:T(8,128)(2,1)} fusion(bf16[512,2048]{1,0:T(8,128)(2,1)S(1)} %copy-done.12, bf16[512,2816]{1,0:T(8,128)(2,1)S(1)} %copy-done.14), kind=kOutput, calls=%fused_computation | convolution fusion | flops 5911347200 | bytes 16515072 | tf_op jit(solution)/shard_map/dot_general | solution.py:1419
  358.4 9.2 %convolution_convert_fusion.1.refs_1_ = bf16[2048,2816]{1,0:T(8,128)(2,1)} fusion(bf16[512,2048]{1,0:T(8,128)(2,1)S(1)} %copy-done.12, bf16[512,2816]{1,0:T(8,128)(2,1)S(1)} %get-tuple-element.80), kind=kOutput, calls=%fused_computation.1 | convolution fusion | flops 5911347200 | bytes 16515072 | tf_op jit(solution)/shard_map/dot_general | solution.py:1419
  367.7 355.6 %backward.1 = (f32[512,2048]{1,0:T(8,128)}, f32[512,2048]{1,0:T(8,128)}, f32[8,2048]{1,0:T(8,128)}, f32[128,2816]{1,0:T(8,128)}, f32[128,2816]{1,0:T(8,128)}, /*...) custom-call(bf16[2048,2816]{1,0:T(8,128)(2,1)} %get-tuple-element.45, ...), custom_call_target="tpu_custom_call" | custom-call | tf_op jit(solution)/shard_map/backward/pallas_call | solution.py:1369
  723.3 1.4 fusion.1
  724.7 1.5 fusion
  726.3 4.8 copy.40
  731.1 0.0 copy-start.7
  731.1 2.1 copy.41
  733.3 0.8 copy.42
  734.1 0.0 copy-done.9
  734.1 0.8 copy.43
  734.9 0.8 copy.44
  735.6 0.0 copy-done.7
  735.7 0.8 copy.45
  736.4 1.1 copy.46
  737.6 1.1 copy.47
  738.7 1.1 copy.48
  (23 shorter events, 0.0 us)
Async XLA Ops:
  0.6 11.0 %copy-start.2 = (f32[128,2816]{1,0:T(8,128)S(1)}, f32[128,2816]{1,0:T(8,128)}, u32[]{:S(2)}) copy-start(f32[128,2816]{1,0:T(8,128)} %param.25) | copy-start | bytes 4325380
  0.7 10.0 %copy-start.1 = (f32[128,2816]{1,0:T(8,128)S(1)}, f32[128,2816]{1,0:T(8,128)}, u32[]{:S(2)}) copy-start(f32[128,2816]{1,0:T(8,128)} %param.24) | copy-start | bytes 4325380
  3.4 9.1 %copy-start.3 = (f32[128,2816]{1,0:T(8,128)S(1)}, f32[128,2816]{1,0:T(8,128)}, u32[]{:S(2)}) copy-start(f32[128,2816]{1,0:T(8,128)} %param.26) | copy-start | bytes 4325380
  304.6 11.0 %copy-start.11 = (f32[512,2816]{1,0:T(8,128)S(1)}, f32[512,2816]{1,0:T(8,128)}, u32[]{:S(2)}) copy-start(f32[512,2816]{1,0:T(8,128)} %get-tuple-element.50) | copy-start | bytes 17301508
  304.6 11.0 %copy-start.13 = (bf16[512,2048]{1,0:T(8,128)(2,1)S(1)}, bf16[512,2048]{1,0:T(8,128)(2,1)}, u32[]{:S(2)}) copy-start(bf16[512,2048]{1,0:T(8,128)(2,1)} %get-tuple-element.47) | copy-start | bytes 6291460
  315.6 24.6 %slice-start = ((s8[11534336]{0:T(1024)(128)(4,1)}), s8[4194304]{0:T(1024)(128)(4,1)S(1)}, s32[]{:S(2)}) async-start(s8[11534336]{0:T(1024)(128)(4,1)} %bitcast.50), calls=%async_computation | async-start | bytes 8388608
  315.6 24.6 %slice-start.1 = ((s8[11534336]{0:T(1024)(128)(4,1)}), s8[3145728]{0:T(1024)(128)(4,1)S(1)}, s32[]{:S(2)}) async-start(s8[11534336]{0:T(1024)(128)(4,1)} %bitcast.50), calls=%async_computation.1 | async-start | bytes 6291456
  329.8 10.5 %slice-start.2 = ((s8[11534336]{0:T(1024)(128)(4,1)}), s8[4194304]{0:T(1024)(128)(4,1)S(1)}, s32[]{:S(2)}) async-start(s8[11534336]{0:T(1024)(128)(4,1)} %bitcast.50), calls=%async_computation.2 | async-start | bytes 8388608
  329.8 10.5 %copy-start.14 = (bf16[512,2816]{1,0:T(8,128)(2,1)S(1)}, bf16[512,2816]{1,0:T(8,128)(2,1)}, u32[]{:S(2)}) copy-start(bf16[512,2816]{1,0:T(8,128)(2,1)} %get-tuple-element.79) | copy-start | bytes 8650756
  340.3 9.1 %copy-start.12 = (bf16[512,2048]{1,0:T(8,128)(2,1)S(1)}, bf16[512,2048]{1,0:T(8,128)(2,1)}, u32[]{:S(2)}) copy-start(bf16[512,2048]{1,0:T(8,128)(2,1)} %get-tuple-element.46) | copy-start | bytes 6291460
  726.3 4.9 copy-start
  731.1 2.1 copy-start.10
  731.1 2.9 copy-start.9
  731.1 3.7 copy-start.8
  731.1 4.5 copy-start.7
  733.3 3.2 copy-start.6
  733.3 4.3 copy-start.5
  734.9 3.8 copy-start.4

commit v5 on v4

--- a/solution.py
+++ b/solution.py
@@ -708,7 +708,7 @@
 
 def front_body(Z, seqs, length, ahead, *refs):
     nw = 7
-    own = refs[:nw]
+    wide_own = refs[:nw]
     x, cot, gain1, gain2, low, hgain, link, ids = refs[nw:nw + 8]
     k0 = nw + 8
     wide = refs[k0:k0 + nw]
@@ -716,10 +716,11 @@
     n1_o, pi_o, pf_o, pg_o, h_o, m_o, mid_o, n2_o, gate_o, up_o, act_o, gy_o, gd_o, rh, start = refs[k0:k0 + 15]
     k0 += 15
     (xv, n1, n2, pi, pf, pg, h, cum, m, wbuf, wob, pn, rn, gate, up, act, gy, stg, e_f,
-     pay, box, row, got) = refs[k0:k0 + 23]
-    k0 += 23
-    s_c, r_c, s_t, r_t, n_s, n_r, w_s, o_s, e_s, g_s, x_s = refs[k0:k0 + 11]
-    sems = refs[k0 + 11:]
+     pay, box, row, got, wst) = refs[k0:k0 + 24]
+    own = refs[k0 + 24:k0 + 24 + nw]
+    k0 += 24 + nw
+    s_c, r_c, s_t, r_t, n_s, n_r, w_s, o_s, e_s, g_s, x_s, f_s = refs[k0:k0 + 12]
+    sems = refs[k0 + 12:]
     w_in, w_f, w_g, w_out, w_mg, w_mu, w_dn = wide
     n, width = x.shape
     C, F = pi.shape[1], gate.shape[1]
@@ -729,12 +730,31 @@
     begin, tick, last, finish = gather_steps(nw, Z, ahead, True, own, wide, sems)
     NP, NF, NW, NC = n // TR, F // TC, C // TC, width // TC
 
+    def own_load(w):
+        return pltpu.make_async_copy(wide_own[w], wst.at[w % 2, :, pl.ds(0, own[w].shape[1])], f_s.at[w % 2])
+
+    def own_low(w):
+        own_load(w).wait()
+        cols = own[w].shape[1]
+
+        def go(i, _):
+            r = pl.ds(pl.multiple_of(i * 16, 16), 16)
+            own[w][r, :] = wst[w % 2, r, :cols].astype(jnp.bfloat16)
+            return 0
+
+        lax.fori_loop(0, own[w].shape[0] // 16, go, 0)
+        if w + 2 < nw:
+            own_load(w + 2).start()
+
+    own_load(0).start()
+    own_load(1).start()
     barrier = pltpu.get_barrier_semaphore()
     for d in [{"shard": (1 - q) * 2 + c}, {"shard": q * 2 + (1 - c)}, OTHER] + [{"ctx": lax.rem(z + o, Z)} for o in range(1, Z)]:
         pl.semaphore_signal(barrier, inc=1, device_id=d, device_id_type=MESH)
     pl.semaphore_wait(barrier, 2 + Z)
 
     for w in range(ahead):
+        own_low(w)
         begin(w)
     load_x = pltpu.make_async_copy(x, xv, x_s.at[0])
     load_x.start()
@@ -858,7 +878,10 @@
 
         lax.fori_loop(j0, j1, go, 0)
 
+    own_low(2)
     norm_in()
+    for w in range(3, nw):
+        own_low(w)
     for w, src, dst, o, k in ((0, w_in, pi, pi_o, 1), (1, w_f, pf, pf_o, 2), (2, w_g, pg, pg_o, 3)):
         if w == 0:
             tick(0, 1)
@@ -944,7 +967,9 @@
         V((n, C), bf), V((2, width, TC), bf), V((2, TC, C), bf), V((n, width), bf), V((n, width), bf), V((n, F), f), V((n, F), f),
         V((n, F), bf), V((n, width), bf), V((2, TC, F), bf), V((2, TR, width), f),
         V((8, C), f), V((Z, 8, C), f), V((n // 128, 128), f), V((n // 128, 128), f),
-        dma((Z - 1,)), dma((Z,)), dma((1,)), dma((1,)), dma((NP,)), dma((NP,)), dma((2,)), dma((12,)), dma((2,)), dma((2,)), dma((1,)),
+        V((2, shards[0].shape[0], F), f),
+    ] + [V(a.shape, bf) for a in shards] + [
+        dma((Z - 1,)), dma((Z,)), dma((1,)), dma((1,)), dma((NP,)), dma((NP,)), dma((2,)), dma((12,)), dma((2,)), dma((2,)), dma((1,)), dma((2,)),
         dma((nw, Z - 1)), dma((nw, Z - 1)), dma((nw, Z - 1)), dma((nw, Z - 1)),
         dma((nw, 2 * Z - 1)), dma((nw, 2 * Z - 1)),
         dma((nw, 4 * Z - 2)), dma((nw, 4 * Z - 2)), dma((nw,)), dma((nw,)), dma((nw,)),
@@ -952,7 +977,7 @@
     res = pl.pallas_call(
         functools.partial(front_body, Z, seqs, length, ahead),
         out_shape=out_shape,
-        in_specs=[vmem] * nw + [anyw] * 2 + [vmem] * 6,
+        in_specs=[anyw] * (nw + 2) + [vmem] * 6,
         out_specs=[anyw] * (len(out_shape) - 2) + [vmem] * 2,
         scratch_shapes=scratch,
         compiler_params=pltpu.CompilerParams(collective_id=cid, has_side_effects=True, vmem_limit_bytes=66_000_000),
@@ -974,23 +999,24 @@
 
 
 def back_body(Z, seqs, length, *refs):
-    (gd, gg, gu, pn, po, x, mid, cot, n1, m, w_out, w_in, w_f, w_g, pi_h, pf_h, pg_h, h_h,
-     rh, start, ids, link, gain1, gain2, low, hgain) = refs[:26]
-    out, dx, vec_out = refs[26:29]
-    grads = refs[29:36]
-    mparts = refs[36:40]
-    rn, ro = refs[40:42]
-    k0 = 42
+    (gd, gy_h, n2_h, act_h, gate_h, up_h, w_dn, w_mg, w_mu, x, mid, cot, n1, m, w_out, w_in, w_f, w_g,
+     pi_h, pf_h, pg_h, h_h, rh, start, ids, link, gain1, gain2, low, hgain) = refs[:30]
+    dx, vec_out = refs[30:32]
+    grads = refs[32:39]
+    mparts = refs[39:45]
+    pn, po, rn, ro = refs[45:49]
+    k0 = 49
     rc, xr, zu, zd, hr = (refs[k0 + 7 * i:k0 + 7 * (i + 1)] for i in range(5))
     k0 += 35
-    (xs, zs, stage, stage_z, fin, dmid, gm, dm, h, pi, pf, pg, gl, tail, dpi, dpf, dpg, n1v, mv, wbuf, wbuf3, stg, sn, rn1,
-     e_f, e_b, vec, vgot, vbox, col, end, pay, box, row, got, acc) = refs[k0:k0 + 36]
-    k0 += 36
-    (l_h, l_n, w_s, g_s, n_s, n_r, o_s, o_r, t_s, t_r, e_s, eo_s, v_s, v_r, vz_s, vz_r, s_c, r_c, s_t, r_t) = refs[k0:k0 + 20]
-    sems = refs[k0 + 20:]
+    (xs, zs, stage, stage_z, fin, dmid, gm, dm, h, pi, pf, pg, gl, tail, dpi, dpf, dpg, n1v, mv, wbuf, tb, du, sn, rn1,
+     e_f, e_b, vec, vgot, vbox, col, end, pay, box, row, got) = refs[k0:k0 + 35]
+    k0 += 35
+    (l_h, l_n, w_s, g_s, n_s, n_r, o_s, o_r, t_s, t_r, e_s, eo_s, v_s, v_r, vz_s, vz_r, s_c, r_c, s_t, r_t, b_s) = refs[k0:k0 + 21]
+    sems = refs[k0 + 21:]
     n, width = x.shape
     C = dm.shape[1]
-    parts = (gd, gg, gu) + tuple(mparts)
+    F = du.shape[1]
+    parts = (gd,) + tuple(mparts)
     sc = Scatter(Z, parts, rc, xr, zu, zd, hr, grads, xs, zs, (stage, stage_z), fin, sems)
     z = sc.z
     t = lax.axis_index("tp")
@@ -1001,8 +1027,7 @@
         pl.semaphore_signal(barrier, inc=1, device_id=d, device_id_type=MESH)
     pl.semaphore_wait(barrier, 2 + Z)
 
-    for w in range(3):
-        sc.c_send(w)
+    sc.c_send(0)
 
     NP = n // TR
     NC = width // TC
@@ -1016,12 +1041,8 @@
     def po_copy(k):
         return remote(po.at[rows_of(k), :], ro.at[rows_of(k), :], o_s.at[k], o_r.at[k], OTHER)
 
-    for k in range(NP):
-        pn_copy(k).start()
-    for k in range(NP):
-        po_copy(k).start()
     early = [pltpu.make_async_copy(a, b, l_h.at[i]) for i, (a, b) in enumerate(
-        ((pi_h, pi), (pf_h, pf), (pg_h, pg), (h_h, h), (n1, n1v), (m, mv)))]
+        ((pi_h, pi), (pf_h, pf), (pg_h, pg), (h_h, h), (m, mv), (gy_h, n1v), (n2_h, gm), (mid, dmid)))]
     for cp in early:
         cp.start()
     vec[...] = jnp.zeros_like(vec)
@@ -1045,53 +1066,139 @@
 
     def p1_load(k):
         pn_copy(k).wait_recv()
-        for cp in piece(k, k % 2, (mid, cot), (pn, rn)):
+        for cp in piece(k, k % 2, (cot,), (pn, rn)):
             cp.start()
 
     def p1(k):
         s = k % 2
-        for cp in piece(k, s, (mid, cot), (pn, rn)):
+        for cp in piece(k, s, (cot,), (pn, rn)):
             cp.wait()
         g = gain2[...]
 
         def go(i, a):
             r = pl.ds(pl.multiple_of(i * 16, 16), 16)
-            v, ct = e_f[s, 0, r, :], e_f[s, 1, r, :]
+            rr = pl.ds(pl.multiple_of(k * TR + i * 16, 16), 16)
+            v, ct = dmid[rr, :], e_f[s, 0, r, :]
             d = e_b[s, 0, r, :].astype(jnp.float32) + e_b[s, 1, r, :].astype(jnp.float32)
             r2 = lax.rsqrt(jnp.mean(v * v, axis=1, keepdims=True) + epsilon)
             gdn = d * g
             inner = jnp.mean(gdn * v, axis=1, keepdims=True)
             o = ct + gdn * r2 - v * (r2 * r2 * r2 * inner)
-            rr = pl.ds(pl.multiple_of(k * TR + i * 16, 16), 16)
             dmid[rr, :] = o
             gm[rr, :] = o.astype(jnp.bfloat16)
             return a + jnp.sum(d * v * r2, axis=0, keepdims=True)
 
         vec[1:2, :] = vec[1:2, :] + lax.fori_loop(0, TR // 16, go, jnp.zeros((1, width), jnp.float32))
 
-    def po_load(k):
-        po_copy(k).wait_recv()
-        for cp in piece(k, k % 2, (mid,), (po, ro)):
-            if cp is not None:
-                cp.start()
-
-    def o_store(k):
-        return pltpu.make_async_copy(e_f.at[k % 2, 1], out.at[rows_of(k), :], eo_s.at[k % 2])
-
-    def p_out(k):
-        s = k % 2
-        for cp in piece(k, s, (mid,), (po, ro)):
-            cp.wait()
-        if k >= 2:
-            o_store(k - 2).wait()
-
-        def go(i, _):
-            r = pl.ds(pl.multiple_of(i * 16, 16), 16)
-            e_f[s, 1, r, :] = e_f[s, 0, r, :] + (e_b[s, 0, r, :].astype(jnp.float32) + e_b[s, 1, r, :].astype(jnp.float32))
+    segments = [(b, a, min(C, F - a)) for b, a in ((dpi, 0), (dpf, C), (dpg, 2 * C))]
+
+    def tile_of(j):
+        return pl.ds(pl.multiple_of(j * TC, TC), TC)
+
+    def glu_loads(j, s):
+        return [pltpu.make_async_copy(a.at[:, tile_of(j)], b, w_s.at[s, i]) for i, (a, b) in enumerate(
+            ((w_dn, wbuf.at[s]), (gate_h, gl.at[:, tile_of(s)]), (up_h, tail.at[:, tile_of(s)])))]
+
+    def glu_cols(g):
+        buf, first, size = segments[g]
+
+        def go(j, _):
+            s = lax.rem(j, 2)
+
+            @pl.when(j + 1 < F // TC)
+            def _():
+                for cp in glu_loads(j + 1, 1 - s):
+                    cp.start()
+
+            for cp in glu_loads(j, s):
+                cp.wait()
+            dm[:, :TC] = jnp.dot(n1v[...], wbuf[s], preferred_element_type=jnp.float32)
+            here, there = tile_of(s), tile_of(j)
+            inside = tile_of(j - first // TC)
+
+            def rows(i, _):
+                r = pl.ds(pl.multiple_of(i * 32, 32), 32)
+                v, u, d = gl[r, here], tail[r, here], dm[r, :TC]
+                sg = sigmoid(v)
+                buf[r, inside] = (d * u * (sg * (1.0 + v * (1.0 - sg)))).astype(jnp.bfloat16)
+                du[r, there] = (d * (v * sg)).astype(jnp.bfloat16)
+                return 0
+
+            lax.fori_loop(0, n // 32, rows, 0)
             return 0
 
-        lax.fori_loop(0, TR // 16, go, 0)
-        o_store(k).start()
+        lax.fori_loop(first // TC, (first + size) // TC, go, 0)
+
+    def w_rows(w, j, s):
+        return pltpu.make_async_copy(w.at[tile_of(j), :], tb.at[s, :, pl.ds(0, F)], w_s.at[2 + s, 0])
+
+    def sn_out(dst, j):
+        return pltpu.make_async_copy(sn.at[j], dst.at[:, tile_of(j)], b_s.at[j])
+
+    def normed(j0, j1):
+        def go(j, _):
+            w_rows(w_mg, j, 0).wait()
+            o = None
+            for buf, first, size in segments:
+                v = dot_t(buf[:, :size], tb[0, :, first:first + size])
+                o = v if o is None else o + v
+
+            @pl.when(j + 1 < NC)
+            def _():
+                w_rows(w_mg, j + 1, 0).start()
+
+            w_rows(w_mu, j, 1).wait()
+            o = o + dot_t(du[...], tb[1, :, :F])
+
+            @pl.when(j + 1 < NC)
+            def _():
+                w_rows(w_mu, j + 1, 1).start()
+
+            sn[j] = o.astype(jnp.bfloat16)
+            sn_out(pn, j).start()
+            return 0
+
+        lax.fori_loop(j0, j1, go, 0)
+
+    def t_copy(dst, j, s):
+        return pltpu.make_async_copy(tb.at[s, :, pl.ds(0, dst.shape[1])], dst.at[tile_of(j), :], g_s.at[s])
+
+    def glu_grad(w, cols, j0, j1):
+        dst = parts[w]
+
+        def go(j, _):
+            s = lax.rem(j, 2)
+
+            @pl.when(j >= 2)
+            def _():
+                t_copy(dst, j - 2, s).wait()
+
+            lhs = gm[:, tile_of(j)]
+            for buf, first, size in cols:
+                tb[s, :, first:first + size] = dot_o(lhs, buf[:, :size]).astype(jnp.bfloat16)
+            t_copy(dst, j, s).start()
+            return 0
+
+        lax.fori_loop(j0, j1, go, 0)
+        if j1 == NC:
+            t_copy(dst, NC - 2, NC % 2).wait()
+            t_copy(dst, NC - 1, (NC - 1) % 2).wait()
+            sc.c_send(w)
+
+    def down(j0, j1):
+        def go(j, _):
+            s = lax.rem(j, 2)
+
+            @pl.when(j + 1 < NC)
+            def _():
+                w_rows(w_dn, j + 1, 1 - s).start()
+
+            w_rows(w_dn, j, s).wait()
+            sn[j] = dot_t(du[...], tb[s, :, :F]).astype(jnp.bfloat16)
+            sn_out(po, j).start()
+            return 0
+
+        lax.fori_loop(j0, j1, go, 0)
 
     NW = C // TC
 
@@ -1114,35 +1221,36 @@
 
         lax.fori_loop(0, NW, go, 0)
 
-    def g_copy(dst, j, s):
-        return pltpu.make_async_copy(stg.at[s], dst.at[pl.ds(pl.multiple_of(j * TC, TC), TC), :], g_s.at[s])
-
     def p4(w, lhs, rhs):
-        dst = mparts[w - 3]
+        dst = parts[w]
 
         def go(j, _):
             s = lax.rem(j, 2)
 
             @pl.when(j >= 2)
             def _():
-                g_copy(dst, j - 2, s).wait()
-
-            stg[s] = dot_o(lhs[:, pl.ds(pl.multiple_of(j * TC, TC), TC)], rhs[...]).astype(jnp.bfloat16)
-            g_copy(dst, j, s).start()
+                t_copy(dst, j - 2, s).wait()
+
+            tb[s, :, :C] = dot_o(lhs[:, tile_of(j)], rhs[...]).astype(jnp.bfloat16)
+            t_copy(dst, j, s).start()
             return 0
 
         lax.fori_loop(0, NC, go, 0)
-        g_copy(dst, NC - 2, NC % 2).wait()
-        g_copy(dst, NC - 1, (NC - 1) % 2).wait()
+        t_copy(dst, NC - 2, NC % 2).wait()
+        t_copy(dst, NC - 1, (NC - 1) % 2).wait()
         sc.c_send(w)
 
+    def w3(j, s):
+        return [pltpu.make_async_copy(a.at[tile_of(j), :], tb.at[s, :, pl.ds(i * C, C)], w_s.at[2 + s, i])
+                for i, a in enumerate((w_in, w_f, w_g))]
+
     def w3_start(j, s):
-        for i, a in enumerate((w_in, w_f, w_g)):
-            pltpu.make_async_copy(a.at[pl.ds(pl.multiple_of(j * TC, TC), TC), :], wbuf3.at[s, i], w_s.at[2 + s, i]).start()
+        for cp in w3(j, s):
+            cp.start()
 
     def w3_wait(j, s):
-        for i, a in enumerate((w_in, w_f, w_g)):
-            pltpu.make_async_copy(a.at[pl.ds(pl.multiple_of(j * TC, TC), TC), :], wbuf3.at[s, i], w_s.at[2 + s, i]).wait()
+        for cp in w3(j, s):
+            cp.wait()
 
     def n_copy(j):
         return remote(sn.at[j], rn1.at[j], t_s.at[j], t_r.at[j], OTHER)
@@ -1156,7 +1264,7 @@
                 w3_start(j + 1, 1 - s)
 
             w3_wait(j, s)
-            o = dot_t(dpi[...], wbuf3[s, 0]) + dot_t(dpf[...], wbuf3[s, 1]) + dot_t(dpg[...], wbuf3[s, 2])
+            o = dot_t(dpi[...], tb[s, :, :C]) + dot_t(dpf[...], tb[s, :, C:2 * C]) + dot_t(dpg[...], tb[s, :, 2 * C:3 * C])
             sn[j] = o.astype(jnp.bfloat16)
             n_copy(j).start()
             return 0
@@ -1183,11 +1291,11 @@
             a, b = v * v, d * g * v
             a, b = a[:, :128] + a[:, 128:], b[:, :128] + b[:, 128:]
             if j == 0:
-                acc[0, r, :] = a
-                acc[1, r, :] = b
+                dm[r, :128] = a
+                dm[r, 128:256] = b
             else:
-                acc[0, r, :] = acc[0, r, :] + a
-                acc[1, r, :] = acc[1, r, :] + b
+                dm[r, :128] = dm[r, :128] + a
+                dm[r, 128:256] = dm[r, 128:256] + b
             return 0
 
         lax.fori_loop(0, n // 16, go, 0, unroll=2)
@@ -1195,10 +1303,10 @@
     def p6b():
         def go(i, _):
             r = pl.ds(pl.multiple_of(i * 16, 16), 16)
-            r1 = lax.rsqrt(jnp.sum(acc[0, r, :], axis=1, keepdims=True) / width + epsilon)
-            inner = jnp.sum(acc[1, r, :], axis=1, keepdims=True) / width
-            acc[0, r, :] = jnp.broadcast_to(r1, (16, 128))
-            acc[1, r, :] = jnp.broadcast_to(r1 * r1 * r1 * inner, (16, 128))
+            r1 = lax.rsqrt(jnp.sum(dm[r, :128], axis=1, keepdims=True) / width + epsilon)
+            inner = jnp.sum(dm[r, 128:256], axis=1, keepdims=True) / width
+            dm[r, :128] = jnp.broadcast_to(r1, (16, 128))
+            dm[r, 128:256] = jnp.broadcast_to(r1 * r1 * r1 * inner, (16, 128))
             return 0
 
         lax.fori_loop(0, n // 16, go, 0, unroll=2)
@@ -1222,8 +1330,8 @@
             r = pl.ds(pl.multiple_of(i * 16, 16), 16)
             v = tail[r, s * TC:(s + 1) * TC]
             d = sn[j, r, :].astype(jnp.float32) + rn1[j, r, :].astype(jnp.float32)
-            r1 = jnp.concatenate([acc[0, r, :], acc[0, r, :]], axis=1)
-            ri = jnp.concatenate([acc[1, r, :], acc[1, r, :]], axis=1)
+            r1 = jnp.concatenate([dm[r, :128], dm[r, :128]], axis=1)
+            ri = jnp.concatenate([dm[r, 128:256], dm[r, 128:256]], axis=1)
             gl[r, s * TC:(s + 1) * TC] = dmid[r, j * TC:(j + 1) * TC] + d * g * r1 - v * ri
             return total + jnp.sum(d * v * r1, axis=0, keepdims=True)
 
@@ -1233,21 +1341,63 @@
     x0, x1, x2, z0, z1, z2 = X(0), X(1), X(2), Zs(0), Zs(1), Zs(2)
     x3, x4, x5, x6 = X(3), X(4), X(5), X(6)
     z3, z4, z5, z6 = Zs(3), Zs(4), Zs(5), Zs(6)
-    tick(*x0, x1[0])
+    for cp in glu_loads(0, 0):
+        cp.start()
+    early[5].wait()
+    glu_cols(0)
+    tick(x0[0])
+    glu_cols(1)
+    tick(x0[1])
+    w_rows(w_mg, 0, 0).start()
+    w_rows(w_mu, 0, 1).start()
+    glu_cols(2)
+    tick(x0[2])
+    load_n1 = pltpu.make_async_copy(n1, n1v, l_h.at[5])
+    load_n1.start()
+    normed(0, NC // 2)
+    tick(x0[3], z0[0])
+    normed(NC // 2, NC)
+    for j in range(NC):
+        sn_out(pn, j).wait()
+    for k in range(NP):
+        pn_copy(k).start()
+    tick(z0[1])
+    early[6].wait()
+    glu_grad(1, segments, 0, NC // 2)
+    tick(z0[2])
+    glu_grad(1, segments, NC // 2, NC)
+    tick(z0[3])
+    glu_grad(2, [(du, 0, F)], 0, NC // 2)
+    tick(x1[0])
+    glu_grad(2, [(du, 0, F)], NC // 2, NC)
+    load_act = pltpu.make_async_copy(act_h, du, l_h.at[6])
+    load_act.start()
+    w_rows(w_dn, 0, 0).start()
+    tick(x1[1])
+    load_act.wait()
+    down(0, NC // 2)
+    tick(x1[2])
+    down(NC // 2, NC)
+    for j in range(NC):
+        sn_out(po, j).wait()
+    for k in range(NP):
+        po_copy(k).start()
     p1_load(0)
-    tick(x1[1])
-    between = [[z0[0], x1[2]], [x1[3]], [z0[1]], [], [z0[2], x2[0]], [], [z0[3], x2[1]], [x2[2]]]
+    tick(x1[3], z1[0])
+    early[7].wait()
+    between = [[z1[1]], [x2[0]], [x2[1]], [z1[2]], [x2[2]], [], [z1[3]], [x2[3]]]
     for k in range(NP):
         if k + 1 < NP:
             p1_load(k + 1)
         p1(k)
         tick(*(between[k] if k < len(between) else []))
     p2()
-    tick(x2[3], z1[0])
-    for cp in early:
+    tick(z2[0])
+    for cp in early[:5]:
         cp.wait()
+    load_n1.wait()
     p4(3, gm, mv)
-    tick(z1[1])
+    tick(z2[1])
     backward_first(n, dm, h, pg, hgain, rh, dpg, col, acc_row(vec, 2, C))
     column_to_rows(col, row, n)
     swap = remote(row, got, s_t.at[0], r_t.at[0], OTHER)
@@ -1258,37 +1408,29 @@
     ends = []
     for sq in range(seqs):
         ends.append(backward_scan_one(sq, length, dm, h, pf, pg, low, hgain, link, rh, col, gl, tail))
-        tick(z1[2 + sq] if sq < 2 else (lambda: None))
+        if sq == 0:
+            tick(z2[2])
     pay[4:8, :] = ids[...]
     for sq in range(seqs):
         pay[sq:sq + 1, :] = ends[sq][1]
         pay[2 + sq:3 + sq, :] = ends[sq][0]
     cps = spread(Z, z, pay, box, s_c, r_c)
-    tick(x3[2], x3[3])
+    tick(x3[2], x3[3], z2[3])
     spread_wait(Z, z, pay, box, s_c, r_c, cps)
     end[...] = suffix_state(Z, z, box)
     backward_last(seqs, length, gl, tail, end, h, start, pi, pf, low, link, dpi, dpf, acc_row(vec, 3, C))
-    tick(z2[0])
+    tick(z3[0])
+    p4(4, n1v, dpi)
+    tick(z3[1], x4[0], x4[1])
+    p4(5, n1v, dpf)
+    tick(x4[2], x4[3], z3[2])
+    p4(6, n1v, dpg)
     w3_start(0, 0)
-    p4(4, n1v, dpi)
-    tick(x4[0], x4[1], z2[1])
-    p4(5, n1v, dpf)
-    tick(x4[2], x4[3], z2[2])
-    p4(6, n1v, dpg)
-    tick(z2[3], x5[0], x5[1])
+    tick(z3[3], x5[0], x5[1])
     p5(0, NC // 2)
-    tick(x5[2], x5[3], z3[0], z3[1])
+    tick(x5[2], x5[3], z4[0], z4[1])
     p5(NC // 2, NC)
-    tick(z3[2], z3[3], *x6)
-    po_load(0)
-    outs = [[z4[0]], [], [z4[1]], [], [z4[2]], [], [z4[3]], []]
-    for k in range(NP):
-        if k + 1 < NP:
-            po_load(k + 1)
-        p_out(k)
-        tick(*(outs[k] if k < len(outs) else []))
-    for k in (NP - 2, NP - 1):
-        o_store(k).wait()
+    tick(z4[2], z4[3], *x6)
     for j in range(NC):
         p6a(j)
         if j % 4 == 3 and j // 4 < 2:
@@ -1320,6 +1462,7 @@
     for k in range(NP):
         pn_copy(k).wait_send()
         po_copy(k).wait_send()
+        po_copy(k).wait_recv()
     for j in range(NC):
         n_copy(j).wait_send()
     for w in range(7):
@@ -1330,23 +1473,23 @@
     return vec.at[k:k + 1, pl.ds(0, C)]
 
 
-def back_all(Z, seqs, length, gd, gg, gu, pn, po, x, mid, cot, n1, m, w_out, w_in, w_f, w_g, pi, pf, pg, h,
-             rh, start, ids, link, gain1, gain2, low, hgain, cid=1):
+def back_all(Z, seqs, length, gd, gy, n2, act, gate, up, w_dn, w_mg, w_mu, x, mid, cot, n1, m, w_out, w_in, w_f, w_g,
+             pi, pf, pg, h, rh, start, ids, link, gain1, gain2, low, hgain, cid=1):
     n, width = x.shape
-    C = pi.shape[1]
+    C, F = pi.shape[1], gate.shape[1]
     dma = pltpu.SemaphoreType.DMA
     bf, f = jnp.bfloat16, jnp.float32
     sh = jax.ShapeDtypeStruct
     anyw, vmem = pl.BlockSpec(memory_space=pl.ANY), pl.BlockSpec(memory_space=pltpu.VMEM)
-    shapes = [gd.shape, gg.shape, gu.shape] + [(width, C)] * 4
+    shapes = [(width, F)] * 3 + [(width, C)] * 4
     R = [s[0] // (4 * Z) for s in shapes]
     N = [s[1] for s in shapes]
     Rm, Nm = max(R), max(N)
     NP, NC = n // TR, width // TC
-    out_shape = ([sh((n, width), f), sh((n, width), f), sh((8, width), f)]
+    out_shape = ([sh((n, width), f), sh((8, width), f)]
                  + [sh((r, k), f) for r, k in zip(R, N)]
-                 + [sh((width, C), bf)] * 4
-                 + [sh((n, width), bf)] * 2
+                 + [sh((width, F), bf)] * 2 + [sh((width, C), bf)] * 4
+                 + [sh((n, width), bf)] * 4
                  + [sh((2 * Z * r, k), bf) for r, k in zip(R, N)]
                  + [sh((Z * r, k), bf) for r, k in zip(R, N)]
                  + [sh((Z * r, k), bf) for r, k in zip(R, N)]
@@ -1357,25 +1500,26 @@
         V((2, Z, Rm, Nm), bf), V((2, Z - 1, Rm, Nm), bf), V((2, 3, Rm, Nm), bf), V((5, Rm, Nm), bf), V((Rm, Nm), f),
         V((n, width), f), V((n, width), bf), V((n, C), f), V((n, C), f), V((n, C), f), V((n, C), f), V((n, C), f),
         V((n, C), f), V((n, C), f), V((n, C), bf), V((n, C), bf), V((n, C), bf), V((n, width), bf), V((n, C), bf),
-        V((2, width, TC), bf), V((2, 3, TC, C), bf), V((2, TC, C), bf), V((NC, n, TC), bf), V((NC, n, TC), bf),
-        V((2, 2, TR, width), f), V((2, 2, TR, width), bf), V((8, width), f), V((2, 8, width), f), V((Z, 8, width), f),
+        V((2, width, TC), bf), V((2, TC, 3 * C), bf), V((n, F), bf), V((NC, n, TC), bf), V((NC, n, TC), bf),
+        V((2, 1, TR, width), f), V((2, 2, TR, width), bf), V((8, width), f), V((2, 8, width), f), V((Z, 8, width), f),
         V((n, 1), f), V((seqs, C), f), V((8, C), f), V((Z, 8, C), f), V((n // 128, 128), f), V((n // 128, 128), f),
-        V((2, n, 128), f),
-        dma((6,)), dma((1,)), dma((4, 3)), dma((2,)), dma((NP,)), dma((NP,)), dma((NP,)), dma((NP,)), dma((NC,)), dma((NC,)),
+        dma((8,)), dma((1,)), dma((4, 3)), dma((2,)), dma((NP,)), dma((NP,)), dma((NP,)), dma((NP,)), dma((NC,)), dma((NC,)),
         dma((2, 4)), dma((2,)), dma((2,)), dma((2,)), dma((Z - 1,)), dma((Z,)), dma((Z - 1,)), dma((Z,)), dma((1,)), dma((1,)),
+        dma((NC,)),
         dma((7, 2)), dma((7, 2)), dma((7, Z)), dma((7, Z)), dma((7, Z - 1)), dma((7, Z)), dma((7, Z)),
         dma((7,)), dma((7,)), dma((3, 5)), dma((7,)),
     ]
     res = pl.pallas_call(
         functools.partial(back_body, Z, seqs, length),
         out_shape=out_shape,
-        in_specs=[anyw] * 18 + [vmem] * 8,
-        out_specs=[anyw, anyw, vmem] + [anyw] * (len(out_shape) - 3),
+        in_specs=[anyw] * 22 + [vmem] * 8,
+        out_specs=[anyw, vmem] + [anyw] * (len(out_shape) - 2),
         scratch_shapes=scratch,
         compiler_params=pltpu.CompilerParams(collective_id=cid, has_side_effects=True, vmem_limit_bytes=66_000_000),
         name="backward",
-    )(gd, gg, gu, pn, po, x, mid, cot, n1, m, w_out, w_in, w_f, w_g, pi, pf, pg, h, rh, start, ids, link, gain1, gain2, low, hgain)
-    return res[0], res[1], res[2], res[3:10]
+    )(gd, gy, n2, act, gate, up, w_dn, w_mg, w_mu, x, mid, cot, n1, m, w_out, w_in, w_f, w_g, pi, pf, pg, h,
+      rh, start, ids, link, gain1, gain2, low, hgain)
+    return res[0], res[1], res[2:9], res[16], res[18]
 
 
 def carried_in(x, axis, combine, identity, reverse):
@@ -1534,9 +1678,7 @@
     rows_all = seqs * length
     small = lax.axis_size("shard") == 4
     Z = lax.axis_size("ctx")
-    shards = [
-        w.astype(bfloat) for w in (w_input, w_forget, w_gate, w_out, w_mlp_gate, w_mlp_up, w_down)
-    ]
+    shards = [w_input, w_forget, w_gate, w_out, w_mlp_gate, w_mlp_up, w_down]
     segs = segment_ids.astype(f32)
     residual_in = block_input.reshape(rows_all, width)
     upstream = cotangent.reshape(rows_all, width)
@@ -1556,9 +1698,16 @@
         (normed_one, pi, pf, pg, h, mixed_in, middle, normed_two, gate_pre, up_pre, activated, upstream_low,
          grad_down, rh, start) = kept
         wide_input, wide_forget, wide_gate, wide_out, wide_mgate, wide_mup, wide_down = wide
-        silu_mlp = jax.nn.silu(gate_pre)
+        grad_resid, vectors, sums, down_mine, down_other = back_all(
+            Z, seqs, length, grad_down, upstream_low, normed_two, activated, gate_pre, up_pre, wide_down, wide_mgate,
+            wide_mup, residual_in, middle, upstream, normed_one, mixed_in, wide_out, wide_input, wide_forget, wide_gate,
+            pi, pf, pg, h, rh, start, ids, link, gain_one, gain_two, low_row, gain_row
+        )
+        output = middle + (down_mine.astype(f32) + down_other.astype(f32))
+        grad_norm_gain, grad_mlp_gain = vectors[0], vectors[1]
+        grad_hidden_gain, grad_lower = vectors[2, :channels], vectors[3, :channels]
     else:
-        wide = [lax.all_gather(w, ("shard", "ctx"), axis=0, tiled=True) for w in shards]
+        wide = [lax.all_gather(w.astype(bfloat), ("shard", "ctx"), axis=0, tiled=True) for w in shards]
         wide_input, wide_forget, wide_gate, wide_out, wide_mgate, wide_mup, wide_down = wide
         scale_one = inverse_rms(residual_in)
         normed_one = (residual_in * scale_one * norm_gain).astype(bfloat)
@@ -1578,22 +1727,13 @@
         activated = (silu_mlp * up_pre).astype(bfloat)
         upstream_low = upstream.astype(bfloat)
         grad_down = outer_sum(upstream_low, activated).astype(bfloat)
-    grad_activ = jnp.dot(upstream_low, wide_down, preferred_element_type=f32)
-    grad_gate_pre = (grad_activ * up_pre * silu_slope(gate_pre)).astype(bfloat)
-    grad_up_pre = (grad_activ * silu_mlp).astype(bfloat)
-    grad_mgate = outer_sum(normed_two, grad_gate_pre).astype(bfloat)
-    grad_mup = outer_sum(normed_two, grad_up_pre).astype(bfloat)
-    down_part = times_back(activated, wide_down).astype(bfloat)
-    normed_part = (times_back(grad_gate_pre, wide_mgate) + times_back(grad_up_pre, wide_mup)).astype(bfloat)
-    if small:
-        output, grad_resid, vectors, sums = back_all(
-            Z, seqs, length, grad_down, grad_mgate, grad_mup, normed_part, down_part, residual_in, middle, upstream,
-            normed_one, mixed_in, wide_out, wide_input, wide_forget, wide_gate, pi, pf, pg, h,
-            rh, start, ids, link, gain_one, gain_two, low_row, gain_row
-        )
-        grad_norm_gain, grad_mlp_gain = vectors[0], vectors[1]
-        grad_hidden_gain, grad_lower = vectors[2, :channels], vectors[3, :channels]
-    else:
+        grad_activ = jnp.dot(upstream_low, wide_down, preferred_element_type=f32)
+        grad_gate_pre = (grad_activ * up_pre * silu_slope(gate_pre)).astype(bfloat)
+        grad_up_pre = (grad_activ * silu_mlp).astype(bfloat)
+        grad_mgate = outer_sum(normed_two, grad_gate_pre).astype(bfloat)
+        grad_mup = outer_sum(normed_two, grad_up_pre).astype(bfloat)
+        down_part = times_back(activated, wide_down).astype(bfloat)
+        normed_part = (times_back(grad_gate_pre, wide_mgate) + times_back(grad_up_pre, wide_mup)).astype(bfloat)
         output = middle + lax.psum(down_part, "tp").astype(f32)
         grad_normed_two = lax.psum(normed_part, "tp").astype(f32)
         grad_mlp_gain = jnp.sum(grad_normed_two * middle * scale_two, axis=0)

time: 752 us -> 705 us (0.938)
  matrix products: 63 us -> 0 us
  Pallas kernels: 647 us -> 678 us
    dot_general x6 -> x0, matrix products: 63 us -> none  [the longest x3 30.6 us: times_back(): lax.dot_general(left_mat, right_mat, (((1,), (1,)), ((), ())), preferred_...]
    pallas_call x1, Pallas kernels: 356 us -> 388 us  [back_all(): pl.pallas_call(functools.partial(back_body, Z, seqs, length), out_shape=o...]
    convert_element_type x7 -> x0, other arithmetic: 10 us -> none  [on_device(): w.astype(bfloat)]
where the time goes in v5:
time: 705 us; the launch traced here: 699 us
  Pallas kernels  678 us (96%)
  local copies, waits for them, and re-layouts  13.3 us (2%)
  other arithmetic  7.61 us (1%)
    pallas_call x1, Pallas kernels, back_all(): pl.pallas_call(functools.partial(back_body, Z, seqs, length), out_shape=o...  388 us
    pallas_call x1, Pallas kernels, front_all(): pl.pallas_call(functools.partial(front_body, Z, seqs, length, ahead), out...  290 us

profile of v5, /device:TPU:0, one launch (start us, length us, event | category | flops | bytes accessed | tf_op | source)
XLA Modules:
  0.0 699.4 jit_solution(1356119791815533515)
XLA Ops:
  0.6 0.7 convert_element_type.9
  1.3 0.2 slice_reduce_fusion.1
  1.5 0.1 compare_select_fusion
  1.6 0.1 pad_bitcast_fusion
  1.7 0.1 pad_maximum_fusion
  1.7 0.7 broadcast_in_dim.32.refs_14_.refs_24_
  2.4 0.9 copy.30
  3.3 290.2 %forward.1 = (bf16[2048,1024]{1,0:T(8,128)(2,1)}, bf16[2048,1024]{1,0:T(8,128)(2,1)}, bf16[2048,1024]{1,0:T(8,128)(2,1)}, bf16[2048,1024]{1,0:T(8,128)(2,1)}, bf...) custom-call(f32[128,1024]{1,0:T(8,128)} %refs_0_.1, ...), custom_call_target="tpu_custom_call" | custom-call | tf_op jit(solution)/shard_map/forward/pallas_call | solution.py:977
  293.5 387.6 %backward.1 = (f32[512,2048]{1,0:T(8,128)}, f32[8,2048]{1,0:T(8,128)}, f32[128,2816]{1,0:T(8,128)}, f32[128,2816]{1,0:T(8,128)}, f32[128,2816]{1,0:T(8,128)}, /*...) custom-call(bf16[2048,2816]{1,0:T(8,128)(2,1)} %get-tuple-element.47, ...), custom_call_target="tpu_custom_call" | custom-call | tf_op jit(solution)/shard_map/backward/pallas_call | solution.py:1512
  681.1 0.0 copy-start
  681.1 6.8 add_add_fusion
  687.9 1.4 fusion.1
  689.3 1.5 fusion
  690.9 0.0 copy-done
  690.9 0.0 copy-start.7
  690.9 0.0 copy-start.6
  690.9 0.0 copy-start.5
  690.9 2.0 copy.39
  692.9 0.0 copy-done.7
  692.9 0.0 copy-start.4
  692.9 0.0 copy-start.3
  692.9 0.8 copy.40
  693.7 0.0 copy-done.6
  693.7 0.0 copy-start.2
  693.7 0.8 copy.41
  694.5 0.0 copy-done.5
  694.5 0.8 copy.42
  695.3 0.0 copy-done.4
  695.3 0.8 copy.43
  696.1 0.0 copy-done.3
  696.1 0.0 copy-start.1
  696.1 1.1 copy.44
  697.2 0.0 copy-done.2
  697.2 1.1 copy.45
  698.3 0.0 copy-done.1
  698.3 1.1 copy.46
  (1 shorter events, 0.0 us)
Async XLA Ops:
  681.1 9.8 %copy-start = (f32[512,2048]{1,0:T(8,128)S(1)}, f32[512,2048]{1,0:T(8,128)}, u32[]{:S(2)}) copy-start(f32[512,2048]{1,0:T(8,128)} %get-tuple-element.70) | copy-start | bytes 12582916
  690.9 2.0 copy-start.7
  690.9 2.8 copy-start.6
  690.9 3.6 copy-start.5
  692.9 2.4 copy-start.4
  692.9 3.2 copy-start.3
  693.7 3.5 copy-start.2
  696.1 2.2 copy-start.1

commit v6 on v5

--- a/solution.py
+++ b/solution.py
@@ -200,65 +200,39 @@
     def x_wait(self, w, n):
         self.on_pair(n, lambda: self.x_copy(w, n, 1).wait_recv(), lambda: self.x_copy(w, n).wait_recv())
 
-    def z_phase(self, w, n):
+    def z_step(self, w, n, end):
+        at_end = (self.z == 0) | (self.z == self.Z - 1)
+
+        @pl.when(at_end if end else jnp.logical_not(at_end))
+        def _():
+            self.z_phase(w, n, end)
+
+    def z_in(self, w, dest, up, k):
+        self.z_copy(w, 0, dest, up).wait_recv()
+        self.load(w, [None] * k + [self.rows((self.zu if up else self.zd)[w], dest, w)], 2)[0].wait()
+
+    def z_phase(self, w, n, end):
         Z, H = self.Z, self.R[w] // 2
         z = self.z
         last = n == Z - 1
-        dest = z if last else pick(z, [t[n] for t in self.ffirst])
+        dest = z if last else self.order(n)
         if n == 0:
             self.c_copy(w, 1).wait_recv()
         self.x_wait(w, n)
         cps = self.load(w, [self.part(w, self.q, self.c, dest), self.rows(self.rc[w], dest + Z, w),
                             self.rows(self.xr[w], dest, w)], 2)
-        if not last:
-            up = dest > z
-            down = dest < z
-            has_in = (up & (z > 0)) | (down & (z < Z - 1))
-
-            @pl.when(up & (z > 0))
-            def _():
-                self.z_copy(w, n, dest, True).wait_recv()
-                cp = self.load(w, [None] * 3 + [self.rows(self.zu[w], dest, w)], 2)
-                cp[0].wait()
-
-            @pl.when(down & (z < Z - 1))
-            def _():
-                self.z_copy(w, n, dest, False).wait_recv()
-                cp = self.load(w, [None] * 3 + [self.rows(self.zd[w], dest, w)], 2)
-                cp[0].wait()
-
-            if w >= 2:
-                self.z_wait_send(w - 2, n)
-            for cp in cps:
-                cp.wait()
-            dst = self.zs.at[w % 2, n, :, pl.ds(0, self.N[w])]
-
-            def store(r, v):
-                dst[pl.ds(r, 16), :] = v.astype(jnp.bfloat16)
-
-            paired = dest == self.zp
-            self.sum_parts(w, paired, has_in, (3,), store)
-
-            @pl.when(up)
-            def _():
-                self.z_copy(w, n, dest, True).start()
-
-            @pl.when(down)
-            def _():
-                self.z_copy(w, n, dest, False).start()
-        else:
-            @pl.when(z > 0)
-            def _():
-                self.z_copy(w, 0, dest, True).wait_recv()
-                cp = self.load(w, [None] * 3 + [self.rows(self.zu[w], dest, w)], 2)
-                cp[0].wait()
-
-            @pl.when(z < Z - 1)
-            def _():
-                self.z_copy(w, 0, dest, False).wait_recv()
-                cp = self.load(w, [None] * 4 + [self.rows(self.zd[w], dest, w)], 2)
-                cp[0].wait()
-
+        if last:
+            if end:
+                @pl.when(z > 0)
+                def _():
+                    self.z_in(w, dest, True, 3)
+
+                @pl.when(z == 0)
+                def _():
+                    self.z_in(w, dest, False, 3)
+            else:
+                self.z_in(w, dest, True, 3)
+                self.z_in(w, dest, False, 4)
             for cp in cps:
                 cp.wait()
             if w >= 1:
@@ -268,34 +242,46 @@
             def store(r, v):
                 dst[pl.ds(r, 16), :] = v
 
-            @pl.when((z > 0) & (z < Z - 1))
+            self.add(w, 2, (0, 1, 2, 3) if end else (0, 1, 2, 3, 4), store)
+            self.f_copy(w).start()
+            return
+        up = dest > z
+        if not end:
+            @pl.when(up)
             def _():
-                self.add(w, 2, (0, 1, 2, 3, 4), store)
-
-            @pl.when(z == 0)
+                self.z_in(w, dest, True, 3)
+
+            @pl.when(jnp.logical_not(up))
             def _():
-                self.add(w, 2, (0, 1, 2, 4), store)
-
-            @pl.when(z == Z - 1)
-            def _():
-                self.add(w, 2, (0, 1, 2, 3), store)
-
-            self.f_copy(w).start()
-
-    def sum_parts(self, w, paired, has_in, extra, store):
-        H = self.R[w] // 2
-        for p in (False, True):
-            for e in (False, True):
-                cond = (paired if p else jnp.logical_not(paired)) & (has_in if e else jnp.logical_not(has_in))
-
-                @pl.when(cond)
-                def _(p=p, e=e):
-                    ex = extra if e else ()
-                    if p:
-                        self.add(w, 2, (0, 1) + ex, store, 0, H)
-                        self.add(w, 2, (0, 1, 2) + ex, store, H, 2 * H)
-                    else:
-                        self.add(w, 2, (0, 1, 2) + ex, store)
+                self.z_in(w, dest, False, 3)
+        if w >= 2:
+            self.z_wait_send(w - 2, n)
+        for cp in cps:
+            cp.wait()
+        dst = self.zs.at[w % 2, n, :, pl.ds(0, self.N[w])]
+
+        def store(r, v):
+            dst[pl.ds(r, 16), :] = v.astype(jnp.bfloat16)
+
+        more = () if end else (3,)
+        paired = dest == self.zp
+
+        @pl.when(paired)
+        def _():
+            self.add(w, 2, (0, 1) + more, store, 0, H)
+            self.add(w, 2, (0, 1, 2) + more, store, H, 2 * H)
+
+        @pl.when(jnp.logical_not(paired))
+        def _():
+            self.add(w, 2, (0, 1, 2) + more, store)
+
+        @pl.when(up)
+        def _():
+            self.z_copy(w, n, dest, True).start()
+
+        @pl.when(jnp.logical_not(up))
+        def _():
+            self.z_copy(w, n, dest, False).start()
 
     def z_wait_send(self, w, n):
         z = self.z
@@ -1052,8 +1038,11 @@
     def X(w):
         return [functools.partial(sc.x_phase, w, k) for k in range(Z)]
 
-    def Zs(w):
-        return [functools.partial(sc.z_phase, w, k) for k in range(Z)]
+    def E(w, k):
+        return functools.partial(sc.z_step, w, k, True)
+
+    def M(w, k):
+        return functools.partial(sc.z_step, w, k, False)
 
     def tick(*todo):
         for s in todo:
@@ -1338,9 +1327,7 @@
         vec[0:1, j * TC:(j + 1) * TC] = lax.fori_loop(0, n // 16, go, jnp.zeros((1, TC), jnp.float32), unroll=2)
         dx_copy(j).start()
 
-    x0, x1, x2, z0, z1, z2 = X(0), X(1), X(2), Zs(0), Zs(1), Zs(2)
-    x3, x4, x5, x6 = X(3), X(4), X(5), X(6)
-    z3, z4, z5, z6 = Zs(3), Zs(4), Zs(5), Zs(6)
+    x0, x1, x2, x3, x4, x5, x6 = (X(w) for w in range(7))
     for cp in glu_loads(0, 0):
         cp.start()
     early[5].wait()
@@ -1348,56 +1335,56 @@
     tick(x0[0])
     glu_cols(1)
     tick(x0[1])
-    w_rows(w_mg, 0, 0).start()
-    w_rows(w_mu, 0, 1).start()
     glu_cols(2)
     tick(x0[2])
     load_n1 = pltpu.make_async_copy(n1, n1v, l_h.at[5])
     load_n1.start()
+    early[6].wait()
+    glu_grad(1, segments, 0, NC // 2)
+    tick(E(0, 0))
+    glu_grad(1, segments, NC // 2, NC)
+    w_rows(w_mg, 0, 0).start()
+    w_rows(w_mu, 0, 1).start()
+    tick(x0[3], M(0, 0), E(0, 1))
     normed(0, NC // 2)
-    tick(x0[3], z0[0])
+    tick(x1[0], M(0, 1), E(0, 2))
     normed(NC // 2, NC)
     for j in range(NC):
         sn_out(pn, j).wait()
     for k in range(NP):
         pn_copy(k).start()
-    tick(z0[1])
-    early[6].wait()
-    glu_grad(1, segments, 0, NC // 2)
-    tick(z0[2])
-    glu_grad(1, segments, NC // 2, NC)
-    tick(z0[3])
+    tick(x1[1], M(0, 2), E(0, 3))
     glu_grad(2, [(du, 0, F)], 0, NC // 2)
-    tick(x1[0])
+    tick(x1[2], M(0, 3))
     glu_grad(2, [(du, 0, F)], NC // 2, NC)
     load_act = pltpu.make_async_copy(act_h, du, l_h.at[6])
     load_act.start()
     w_rows(w_dn, 0, 0).start()
-    tick(x1[1])
+    tick(E(1, 0))
     load_act.wait()
     down(0, NC // 2)
-    tick(x1[2])
+    tick(x1[3], M(1, 0), E(1, 1))
     down(NC // 2, NC)
     for j in range(NC):
         sn_out(po, j).wait()
     for k in range(NP):
         po_copy(k).start()
     p1_load(0)
-    tick(x1[3], z1[0])
+    tick(x2[0], M(1, 1), E(1, 2))
     early[7].wait()
-    between = [[z1[1]], [x2[0]], [x2[1]], [z1[2]], [x2[2]], [], [z1[3]], [x2[3]]]
+    between = [[], [x2[1]], [], [M(1, 2), E(1, 3)], [], [x2[2]], [], [M(1, 3)]]
     for k in range(NP):
         if k + 1 < NP:
             p1_load(k + 1)
         p1(k)
         tick(*(between[k] if k < len(between) else []))
     p2()
-    tick(z2[0])
+    tick(x2[3], E(2, 0))
     for cp in early[:5]:
         cp.wait()
     load_n1.wait()
     p4(3, gm, mv)
-    tick(z2[1])
+    tick(M(2, 0), E(2, 1))
     backward_first(n, dm, h, pg, hgain, rh, dpg, col, acc_row(vec, 2, C))
     column_to_rows(col, row, n)
     swap = remote(row, got, s_t.at[0], r_t.at[0], OTHER)
@@ -1409,51 +1396,52 @@
     for sq in range(seqs):
         ends.append(backward_scan_one(sq, length, dm, h, pf, pg, low, hgain, link, rh, col, gl, tail))
         if sq == 0:
-            tick(z2[2])
+            tick(x3[2], M(2, 1), E(2, 2))
     pay[4:8, :] = ids[...]
     for sq in range(seqs):
         pay[sq:sq + 1, :] = ends[sq][1]
         pay[2 + sq:3 + sq, :] = ends[sq][0]
     cps = spread(Z, z, pay, box, s_c, r_c)
-    tick(x3[2], x3[3], z2[3])
+    tick(x3[3], M(2, 2), E(2, 3))
     spread_wait(Z, z, pay, box, s_c, r_c, cps)
     end[...] = suffix_state(Z, z, box)
     backward_last(seqs, length, gl, tail, end, h, start, pi, pf, low, link, dpi, dpf, acc_row(vec, 3, C))
-    tick(z3[0])
+    tick(M(2, 3), E(3, 0))
     p4(4, n1v, dpi)
-    tick(z3[1], x4[0], x4[1])
+    tick(x4[0], x4[1], M(3, 0), E(3, 1))
     p4(5, n1v, dpf)
-    tick(x4[2], x4[3], z3[2])
+    tick(x4[2], x4[3], M(3, 1), E(3, 2))
     p4(6, n1v, dpg)
     w3_start(0, 0)
-    tick(z3[3], x5[0], x5[1])
+    tick(x5[0], x5[1], M(3, 2), E(3, 3))
     p5(0, NC // 2)
-    tick(x5[2], x5[3], z4[0], z4[1])
+    tick(x5[2], M(3, 3), E(4, 0))
     p5(NC // 2, NC)
-    tick(z4[2], z4[3], *x6)
+    tick(x5[3], x6[0], x6[1], M(4, 0), E(4, 1))
+    late = {3: [x6[2], M(4, 1), E(4, 2)], 7: [x6[3], M(4, 2), E(4, 3)]}
     for j in range(NC):
         p6a(j)
-        if j % 4 == 3 and j // 4 < 2:
-            tick(z5[j // 4])
+        tick(*late.get(j, []))
     p6b()
+    tick(M(4, 3), E(5, 0))
+    late = {1: [M(5, 0), E(5, 1)], 3: [M(5, 1), E(5, 2)], 5: [M(5, 2), E(5, 3)], 7: [M(5, 3), E(6, 0)]}
     for j in range(NC):
         p6c(j)
-        if j % 4 == 3 and j // 4 < 2:
-            tick(z5[2 + j // 4])
+        tick(*late.get(j, []))
     for j in (NC - 2, NC - 1):
         dx_copy(j).wait()
     first = remote(vec, vgot.at[0], v_s.at[0], v_r.at[0], sc.C)
     first.start()
-    tick(z6[0])
+    tick(M(6, 0), E(6, 1))
     first.wait()
     vec[...] = vec[...] + vgot[0]
     second = remote(vec, vgot.at[1], v_s.at[1], v_r.at[1], sc.X)
     second.start()
-    tick(z6[1])
+    tick(M(6, 1), E(6, 2))
     second.wait()
     vec[...] = vec[...] + vgot[1]
     cps = spread(Z, z, vec, vbox, vz_s, vz_r)
-    tick(z6[2], z6[3])
+    tick(M(6, 2), E(6, 3), M(6, 3))
     spread_wait(Z, z, vec, vbox, vz_s, vz_r, cps)
     total = vbox[0]
     for k in range(1, Z):

time: 705 us -> 681 us (0.966)
  Pallas kernels: 678 us -> 654 us
    pallas_call x1, Pallas kernels: 388 us -> 364 us  [back_all(): pl.pallas_call(functools.partial(back_body, Z, seqs, length), out_shape=o...]
where the time goes in v6:
time: 681 us; the launch traced here: 676 us
  Pallas kernels  654 us (96%)
  local copies, waits for them, and re-layouts  13.3 us (2%)
  other arithmetic  7.61 us (1%)
    pallas_call x1, Pallas kernels, back_all(): pl.pallas_call(functools.partial(back_body, Z, seqs, length), out_shape=o...  364 us
    pallas_call x1, Pallas kernels, front_all(): pl.pallas_call(functools.partial(front_body, Z, seqs, length, ahead), out...  290 us

profile of v6, /device:TPU:0, one launch (start us, length us, event | category | flops | bytes accessed | tf_op | source)
XLA Modules:
  0.0 675.8 jit_solution(9451298174412424847)
XLA Ops:
  0.6 0.7 convert_element_type.9
  1.3 0.2 slice_reduce_fusion.1
  1.5 0.1 compare_select_fusion
  1.6 0.1 pad_bitcast_fusion
  1.7 0.1 pad_maximum_fusion
  1.7 0.7 broadcast_in_dim.32.refs_14_.refs_24_
  2.4 0.9 copy.30
  3.3 290.2 %forward.1 = (bf16[2048,1024]{1,0:T(8,128)(2,1)}, bf16[2048,1024]{1,0:T(8,128)(2,1)}, bf16[2048,1024]{1,0:T(8,128)(2,1)}, bf16[2048,1024]{1,0:T(8,128)(2,1)}, bf...) custom-call(f32[128,1024]{1,0:T(8,128)} %refs_0_.1, ...), custom_call_target="tpu_custom_call" | custom-call | tf_op jit(solution)/shard_map/forward/pallas_call | solution.py:963
  293.5 364.1 %backward.1 = (f32[512,2048]{1,0:T(8,128)}, f32[8,2048]{1,0:T(8,128)}, f32[128,2816]{1,0:T(8,128)}, f32[128,2816]{1,0:T(8,128)}, f32[128,2816]{1,0:T(8,128)}, /*...) custom-call(bf16[2048,2816]{1,0:T(8,128)(2,1)} %get-tuple-element.47, ...), custom_call_target="tpu_custom_call" | custom-call | tf_op jit(solution)/shard_map/backward/pallas_call | solution.py:1500
  657.6 0.0 copy-start
  657.6 6.8 %add_add_fusion = f32[512,2048]{1,0:T(8,128)} fusion(f32[512,2048]{1,0:T(8,128)} %get-tuple-element.46.refs_10_, bf16[512,2048]{1,0:T(8,128)(2,1)} %get-tuple-element.69, bf16[512,2048]{1,0:T(8,128)(2,1)} %get-tuple-element.68), kind=kLoop, calls=%fused_computation | loop fusion | flops 4194304 | bytes 12582912 | tf_op jit(solution)/shard_map/add | solution.py:1694
  664.3 1.4 fusion.1
  665.8 1.5 fusion
  667.3 0.0 copy-done
  667.3 0.0 copy-start.7
  667.3 0.0 copy-start.6
  667.3 0.0 copy-start.5
  667.3 2.0 copy.39
  669.3 0.0 copy-done.7
  669.3 0.0 copy-start.4
  669.3 0.0 copy-start.3
  669.3 0.8 copy.40
  670.1 0.0 copy-done.6
  670.1 0.0 copy-start.2
  670.1 0.8 copy.41
  670.9 0.0 copy-done.5
  670.9 0.8 copy.42
  671.7 0.0 copy-done.4
  671.7 0.8 copy.43
  672.5 0.0 copy-done.3
  672.5 0.0 copy-start.1
  672.5 1.1 copy.44
  673.6 0.0 copy-done.2
  673.6 1.1 copy.45
  674.7 0.0 copy-done.1
  674.7 1.1 copy.46
  (1 shorter events, 0.0 us)
Async XLA Ops:
  657.6 9.8 %copy-start = (f32[512,2048]{1,0:T(8,128)S(1)}, f32[512,2048]{1,0:T(8,128)}, u32[]{:S(2)}) copy-start(f32[512,2048]{1,0:T(8,128)} %get-tuple-element.70) | copy-start | bytes 12582916
  667.3 2.0 copy-start.7
  667.3 2.8 copy-start.6
  667.3 3.6 copy-start.5
  669.3 2.4 copy-start.4
  669.3 3.2 copy-start.3
  670.1 3.5 copy-start.2
  672.5 2.2 copy-start.1

commit v7 on v6

--- a/solution.py
+++ b/solution.py
@@ -1384,7 +1384,7 @@
         cp.wait()
     load_n1.wait()
     p4(3, gm, mv)
-    tick(M(2, 0), E(2, 1))
+    tick(M(2, 0))
     backward_first(n, dm, h, pg, hgain, rh, dpg, col, acc_row(vec, 2, C))
     column_to_rows(col, row, n)
     swap = remote(row, got, s_t.at[0], r_t.at[0], OTHER)
@@ -1396,35 +1396,36 @@
     for sq in range(seqs):
         ends.append(backward_scan_one(sq, length, dm, h, pf, pg, low, hgain, link, rh, col, gl, tail))
         if sq == 0:
-            tick(x3[2], M(2, 1), E(2, 2))
+            tick(x3[2])
     pay[4:8, :] = ids[...]
     for sq in range(seqs):
         pay[sq:sq + 1, :] = ends[sq][1]
         pay[2 + sq:3 + sq, :] = ends[sq][0]
     cps = spread(Z, z, pay, box, s_c, r_c)
-    tick(x3[3], M(2, 2), E(2, 3))
+    w3_start(0, 0)
+    tick(E(2, 1), x3[3], M(2, 1), E(2, 2))
     spread_wait(Z, z, pay, box, s_c, r_c, cps)
     end[...] = suffix_state(Z, z, box)
     backward_last(seqs, length, gl, tail, end, h, start, pi, pf, low, link, dpi, dpf, acc_row(vec, 3, C))
+    tick(M(2, 2), E(2, 3))
+    p5(0, NC // 2)
     tick(M(2, 3), E(3, 0))
+    p5(NC // 2, NC)
+    tick(M(3, 0), E(3, 1))
     p4(4, n1v, dpi)
-    tick(x4[0], x4[1], M(3, 0), E(3, 1))
+    tick(M(3, 1), E(3, 2), x4[0], x4[1])
     p4(5, n1v, dpf)
-    tick(x4[2], x4[3], M(3, 1), E(3, 2))
+    tick(M(3, 2), E(3, 3), x4[2], x4[3])
     p4(6, n1v, dpg)
-    w3_start(0, 0)
-    tick(x5[0], x5[1], M(3, 2), E(3, 3))
-    p5(0, NC // 2)
-    tick(x5[2], M(3, 3), E(4, 0))
-    p5(NC // 2, NC)
-    tick(x5[3], x6[0], x6[1], M(4, 0), E(4, 1))
-    late = {3: [x6[2], M(4, 1), E(4, 2)], 7: [x6[3], M(4, 2), E(4, 3)]}
+    tick(M(3, 3), E(4, 0), x5[0], x5[1])
+    late = [[M(4, 0), E(4, 1)], [x5[2], x5[3]], [M(4, 1), E(4, 2)], [x6[0], x6[1]], [M(4, 2), E(4, 3)], [x6[2]],
+            [M(4, 3), E(5, 0)], [x6[3]]]
     for j in range(NC):
         p6a(j)
-        tick(*late.get(j, []))
+        tick(*(late[j] if j < len(late) else []))
     p6b()
-    tick(M(4, 3), E(5, 0))
-    late = {1: [M(5, 0), E(5, 1)], 3: [M(5, 1), E(5, 2)], 5: [M(5, 2), E(5, 3)], 7: [M(5, 3), E(6, 0)]}
+    tick(M(5, 0), E(5, 1))
+    late = {1: [M(5, 1), E(5, 2)], 3: [M(5, 2), E(5, 3)], 5: [M(5, 3), E(6, 0)], 7: [M(6, 0), E(6, 1)]}
     for j in range(NC):
         p6c(j)
         tick(*late.get(j, []))
@@ -1432,16 +1433,16 @@
         dx_copy(j).wait()
     first = remote(vec, vgot.at[0], v_s.at[0], v_r.at[0], sc.C)
     first.start()
-    tick(M(6, 0), E(6, 1))
+    tick(M(6, 1), E(6, 2))
     first.wait()
     vec[...] = vec[...] + vgot[0]
     second = remote(vec, vgot.at[1], v_s.at[1], v_r.at[1], sc.X)
     second.start()
-    tick(M(6, 1), E(6, 2))
+    tick(M(6, 2), E(6, 3))
     second.wait()
     vec[...] = vec[...] + vgot[1]
     cps = spread(Z, z, vec, vbox, vz_s, vz_r)
-    tick(M(6, 2), E(6, 3), M(6, 3))
+    tick(M(6, 3))
     spread_wait(Z, z, vec, vbox, vz_s, vz_r, cps)
     total = vbox[0]
     for k in range(1, Z):

time: 681 us -> 657 us (0.965)
  Pallas kernels: 654 us -> 630 us
    pallas_call x1, Pallas kernels: 364 us -> 340 us  [back_all(): pl.pallas_call(functools.partial(back_body, Z, seqs, length), out_shape=o...]
where the time goes in v7:
time: 657 us; the launch traced here: 652 us
  Pallas kernels  630 us (96%)
  local copies, waits for them, and re-layouts  13.3 us (2%)
  other arithmetic  7.61 us (1%)
    pallas_call x1, Pallas kernels, back_all(): pl.pallas_call(functools.partial(back_body, Z, seqs, length), out_shape=o...  340 us
    pallas_call x1, Pallas kernels, front_all(): pl.pallas_call(functools.partial(front_body, Z, seqs, length, ahead), out...  290 us

profile of v7, /device:TPU:0, one launch (start us, length us, event | category | flops | bytes accessed | tf_op | source)
XLA Modules:
  0.0 652.0 jit_solution(17694384906480952035)
XLA Ops:
  0.6 0.7 convert_element_type.9
  1.3 0.2 slice_reduce_fusion.1
  1.5 0.1 compare_select_fusion
  1.6 0.1 pad_bitcast_fusion
  1.7 0.1 pad_maximum_fusion
  1.7 0.7 broadcast_in_dim.32.refs_14_.refs_24_
  2.4 0.9 copy.30
  3.3 290.2 %forward.1 = (bf16[2048,1024]{1,0:T(8,128)(2,1)}, bf16[2048,1024]{1,0:T(8,128)(2,1)}, bf16[2048,1024]{1,0:T(8,128)(2,1)}, bf16[2048,1024]{1,0:T(8,128)(2,1)}, bf...) custom-call(f32[128,1024]{1,0:T(8,128)} %refs_0_.1, ...), custom_call_target="tpu_custom_call" | custom-call | tf_op jit(solution)/shard_map/forward/pallas_call | solution.py:963
  293.5 340.3 %backward.1 = (f32[512,2048]{1,0:T(8,128)}, f32[8,2048]{1,0:T(8,128)}, f32[128,2816]{1,0:T(8,128)}, f32[128,2816]{1,0:T(8,128)}, f32[128,2816]{1,0:T(8,128)}, /*...) custom-call(bf16[2048,2816]{1,0:T(8,128)(2,1)} %get-tuple-element.47, ...), custom_call_target="tpu_custom_call" | custom-call | tf_op jit(solution)/shard_map/backward/pallas_call | solution.py:1501
  633.7 0.0 copy-start
  633.7 6.8 %add_add_fusion = f32[512,2048]{1,0:T(8,128)} fusion(f32[512,2048]{1,0:T(8,128)} %get-tuple-element.46.refs_10_, bf16[512,2048]{1,0:T(8,128)(2,1)} %get-tuple-element.69, bf16[512,2048]{1,0:T(8,128)(2,1)} %get-tuple-element.68), kind=kLoop, calls=%fused_computation | loop fusion | flops 4194304 | bytes 12582912 | tf_op jit(solution)/shard_map/add | solution.py:1695
  640.5 1.4 fusion.1
  642.0 1.5 fusion
  643.5 0.0 copy-done
  643.5 0.0 copy-start.7
  643.5 0.0 copy-start.6
  643.5 0.0 copy-start.5
  643.5 2.0 copy.39
  645.5 0.0 copy-done.7
  645.5 0.0 copy-start.4
  645.5 0.0 copy-start.3
  645.5 0.8 copy.40
  646.3 0.0 copy-done.6
  646.3 0.0 copy-start.2
  646.3 0.8 copy.41
  647.1 0.0 copy-done.5
  647.1 0.8 copy.42
  647.9 0.0 copy-done.4
  647.9 0.8 copy.43
  648.7 0.0 copy-done.3
  648.7 0.0 copy-start.1
  648.7 1.1 copy.44
  649.8 0.0 copy-done.2
  649.8 1.1 copy.45
  650.9 0.0 copy-done.1
  650.9 1.1 copy.46
  (1 shorter events, 0.0 us)
Async XLA Ops:
  633.7 9.8 %copy-start = (f32[512,2048]{1,0:T(8,128)S(1)}, f32[512,2048]{1,0:T(8,128)}, u32[]{:S(2)}) copy-start(f32[512,2048]{1,0:T(8,128)} %get-tuple-element.70) | copy-start | bytes 12582916
  643.5 2.0 copy-start.7
  643.5 2.8 copy-start.6
  643.5 3.6 copy-start.5
  645.5 2.4 copy-start.4
  645.5 3.2 copy-start.3
  646.3 3.5 copy-start.2
  648.7 2.2 copy-start.1
